TPU v7x, 32 devices: a whole 2x2x4 slice. The times are simulated.
32 devices in a mesh: gx: 4 (over y, x), gy: 2 (over core), gz: 4 (over z).
Axes of the slice: x: 2, y: 2, z: 4, core: 2. Of those that a mesh axis runs over, the one named last changes fastest.
Arguments:
- trace_maps: bfloat16 [4, 2, 4, 2, 1024, 1024], P('gx', 'gy', 'gz'), may hold values from -0.109375 to 0.109375
- sources: float32 [4, 2, 4, 2, 16, 1024], P('gx', 'gy', 'gz'), may hold values from -6 to 6
- corner: int32 [1], replicated, may hold values from 0 to 7
Outputs:
- traces: bfloat16 [4, 2, 4, 2, 16, 1024], P('gx', 'gy', 'gz')
All inputs are finite; a program needn't handle non-finite values.
Results may differ from a plain program's by a relative error of at most 0.012.
Values may be sent and summed in bfloat16 or wider, within the bound.
No kernel may reach another device: no remote copies, remote signals or barrier semaphores. Data moves between devices by JAX's collectives and lax.ppermute only.
A program may use at most 64 MiB of HBM per device.

v0:
```python
import functools
import itertools

import jax
import jax.numpy as jnp
from jax import lax
from jax.experimental import pallas as pl
from jax.experimental.pallas import tpu as pltpu
from jax.sharding import PartitionSpec as P

STEPS = 6
AXES = ("gx", "gy", "gz")
ORDER = (0, 2, 1)
ROOM = pltpu.CompilerParams(vmem_limit_bytes=8 * 1024 * 1024)


def places(sizes):
    return itertools.product(*(range(size) for size in sizes))


def number(sizes, place):
    flat = 0
    for index, size in zip(place, sizes):
        flat = flat * size + index
    return flat


def depth_of(sizes, bits, place):
    return sum(
        index if bit else size - 1 - index for index, size, bit in zip(place, sizes, bits)
    )


def level_edges(sizes, bits, axis, level):
    edges = []
    for place in places(sizes):
        index = place[axis] + (1 if bits[axis] else -1)
        if 0 <= index < sizes[axis] and depth_of(sizes, bits, place) == level:
            edges.append((place, place[:axis] + (index,) + place[axis + 1 :]))
    return edges


def hop_edges(sizes, bits, axis, hop):
    back = tuple(1 - bit for bit in bits)
    return level_edges(sizes, bits, axis, hop - 1) + level_edges(sizes, back, axis, hop - 1)


def clash(edges):
    sources, targets = zip(*edges) if edges else ((), ())
    return len(set(sources)) < len(sources) or len(set(targets)) < len(targets)


def fits_wave(sizes):
    deepest = sum(size - 1 for size in sizes)
    return deepest <= STEPS + 1 and deepest % 2 == 1


SHARED = (
    ((1, 2), (3, 7), (4, 6), (5,)),
    ((1, 7), (2, 6), (3, 5), (4,)),
    ((1, 2, 4), (3, 7), (5, 6)),
)


def pairs_of(sizes, bits, axis, hop):
    deepest = sum(size - 1 for size in sizes)
    own = hop_edges(sizes, bits, axis, hop)
    group = next((group for group in SHARED[axis] if hop in group), (hop,))
    edges = [edge for other in group if other <= deepest for edge in hop_edges(sizes, bits, axis, other)]
    edges = sorted(set(edges))
    if clash(edges):
        edges = own
    assert not clash(edges)
    return sorted((number(sizes, source), number(sizes, target)) for source, target in edges)


def my_depth(sizes, bits):
    return depth_of(sizes, bits, tuple(lax.axis_index(axis) for axis in AXES))


def begin_kernel(sizes, bits, lead_ref, sources_ref, message_ref, traces_ref, held_ref, arrived):
    lead = lead_ref[0]
    copies = [
        pltpu.make_async_copy(
            sources_ref.at[lead if slot == 0 else 1 - lead], held_ref.at[slot], arrived.at[slot]
        )
        for slot in range(2)
    ]
    for copy in copies:
        copy.start()
    for copy in copies:
        copy.wait()
    traces_ref[...] = held_ref[...].astype(traces_ref.dtype)
    rows = held_ref.shape[1]
    if message_ref.shape[0] > rows:
        message_ref[rows:] = jnp.zeros_like(message_ref[rows:])
    entry = my_depth(sizes, bits) == 0
    message_ref[:rows] = jnp.where(entry, traces_ref[0], traces_ref[1])


def begin(sizes, bits, chains, lead, sources):
    _, rows, face = sources.shape
    vmem = pl.BlockSpec(memory_space=pltpu.VMEM)
    return pl.pallas_call(
        functools.partial(begin_kernel, sizes, bits),
        out_shape=(
            pltpu.VMEM((chains * rows, face), jnp.bfloat16),
            pltpu.VMEM(sources.shape, jnp.bfloat16),
            pltpu.VMEM(sources.shape, sources.dtype),
        ),
        in_specs=[pl.BlockSpec(memory_space=pltpu.SMEM), pl.BlockSpec(memory_space=pl.ANY)],
        out_specs=(vmem, vmem, vmem),
        scratch_shapes=[pltpu.SemaphoreType.DMA((2,))],
        compiler_params=ROOM,
        name="begin",
    )(lead, sources)


def load_kernel(lead_ref, maps_ref, after_ref, held_ref, arrived):
    lead = lead_ref[0]
    copies = [
        pltpu.make_async_copy(
            maps_ref.at[lead if slot == 0 else 1 - lead], held_ref.at[slot], arrived.at[slot]
        )
        for slot in range(2)
    ]
    for copy in copies:
        copy.start()
    for copy in copies:
        copy.wait()


def load(lead, maps, after):
    hbm = pl.BlockSpec(memory_space=pl.ANY)
    return pl.pallas_call(
        load_kernel,
        out_shape=pltpu.VMEM(maps.shape, maps.dtype),
        in_specs=[pl.BlockSpec(memory_space=pltpu.SMEM), hbm, hbm],
        out_specs=pl.BlockSpec(memory_space=pltpu.VMEM),
        scratch_shapes=[pltpu.SemaphoreType.DMA((2,))],
        compiler_params=ROOM,
        name="load",
    )(lead, maps, after)


def hop_kernel(
    hop, sizes, bits, lead_ref, y_ref, z_ref, x_ref, maps_ref, sources_ref, old_ref, *results
):
    deepest = sum(size - 1 for size in sizes)
    depth = my_depth(sizes, bits)
    back = deepest - depth
    last = hop == deepest
    traces_ref = results[-1]
    rows = sources_ref.shape[1]

    def place_of(slot):
        return jnp.where(lead_ref[0] == 0, slot, 1 - slot) if last else slot

    for slot in range(2):
        traces_ref[place_of(slot)] = old_ref[slot]

    @pl.when((depth == hop) | (back == hop))
    def _():
        slot = jnp.where(depth == hop, 0, 1)
        summed = x_ref[...].astype(jnp.float32) + y_ref[...].astype(jnp.float32)
        summed = summed + z_ref[...].astype(jnp.float32)
        mapped = jnp.dot(
            summed.astype(jnp.bfloat16), maps_ref[slot], preferred_element_type=jnp.float32
        )
        source = sources_ref[slot]
        for chain in range(mapped.shape[0] // rows):
            part = slice(chain * rows, (chain + 1) * rows)
            new = (mapped[part] + source).astype(jnp.bfloat16)
            if not last:
                results[0][part] = new
            if chain == max(0, hop - STEPS):
                traces_ref[place_of(slot)] = new


def take_hop(hop, sizes, bits, lead, came, maps, sources, traces):
    last = hop == sum(size - 1 for size in sizes)
    vmem = pl.BlockSpec(memory_space=pltpu.VMEM)
    came = [came[axis] for axis in reversed(ORDER)]
    held = [pltpu.with_memory_space_constraint(a, pltpu.VMEM) for a in came]
    held += [pltpu.with_memory_space_constraint(a, pltpu.VMEM) for a in (maps, sources, traces)]
    shapes = (jax.ShapeDtypeStruct(traces.shape, traces.dtype),)
    if not last:
        shapes = (
            pltpu.VMEM(came[0].shape, came[0].dtype),
            pltpu.VMEM(traces.shape, traces.dtype),
        )
    results = pl.pallas_call(
        functools.partial(hop_kernel, hop, sizes, bits),
        out_shape=shapes,
        in_specs=[pl.BlockSpec(memory_space=pltpu.SMEM if last else pl.ANY)] + [vmem] * 6,
        out_specs=(vmem,) * len(shapes),
        compiler_params=ROOM,
        name=f"hop{hop}",
    )(lead, *held)
    return results[0], results[-1]


def wave(sizes, bits, lead, maps, sources):
    deepest = sum(size - 1 for size in sizes)
    chains = max(0, deepest - STEPS) + 1
    message, traces, sources = begin(sizes, bits, chains, lead, sources)
    for hop in range(1, deepest + 1):
        came = [None] * 3
        for axis in ORDER:
            came[axis] = lax.ppermute(message, AXES, pairs_of(sizes, bits, axis, hop))
        if hop == 1:
            maps = load(lead, maps, message)
        message, traces = take_hop(hop, sizes, bits, lead, came, maps, sources, traces)
    return traces


def passed_along(array, axis, by):
    devices = lax.axis_size(axis)
    pairs = [(i, i + by) for i in range(devices) if 0 <= i + by < devices]
    return lax.ppermute(array, axis, pairs)


def stepped(code, maps, sources):
    traces = sources.astype(jnp.bfloat16)
    for _ in range(STEPS):
        incoming = jnp.zeros(sources.shape, jnp.float32)
        for position, axis in enumerate(AXES):
            up = (jnp.right_shift(code, position) & 1) == 1
            lower = passed_along(jnp.where(up, traces[0], traces[1]), axis, 1)
            upper = passed_along(jnp.where(up, traces[1], traces[0]), axis, -1)
            came = jnp.stack([jnp.where(up, lower, upper), jnp.where(up, upper, lower)])
            incoming = incoming + came.astype(jnp.float32)
        mapped = jnp.einsum(
            "scf,sfg->scg", incoming.astype(jnp.bfloat16), maps, preferred_element_type=jnp.float32
        )
        traces = (mapped + sources).astype(jnp.bfloat16)
    return traces


def solution(mesh):
    sizes = tuple(mesh.shape[axis] for axis in AXES)

    def shards(trace_maps, sources, corner):
        maps = trace_maps[0, 0, 0]
        rows = sources[0, 0, 0]
        code = corner[0]
        if not fits_wave(sizes):
            return stepped(code, maps, rows)[None, None, None]
        lead = 1 - (jnp.right_shift(code, 1) & 1)
        code = jnp.where(lead == 1, 7 - code, code)
        kind = (code & 1) + 2 * (jnp.right_shift(code, 2) & 1)

        def branch(kind):
            bits = (kind & 1, 1, kind >> 1)
            return lambda *operands: wave(sizes, bits, *operands)

        traces = lax.switch(
            kind, [branch(kind) for kind in range(4)], lead.reshape(1), maps, rows
        )
        return traces[None, None, None]

    return jax.shard_map(
        shards,
        mesh=mesh,
        in_specs=(
            P("gx", "gy", "gz", None, None, None),
            P("gx", "gy", "gz", None, None, None),
            P(),
        ),
        out_specs=P("gx", "gy", "gz", None, None, None),
        check_vma=False,
    )
```

profile of v0, /device:TPU:12, one launch (start us, length us, event | category | flops | bytes accessed | tf_op | source)
XLA Modules:
  0.0 56.9 jit_solution(9781164180151338118)
XLA Ops:
  0.7 55.6 %conditional.1 = (bf16[1,1,1,2,16,1024]{5,4,3,2,1,0:T(8,128)(2,1)S(1)}) conditional(s32[]{:T(128)} %clamp.3, (s32[]{:T(128)}, f32[1,1,1,2,16,1024]{5,4,3,2,1,0:T(8,128)}, bf16[1,1,1,2,1024,1024]{5,4,3,2,1,0:T(8,128)(2,1)}) %tuple.21, (s32[]{:T(128)}, f32[1,1,1,2,16,1024]{5,4,3,2,1,0:T(8,128)}, ...), branch_computations={%region_0.1_spmd, %region_1.2_spmd, %region_2.3_spmd, %region_3.4_... | conditional | bytes 5505872 | solution.py:257
  0.7 0.9 %begin.4 = (bf16[32,1024]{1,0:T(8,128)(2,1)S(1)}, bf16[2,16,1024]{2,1,0:T(8,128)(2,1)S(1)}, f32[2,16,1024]{2,1,0:T(8,128)S(1)}) custom-call(s32[1]{0:T(128)} %bitcast.lead_ref, f32[2,16,1024]{2,1,0:T(8,128)} %bitcast.24), custom_call_target="tpu_custom_call" | custom-call | tf_op jit(solution)/shard_map/cond/branch_0_fun/begin/pallas_call | solution.py:104
  1.6 0.7 %collective-permute-start.2 = (bf16[32,1024]{1,0:T(8,128)(2,1)S(1)}, bf16[32,1024]{1,0:T(8,128)(2,1)S(1)}, u32[]{:S(2)}, u32[]{:S(2)}) collective-permute-start(bf16[32,1024]{1,0:T(8,128)(2,1)S(1)} %get-tuple-element.49.after_ref), channel_id=1, source_target_pairs={{0,8},{4,12},{5,13},{12,20},{19,11},{26,18},{27,19},{31,23}} | collective-permute-start | bytes 196616 | tf_op jit(solution)/shard_map/cond/branch_0_fun/ppermute | solution.py:210
  2.3 2.4 %collective-permute-start.1 = (bf16[32,1024]{1,0:T(8,128)(2,1)S(1)}, bf16[32,1024]{1,0:T(8,128)(2,1)S(1)}, u32[]{:S(2)}, u32[]{:S(2)}) collective-permute-start(bf16[32,1024]{1,0:T(8,128)(2,1)S(1)} %get-tuple-element.49.after_ref), channel_id=1, source_target_pairs={{0,1},{2,3},{3,2},{4,5},{5,6},{9,10},{10,9},{12,13},{14,15},{15,14... | collective-permute-start | bytes 196616 | tf_op jit(solution)/shard_map/cond/branch_0_fun/ppermute | solution.py:210
  4.6 0.7 %collective-permute-start = (bf16[32,1024]{1,0:T(8,128)(2,1)S(1)}, bf16[32,1024]{1,0:T(8,128)(2,1)S(1)}, u32[]{:S(2)}, u32[]{:S(2)}) collective-permute-start(bf16[32,1024]{1,0:T(8,128)(2,1)S(1)} %get-tuple-element.49.after_ref), channel_id=1, source_target_pairs={{0,4},{4,0},{27,31},{31,27}} | collective-permute-start | bytes 196616 | tf_op jit(solution)/shard_map/cond/branch_0_fun/ppermute | solution.py:210
  5.3 2.2 %load.4.maps_ref = bf16[2,1024,1024]{2,1,0:T(8,128)(2,1)S(1)} custom-call(s32[1]{0:T(128)} %bitcast.lead_ref, bf16[2,1024,1024]{2,1,0:T(8,128)(2,1)} %bitcast.20, bf16[32,1024]{1,0:T(8,128)(2,1)S(1)} %get-tuple-element.49.after_ref), custom_call_target="tpu_custom_call" | custom-call | tf_op jit(solution)/shard_map/cond/branch_0_fun/load/pallas_call | solution.py:135
  7.6 0.0 collective-permute-done.2.x_ref
  7.6 0.9 %collective-permute-done.1.z_ref = bf16[32,1024]{1,0:T(8,128)(2,1)S(1)} collective-permute-done((bf16[32,1024]{1,0:T(8,128)(2,1)S(1)}, bf16[32,1024]{1,0:T(8,128)(2,1)S(1)}, u32[]{:S(2)}, u32[]{:S(2)}) %collective-permute-start.1) | collective-permute-done | bytes 65568 | tf_op jit(solution)/shard_map/cond/branch_0_fun/ppermute | solution.py:210
  8.4 0.0 collective-permute-done.y_ref
  8.4 0.7 %collective-permute-start.5 = (bf16[32,1024]{1,0:T(8,128)(2,1)S(1)}, bf16[32,1024]{1,0:T(8,128)(2,1)S(1)}, u32[]{:S(2)}, u32[]{:S(2)}) collective-permute-start(bf16[32,1024]{1,0:T(8,128)(2,1)S(1)} %get-tuple-element.53), channel_id=1, source_target_pairs={{0,8},{4,12},{5,13},{12,20},{19,11},{26,18},{27,19},{31,23}} | collective-permute-start | bytes 196616 | tf_op jit(solution)/shard_map/cond/branch_0_fun/ppermute | solution.py:210
  9.1 2.7 %collective-permute-start.4 = (bf16[32,1024]{1,0:T(8,128)(2,1)S(1)}, bf16[32,1024]{1,0:T(8,128)(2,1)S(1)}, u32[]{:S(2)}, u32[]{:S(2)}) collective-permute-start(bf16[32,1024]{1,0:T(8,128)(2,1)S(1)} %get-tuple-element.53), channel_id=1, source_target_pairs={{0,1},{2,3},{3,2},{4,5},{5,6},{9,10},{10,9},{12,13},{14,15},{15,14... | collective-permute-start | bytes 196616 | tf_op jit(solution)/shard_map/cond/branch_0_fun/ppermute | solution.py:210
  11.8 0.7 %collective-permute-start.3 = (bf16[32,1024]{1,0:T(8,128)(2,1)S(1)}, bf16[32,1024]{1,0:T(8,128)(2,1)S(1)}, u32[]{:S(2)}, u32[]{:S(2)}) collective-permute-start(bf16[32,1024]{1,0:T(8,128)(2,1)S(1)} %get-tuple-element.53), channel_id=1, source_target_pairs={{1,5},{5,1},{8,12},{12,8},{19,23},{23,19},{26,30},{30,26}} | collective-permute-start | bytes 196616 | tf_op jit(solution)/shard_map/cond/branch_0_fun/ppermute | solution.py:210
  12.5 0.0 collective-permute-done.5.x_ref
  12.5 2.8 %collective-permute-done.4.z_ref = bf16[32,1024]{1,0:T(8,128)(2,1)S(1)} collective-permute-done((bf16[32,1024]{1,0:T(8,128)(2,1)S(1)}, bf16[32,1024]{1,0:T(8,128)(2,1)S(1)}, u32[]{:S(2)}, u32[]{:S(2)}) %collective-permute-start.4) | collective-permute-done | bytes 65568 | tf_op jit(solution)/shard_map/cond/branch_0_fun/ppermute | solution.py:210
  15.3 0.0 collective-permute-done.3.y_ref
  15.3 1.3 %collective-permute-start.8 = (bf16[32,1024]{1,0:T(8,128)(2,1)S(1)}, bf16[32,1024]{1,0:T(8,128)(2,1)S(1)}, u32[]{:S(2)}, u32[]{:S(2)}) collective-permute-start(bf16[32,1024]{1,0:T(8,128)(2,1)S(1)} %get-tuple-element.55), channel_id=1, source_target_pairs={{1,9},{6,14},{8,16},{11,3},{12,4},{13,21},{18,10},{19,27},{20,28},... | collective-permute-start | bytes 196616 | tf_op jit(solution)/shard_map/cond/branch_0_fun/ppermute | solution.py:210
  16.6 1.3 %collective-permute-start.7 = (bf16[32,1024]{1,0:T(8,128)(2,1)S(1)}, bf16[32,1024]{1,0:T(8,128)(2,1)S(1)}, u32[]{:S(2)}, u32[]{:S(2)}) collective-permute-start(bf16[32,1024]{1,0:T(8,128)(2,1)S(1)} %get-tuple-element.55), channel_id=1, source_target_pairs={{1,2},{5,4},{6,7},{8,9},{11,10},{13,14},{18,17},{20,21},{23,22},{2... | collective-permute-start | bytes 196616 | tf_op jit(solution)/shard_map/cond/branch_0_fun/ppermute | solution.py:210
  17.9 0.7 %collective-permute-start.6 = (bf16[32,1024]{1,0:T(8,128)(2,1)S(1)}, bf16[32,1024]{1,0:T(8,128)(2,1)S(1)}, u32[]{:S(2)}, u32[]{:S(2)}) collective-permute-start(bf16[32,1024]{1,0:T(8,128)(2,1)S(1)} %get-tuple-element.55), channel_id=1, source_target_pairs={{2,6},{6,2},{9,13},{11,15},{13,9},{15,11},{16,20},{18,22},{20,16},... | collective-permute-start | bytes 196616 | tf_op jit(solution)/shard_map/cond/branch_0_fun/ppermute | solution.py:210
  18.6 5.1 %collective-permute-done.8.x_ref = bf16[32,1024]{1,0:T(8,128)(2,1)S(1)} collective-permute-done((bf16[32,1024]{1,0:T(8,128)(2,1)S(1)}, bf16[32,1024]{1,0:T(8,128)(2,1)S(1)}, u32[]{:S(2)}, u32[]{:S(2)}) %collective-permute-start.8) | collective-permute-done | bytes 65568 | tf_op jit(solution)/shard_map/cond/branch_0_fun/ppermute | solution.py:210
  23.7 0.7 %collective-permute-done.7.z_ref = bf16[32,1024]{1,0:T(8,128)(2,1)S(1)} collective-permute-done((bf16[32,1024]{1,0:T(8,128)(2,1)S(1)}, bf16[32,1024]{1,0:T(8,128)(2,1)S(1)}, u32[]{:S(2)}, u32[]{:S(2)}) %collective-permute-start.7) | collective-permute-done | bytes 65568 | tf_op jit(solution)/shard_map/cond/branch_0_fun/ppermute | solution.py:210
  24.4 0.0 collective-permute-done.6.y_ref
  24.4 0.5 hop3.4
  24.9 2.0 %collective-permute-start.11 = (bf16[32,1024]{1,0:T(8,128)(2,1)S(1)}, bf16[32,1024]{1,0:T(8,128)(2,1)S(1)}, u32[]{:S(2)}, u32[]{:S(2)}) collective-permute-start(bf16[32,1024]{1,0:T(8,128)(2,1)S(1)} %get-tuple-element.57), channel_id=1, source_target_pairs={{2,10},{7,15},{8,0},{9,17},{10,2},{11,19},{13,5},{14,22},{15,7},{1... | collective-permute-start | bytes 196616 | tf_op jit(solution)/shard_map/cond/branch_0_fun/ppermute | solution.py:210
  26.9 4.5 %collective-permute-start.10 = (bf16[32,1024]{1,0:T(8,128)(2,1)S(1)}, bf16[32,1024]{1,0:T(8,128)(2,1)S(1)}, u32[]{:S(2)}, u32[]{:S(2)}) collective-permute-start(bf16[32,1024]{1,0:T(8,128)(2,1)S(1)} %get-tuple-element.57), channel_id=1, source_target_pairs={{0,1},{2,3},{3,2},{4,5},{5,6},{9,10},{10,9},{12,13},{14,15},{15,14... | collective-permute-start | bytes 196616 | tf_op jit(solution)/shard_map/cond/branch_0_fun/ppermute | solution.py:210
  31.4 1.9 %collective-permute-start.9 = (bf16[32,1024]{1,0:T(8,128)(2,1)S(1)}, bf16[32,1024]{1,0:T(8,128)(2,1)S(1)}, u32[]{:S(2)}, u32[]{:S(2)}) collective-permute-start(bf16[32,1024]{1,0:T(8,128)(2,1)S(1)} %get-tuple-element.57), channel_id=1, source_target_pairs={{3,7},{7,3},{10,14},{14,10},{17,21},{21,17},{24,28},{28,24}} | collective-permute-start | bytes 196616 | tf_op jit(solution)/shard_map/cond/branch_0_fun/ppermute | solution.py:210
  33.3 0.0 collective-permute-done.11.x_ref
  33.3 0.3 collective-permute-done.10.z_ref
  33.6 0.9 %collective-permute-done.9.y_ref = bf16[32,1024]{1,0:T(8,128)(2,1)S(1)} collective-permute-done((bf16[32,1024]{1,0:T(8,128)(2,1)S(1)}, bf16[32,1024]{1,0:T(8,128)(2,1)S(1)}, u32[]{:S(2)}, u32[]{:S(2)}) %collective-permute-start.9) | collective-permute-done | bytes 65568 | tf_op jit(solution)/shard_map/cond/branch_0_fun/ppermute | solution.py:210
  34.5 0.5 hop4.4
  35.0 1.3 %collective-permute-start.14 = (bf16[32,1024]{1,0:T(8,128)(2,1)S(1)}, bf16[32,1024]{1,0:T(8,128)(2,1)S(1)}, u32[]{:S(2)}, u32[]{:S(2)}) collective-permute-start(bf16[32,1024]{1,0:T(8,128)(2,1)S(1)} %get-tuple-element.59), channel_id=1, source_target_pairs={{3,11},{9,1},{10,18},{14,6},{15,23},{16,8},{17,25},{21,13},{22,30}... | collective-permute-start | bytes 196616 | tf_op jit(solution)/shard_map/cond/branch_0_fun/ppermute | solution.py:210
  36.3 1.5 %collective-permute-start.13 = (bf16[32,1024]{1,0:T(8,128)(2,1)S(1)}, bf16[32,1024]{1,0:T(8,128)(2,1)S(1)}, u32[]{:S(2)}, u32[]{:S(2)}) collective-permute-start(bf16[32,1024]{1,0:T(8,128)(2,1)S(1)} %get-tuple-element.59), channel_id=1, source_target_pairs={{1,0},{2,1},{6,5},{7,6},{9,8},{10,11},{13,12},{14,13},{17,18},{18,... | collective-permute-start | bytes 196616 | tf_op jit(solution)/shard_map/cond/branch_0_fun/ppermute | solution.py:210
  37.8 0.7 %collective-permute-start.12 = (bf16[32,1024]{1,0:T(8,128)(2,1)S(1)}, bf16[32,1024]{1,0:T(8,128)(2,1)S(1)}, u32[]{:S(2)}, u32[]{:S(2)}) collective-permute-start(bf16[32,1024]{1,0:T(8,128)(2,1)S(1)} %get-tuple-element.59), channel_id=1, source_target_pairs={{2,6},{6,2},{9,13},{11,15},{13,9},{15,11},{16,20},{18,22},{20,16},... | collective-permute-start | bytes 196616 | tf_op jit(solution)/shard_map/cond/branch_0_fun/ppermute | solution.py:210
  38.5 0.0 collective-permute-done.14.x_ref
  38.5 1.2 %collective-permute-done.13.z_ref = bf16[32,1024]{1,0:T(8,128)(2,1)S(1)} collective-permute-done((bf16[32,1024]{1,0:T(8,128)(2,1)S(1)}, bf16[32,1024]{1,0:T(8,128)(2,1)S(1)}, u32[]{:S(2)}, u32[]{:S(2)}) %collective-permute-start.13) | collective-permute-done | bytes 65568 | tf_op jit(solution)/shard_map/cond/branch_0_fun/ppermute | solution.py:210
  39.7 0.0 collective-permute-done.12.y_ref
  39.7 4.3 %collective-permute-start.17 = (bf16[32,1024]{1,0:T(8,128)(2,1)S(1)}, bf16[32,1024]{1,0:T(8,128)(2,1)S(1)}, u32[]{:S(2)}, u32[]{:S(2)}) collective-permute-start(bf16[32,1024]{1,0:T(8,128)(2,1)S(1)} %get-tuple-element.61), channel_id=1, source_target_pairs={{2,10},{7,15},{8,0},{9,17},{10,2},{11,19},{13,5},{14,22},{15,7},{1... | collective-permute-start | bytes 196616 | tf_op jit(solution)/shard_map/cond/branch_0_fun/ppermute | solution.py:210
  44.0 1.8 %collective-permute-start.16 = (bf16[32,1024]{1,0:T(8,128)(2,1)S(1)}, bf16[32,1024]{1,0:T(8,128)(2,1)S(1)}, u32[]{:S(2)}, u32[]{:S(2)}) collective-permute-start(bf16[32,1024]{1,0:T(8,128)(2,1)S(1)} %get-tuple-element.61), channel_id=1, source_target_pairs={{1,0},{2,1},{6,5},{7,6},{9,8},{10,11},{13,12},{14,13},{17,18},{18,... | collective-permute-start | bytes 196616 | tf_op jit(solution)/shard_map/cond/branch_0_fun/ppermute | solution.py:210
  45.8 0.7 %collective-permute-start.15 = (bf16[32,1024]{1,0:T(8,128)(2,1)S(1)}, bf16[32,1024]{1,0:T(8,128)(2,1)S(1)}, u32[]{:S(2)}, u32[]{:S(2)}) collective-permute-start(bf16[32,1024]{1,0:T(8,128)(2,1)S(1)} %get-tuple-element.61), channel_id=1, source_target_pairs={{1,5},{5,1},{8,12},{12,8},{19,23},{23,19},{26,30},{30,26}} | collective-permute-start | bytes 196616 | tf_op jit(solution)/shard_map/cond/branch_0_fun/ppermute | solution.py:210
  46.5 0.3 collective-permute-done.17.x_ref
  46.8 0.9 %collective-permute-done.16.z_ref = bf16[32,1024]{1,0:T(8,128)(2,1)S(1)} collective-permute-done((bf16[32,1024]{1,0:T(8,128)(2,1)S(1)}, bf16[32,1024]{1,0:T(8,128)(2,1)S(1)}, u32[]{:S(2)}, u32[]{:S(2)}) %collective-permute-start.16) | collective-permute-done | bytes 65568 | tf_op jit(solution)/shard_map/cond/branch_0_fun/ppermute | solution.py:210
  47.7 0.0 collective-permute-done.15.y_ref
  47.7 1.3 %collective-permute-start.20 = (bf16[32,1024]{1,0:T(8,128)(2,1)S(1)}, bf16[32,1024]{1,0:T(8,128)(2,1)S(1)}, u32[]{:S(2)}, u32[]{:S(2)}) collective-permute-start(bf16[32,1024]{1,0:T(8,128)(2,1)S(1)} %get-tuple-element.63), channel_id=1, source_target_pairs={{1,9},{6,14},{8,16},{11,3},{12,4},{13,21},{18,10},{19,27},{20,28},... | collective-permute-start | bytes 196616 | tf_op jit(solution)/shard_map/cond/branch_0_fun/ppermute | solution.py:210
  49.0 1.3 %collective-permute-start.19 = (bf16[32,1024]{1,0:T(8,128)(2,1)S(1)}, bf16[32,1024]{1,0:T(8,128)(2,1)S(1)}, u32[]{:S(2)}, u32[]{:S(2)}) collective-permute-start(bf16[32,1024]{1,0:T(8,128)(2,1)S(1)} %get-tuple-element.63), channel_id=1, source_target_pairs={{1,2},{5,4},{6,7},{8,9},{11,10},{13,14},{18,17},{20,21},{23,22},{2... | collective-permute-start | bytes 196616 | tf_op jit(solution)/shard_map/cond/branch_0_fun/ppermute | solution.py:210
  50.3 0.7 %collective-permute-start.18 = (bf16[32,1024]{1,0:T(8,128)(2,1)S(1)}, bf16[32,1024]{1,0:T(8,128)(2,1)S(1)}, u32[]{:S(2)}, u32[]{:S(2)}) collective-permute-start(bf16[32,1024]{1,0:T(8,128)(2,1)S(1)} %get-tuple-element.63), channel_id=1, source_target_pairs={{0,4},{4,0},{27,31},{31,27}} | collective-permute-start | bytes 196616 | tf_op jit(solution)/shard_map/cond/branch_0_fun/ppermute | solution.py:210
  51.0 2.9 %collective-permute-done.20.x_ref = bf16[32,1024]{1,0:T(8,128)(2,1)S(1)} collective-permute-done((bf16[32,1024]{1,0:T(8,128)(2,1)S(1)}, bf16[32,1024]{1,0:T(8,128)(2,1)S(1)}, u32[]{:S(2)}, u32[]{:S(2)}) %collective-permute-start.20) | collective-permute-done | bytes 65568 | tf_op jit(solution)/shard_map/cond/branch_0_fun/ppermute | solution.py:210
  53.8 2.4 %collective-permute-done.19.z_ref = bf16[32,1024]{1,0:T(8,128)(2,1)S(1)} collective-permute-done((bf16[32,1024]{1,0:T(8,128)(2,1)S(1)}, bf16[32,1024]{1,0:T(8,128)(2,1)S(1)}, u32[]{:S(2)}, u32[]{:S(2)}) %collective-permute-start.19) | collective-permute-done | bytes 65568 | tf_op jit(solution)/shard_map/cond/branch_0_fun/ppermute | solution.py:210
  56.2 0.0 collective-permute-done.18.y_ref
  56.3 0.0 copy-start
  56.3 0.6 %copy-done = bf16[1,1,1,2,16,1024]{5,4,3,2,1,0:T(8,128)(2,1)} copy-done((bf16[1,1,1,2,16,1024]{5,4,3,2,1,0:T(8,128)(2,1)}, bf16[1,1,1,2,16,1024]{5,4,3,2,1,0:T(8,128)(2,1)S(1)}, u32[]{:S(2)}) %copy-start) | copy-done | bytes 65560
  (5 shorter events, 0.1 us)
Async XLA Ops:
  1.6 6.0 %collective-permute-start.2 = (bf16[32,1024]{1,0:T(8,128)(2,1)S(1)}, bf16[32,1024]{1,0:T(8,128)(2,1)S(1)}, u32[]{:S(2)}, u32[]{:S(2)}) collective-permute-start(bf16[32,1024]{1,0:T(8,128)(2,1)S(1)} %get-tuple-element.49.after_ref), channel_id=1, source_target_pairs={{0,8},{4,12},{5,13},{12,20},{19,11},{26,18},{27,19},{31,23}} | collective-permute-start | bytes 196616 | tf_op jit(solution)/shard_map/cond/branch_0_fun/ppermute | solution.py:210
  2.3 6.2 %collective-permute-start.1 = (bf16[32,1024]{1,0:T(8,128)(2,1)S(1)}, bf16[32,1024]{1,0:T(8,128)(2,1)S(1)}, u32[]{:S(2)}, u32[]{:S(2)}) collective-permute-start(bf16[32,1024]{1,0:T(8,128)(2,1)S(1)} %get-tuple-element.49.after_ref), channel_id=1, source_target_pairs={{0,1},{2,3},{3,2},{4,5},{5,6},{9,10},{10,9},{12,13},{14,15},{15,14... | collective-permute-start | bytes 196616 | tf_op jit(solution)/shard_map/cond/branch_0_fun/ppermute | solution.py:210
  4.6 3.8 %collective-permute-start = (bf16[32,1024]{1,0:T(8,128)(2,1)S(1)}, bf16[32,1024]{1,0:T(8,128)(2,1)S(1)}, u32[]{:S(2)}, u32[]{:S(2)}) collective-permute-start(bf16[32,1024]{1,0:T(8,128)(2,1)S(1)} %get-tuple-element.49.after_ref), channel_id=1, source_target_pairs={{0,4},{4,0},{27,31},{31,27}} | collective-permute-start | bytes 196616 | tf_op jit(solution)/shard_map/cond/branch_0_fun/ppermute | solution.py:210
  8.4 4.0 %collective-permute-start.5 = (bf16[32,1024]{1,0:T(8,128)(2,1)S(1)}, bf16[32,1024]{1,0:T(8,128)(2,1)S(1)}, u32[]{:S(2)}, u32[]{:S(2)}) collective-permute-start(bf16[32,1024]{1,0:T(8,128)(2,1)S(1)} %get-tuple-element.53), channel_id=1, source_target_pairs={{0,8},{4,12},{5,13},{12,20},{19,11},{26,18},{27,19},{31,23}} | collective-permute-start | bytes 196616 | tf_op jit(solution)/shard_map/cond/branch_0_fun/ppermute | solution.py:210
  9.1 6.2 %collective-permute-start.4 = (bf16[32,1024]{1,0:T(8,128)(2,1)S(1)}, bf16[32,1024]{1,0:T(8,128)(2,1)S(1)}, u32[]{:S(2)}, u32[]{:S(2)}) collective-permute-start(bf16[32,1024]{1,0:T(8,128)(2,1)S(1)} %get-tuple-element.53), channel_id=1, source_target_pairs={{0,1},{2,3},{3,2},{4,5},{5,6},{9,10},{10,9},{12,13},{14,15},{15,14... | collective-permute-start | bytes 196616 | tf_op jit(solution)/shard_map/cond/branch_0_fun/ppermute | solution.py:210
  11.8 3.5 %collective-permute-start.3 = (bf16[32,1024]{1,0:T(8,128)(2,1)S(1)}, bf16[32,1024]{1,0:T(8,128)(2,1)S(1)}, u32[]{:S(2)}, u32[]{:S(2)}) collective-permute-start(bf16[32,1024]{1,0:T(8,128)(2,1)S(1)} %get-tuple-element.53), channel_id=1, source_target_pairs={{1,5},{5,1},{8,12},{12,8},{19,23},{23,19},{26,30},{30,26}} | collective-permute-start | bytes 196616 | tf_op jit(solution)/shard_map/cond/branch_0_fun/ppermute | solution.py:210
  15.3 8.4 %collective-permute-start.8 = (bf16[32,1024]{1,0:T(8,128)(2,1)S(1)}, bf16[32,1024]{1,0:T(8,128)(2,1)S(1)}, u32[]{:S(2)}, u32[]{:S(2)}) collective-permute-start(bf16[32,1024]{1,0:T(8,128)(2,1)S(1)} %get-tuple-element.55), channel_id=1, source_target_pairs={{1,9},{6,14},{8,16},{11,3},{12,4},{13,21},{18,10},{19,27},{20,28},... | collective-permute-start | bytes 196616 | tf_op jit(solution)/shard_map/cond/branch_0_fun/ppermute | solution.py:210
  16.6 7.8 %collective-permute-start.7 = (bf16[32,1024]{1,0:T(8,128)(2,1)S(1)}, bf16[32,1024]{1,0:T(8,128)(2,1)S(1)}, u32[]{:S(2)}, u32[]{:S(2)}) collective-permute-start(bf16[32,1024]{1,0:T(8,128)(2,1)S(1)} %get-tuple-element.55), channel_id=1, source_target_pairs={{1,2},{5,4},{6,7},{8,9},{11,10},{13,14},{18,17},{20,21},{23,22},{2... | collective-permute-start | bytes 196616 | tf_op jit(solution)/shard_map/cond/branch_0_fun/ppermute | solution.py:210
  17.9 6.5 %collective-permute-start.6 = (bf16[32,1024]{1,0:T(8,128)(2,1)S(1)}, bf16[32,1024]{1,0:T(8,128)(2,1)S(1)}, u32[]{:S(2)}, u32[]{:S(2)}) collective-permute-start(bf16[32,1024]{1,0:T(8,128)(2,1)S(1)} %get-tuple-element.55), channel_id=1, source_target_pairs={{2,6},{6,2},{9,13},{11,15},{13,9},{15,11},{16,20},{18,22},{20,16},... | collective-permute-start | bytes 196616 | tf_op jit(solution)/shard_map/cond/branch_0_fun/ppermute | solution.py:210
  24.9 8.4 %collective-permute-start.11 = (bf16[32,1024]{1,0:T(8,128)(2,1)S(1)}, bf16[32,1024]{1,0:T(8,128)(2,1)S(1)}, u32[]{:S(2)}, u32[]{:S(2)}) collective-permute-start(bf16[32,1024]{1,0:T(8,128)(2,1)S(1)} %get-tuple-element.57), channel_id=1, source_target_pairs={{2,10},{7,15},{8,0},{9,17},{10,2},{11,19},{13,5},{14,22},{15,7},{1... | collective-permute-start | bytes 196616 | tf_op jit(solution)/shard_map/cond/branch_0_fun/ppermute | solution.py:210
  26.9 6.7 %collective-permute-start.10 = (bf16[32,1024]{1,0:T(8,128)(2,1)S(1)}, bf16[32,1024]{1,0:T(8,128)(2,1)S(1)}, u32[]{:S(2)}, u32[]{:S(2)}) collective-permute-start(bf16[32,1024]{1,0:T(8,128)(2,1)S(1)} %get-tuple-element.57), channel_id=1, source_target_pairs={{0,1},{2,3},{3,2},{4,5},{5,6},{9,10},{10,9},{12,13},{14,15},{15,14... | collective-permute-start | bytes 196616 | tf_op jit(solution)/shard_map/cond/branch_0_fun/ppermute | solution.py:210
  31.4 3.1 %collective-permute-start.9 = (bf16[32,1024]{1,0:T(8,128)(2,1)S(1)}, bf16[32,1024]{1,0:T(8,128)(2,1)S(1)}, u32[]{:S(2)}, u32[]{:S(2)}) collective-permute-start(bf16[32,1024]{1,0:T(8,128)(2,1)S(1)} %get-tuple-element.57), channel_id=1, source_target_pairs={{3,7},{7,3},{10,14},{14,10},{17,21},{21,17},{24,28},{28,24}} | collective-permute-start | bytes 196616 | tf_op jit(solution)/shard_map/cond/branch_0_fun/ppermute | solution.py:210
  35.0 3.5 %collective-permute-start.14 = (bf16[32,1024]{1,0:T(8,128)(2,1)S(1)}, bf16[32,1024]{1,0:T(8,128)(2,1)S(1)}, u32[]{:S(2)}, u32[]{:S(2)}) collective-permute-start(bf16[32,1024]{1,0:T(8,128)(2,1)S(1)} %get-tuple-element.59), channel_id=1, source_target_pairs={{3,11},{9,1},{10,18},{14,6},{15,23},{16,8},{17,25},{21,13},{22,30}... | collective-permute-start | bytes 196616 | tf_op jit(solution)/shard_map/cond/branch_0_fun/ppermute | solution.py:210
  36.3 3.4 %collective-permute-start.13 = (bf16[32,1024]{1,0:T(8,128)(2,1)S(1)}, bf16[32,1024]{1,0:T(8,128)(2,1)S(1)}, u32[]{:S(2)}, u32[]{:S(2)}) collective-permute-start(bf16[32,1024]{1,0:T(8,128)(2,1)S(1)} %get-tuple-element.59), channel_id=1, source_target_pairs={{1,0},{2,1},{6,5},{7,6},{9,8},{10,11},{13,12},{14,13},{17,18},{18,... | collective-permute-start | bytes 196616 | tf_op jit(solution)/shard_map/cond/branch_0_fun/ppermute | solution.py:210
  37.8 1.9 %collective-permute-start.12 = (bf16[32,1024]{1,0:T(8,128)(2,1)S(1)}, bf16[32,1024]{1,0:T(8,128)(2,1)S(1)}, u32[]{:S(2)}, u32[]{:S(2)}) collective-permute-start(bf16[32,1024]{1,0:T(8,128)(2,1)S(1)} %get-tuple-element.59), channel_id=1, source_target_pairs={{2,6},{6,2},{9,13},{11,15},{13,9},{15,11},{16,20},{18,22},{20,16},... | collective-permute-start | bytes 196616 | tf_op jit(solution)/shard_map/cond/branch_0_fun/ppermute | solution.py:210
  39.7 7.1 %collective-permute-start.17 = (bf16[32,1024]{1,0:T(8,128)(2,1)S(1)}, bf16[32,1024]{1,0:T(8,128)(2,1)S(1)}, u32[]{:S(2)}, u32[]{:S(2)}) collective-permute-start(bf16[32,1024]{1,0:T(8,128)(2,1)S(1)} %get-tuple-element.61), channel_id=1, source_target_pairs={{2,10},{7,15},{8,0},{9,17},{10,2},{11,19},{13,5},{14,22},{15,7},{1... | collective-permute-start | bytes 196616 | tf_op jit(solution)/shard_map/cond/branch_0_fun/ppermute | solution.py:210
  44.0 3.6 %collective-permute-start.16 = (bf16[32,1024]{1,0:T(8,128)(2,1)S(1)}, bf16[32,1024]{1,0:T(8,128)(2,1)S(1)}, u32[]{:S(2)}, u32[]{:S(2)}) collective-permute-start(bf16[32,1024]{1,0:T(8,128)(2,1)S(1)} %get-tuple-element.61), channel_id=1, source_target_pairs={{1,0},{2,1},{6,5},{7,6},{9,8},{10,11},{13,12},{14,13},{17,18},{18,... | collective-permute-start | bytes 196616 | tf_op jit(solution)/shard_map/cond/branch_0_fun/ppermute | solution.py:210
  45.8 1.9 %collective-permute-start.15 = (bf16[32,1024]{1,0:T(8,128)(2,1)S(1)}, bf16[32,1024]{1,0:T(8,128)(2,1)S(1)}, u32[]{:S(2)}, u32[]{:S(2)}) collective-permute-start(bf16[32,1024]{1,0:T(8,128)(2,1)S(1)} %get-tuple-element.61), channel_id=1, source_target_pairs={{1,5},{5,1},{8,12},{12,8},{19,23},{23,19},{26,30},{30,26}} | collective-permute-start | bytes 196616 | tf_op jit(solution)/shard_map/cond/branch_0_fun/ppermute | solution.py:210
  47.7 6.2 %collective-permute-start.20 = (bf16[32,1024]{1,0:T(8,128)(2,1)S(1)}, bf16[32,1024]{1,0:T(8,128)(2,1)S(1)}, u32[]{:S(2)}, u32[]{:S(2)}) collective-permute-start(bf16[32,1024]{1,0:T(8,128)(2,1)S(1)} %get-tuple-element.63), channel_id=1, source_target_pairs={{1,9},{6,14},{8,16},{11,3},{12,4},{13,21},{18,10},{19,27},{20,28},... | collective-permute-start | bytes 196616 | tf_op jit(solution)/shard_map/cond/branch_0_fun/ppermute | solution.py:210
  49.0 7.2 %collective-permute-start.19 = (bf16[32,1024]{1,0:T(8,128)(2,1)S(1)}, bf16[32,1024]{1,0:T(8,128)(2,1)S(1)}, u32[]{:S(2)}, u32[]{:S(2)}) collective-permute-start(bf16[32,1024]{1,0:T(8,128)(2,1)S(1)} %get-tuple-element.63), channel_id=1, source_target_pairs={{1,2},{5,4},{6,7},{8,9},{11,10},{13,14},{18,17},{20,21},{23,22},{2... | collective-permute-start | bytes 196616 | tf_op jit(solution)/shard_map/cond/branch_0_fun/ppermute | solution.py:210
  50.3 5.9 %collective-permute-start.18 = (bf16[32,1024]{1,0:T(8,128)(2,1)S(1)}, bf16[32,1024]{1,0:T(8,128)(2,1)S(1)}, u32[]{:S(2)}, u32[]{:S(2)}) collective-permute-start(bf16[32,1024]{1,0:T(8,128)(2,1)S(1)} %get-tuple-element.63), channel_id=1, source_target_pairs={{0,4},{4,0},{27,31},{31,27}} | collective-permute-start | bytes 196616 | tf_op jit(solution)/shard_map/cond/branch_0_fun/ppermute | solution.py:210
  56.3 0.6 %copy-start = (bf16[1,1,1,2,16,1024]{5,4,3,2,1,0:T(8,128)(2,1)}, bf16[1,1,1,2,16,1024]{5,4,3,2,1,0:T(8,128)(2,1)S(1)}, u32[]{:S(2)}) copy-start(bf16[1,1,1,2,16,1024]{5,4,3,2,1,0:T(8,128)(2,1)S(1)} %get-tuple-element.308) | copy-start | bytes 196612
where the time goes:
time: 57.1 us; the launch traced here: 56.9 us
  starting transfers between devices  32.8 us (57%)
  waiting for transfers between devices  18.4 us (32%)
  Pallas kernels  4.15 us (7%)
  between operations  0.68 us (1%)
  local copies, waits for them, and re-layouts  0.62 us (1%)
    ppermute x21, starting transfers between devices, wave(): came[axis] = lax.ppermute(message, AXES, pairs_of(sizes, bits, axis, hop))  32.8 us
    ppermute x21, waiting for transfers between devices, wave(): came[axis] = lax.ppermute(message, AXES, pairs_of(sizes, bits, axis, hop))  18.4 us
    pallas_call x1, Pallas kernels, load(): pl.pallas_call(load_kernel, out_shape=pltpu.VMEM(maps.shape, maps.dtype),...  2.24 us
  transfers between devices with their start and end apart: 21, of which 11 were waited for; matrix products, arithmetic and copies ran while one was open for 0% of the time, Pallas kernels for 4%

commit v1 on v0

--- a/solution.py
+++ b/solution.py
@@ -56,21 +56,43 @@
 
 
 SHARED = (
-    ((1, 2), (3, 7), (4, 6), (5,)),
-    ((1, 7), (2, 6), (3, 5), (4,)),
-    ((1, 2, 4), (3, 7), (5, 6)),
+    (
+        (0, 1, 2, 3, 4, 5, 6),
+        (7, 8, 9, 3, 10, 11, 6),
+        (7, 9, 8, 12, 11, 10, 6),
+        (0, 2, 1, 12, 5, 4, 6),
+    ),
+    (
+        (0, 1, 2, 3, 1, 4, 5),
+        (0, 2, 4, 6, 7, 2, 5),
+        (5, 2, 8, 9, 4, 2, 3),
+        (5, 4, 1, 3, 2, 1, 0),
+    ),
+    (
+        (0, 1, 2, 3, 4, 5, 6),
+        (7, 8, 9, 10, 11, 12, 6),
+        (8, 7, 13, 3, 12, 11, 6),
+        (1, 0, 14, 10, 5, 4, 6),
+    ),
 )
 
 
+def kind_bits(kind):
+    return (kind & 1, 1, kind >> 1)
+
+
 def pairs_of(sizes, bits, axis, hop):
     deepest = sum(size - 1 for size in sizes)
     own = hop_edges(sizes, bits, axis, hop)
-    group = next((group for group in SHARED[axis] if hop in group), (hop,))
-    edges = [edge for other in group if other <= deepest for edge in hop_edges(sizes, bits, axis, other)]
-    edges = sorted(set(edges))
-    if clash(edges):
-        edges = own
-    assert not clash(edges)
+    number_of = SHARED[axis][bits[0] + 2 * bits[2]][hop - 1]
+    edges = set(own)
+    for kind, row in enumerate(SHARED[axis]):
+        for other, found in enumerate(row, 1):
+            if found == number_of and other <= deepest:
+                edges.update(hop_edges(sizes, kind_bits(kind), axis, other))
+    if clash(sorted(edges)):
+        edges = set(own)
+    assert not clash(sorted(edges))
     return sorted((number(sizes, source), number(sizes, target)) for source, target in edges)
 
 
@@ -78,39 +100,45 @@
     return depth_of(sizes, bits, tuple(lax.axis_index(axis) for axis in AXES))
 
 
-def begin_kernel(sizes, bits, lead_ref, sources_ref, message_ref, traces_ref, held_ref, arrived):
-    lead = lead_ref[0]
+def chains_sent(hop, deepest):
+    return range(max(0, hop - STEPS), min(max(0, deepest - STEPS), hop - 1) + 1)
+
+
+def begin_kernel(sizes, bits, lead_hbm, sources_hbm, message_ref, traces_ref, held_ref, lead_ref, raw_ref, arrived):
     copies = [
-        pltpu.make_async_copy(
-            sources_ref.at[lead if slot == 0 else 1 - lead], held_ref.at[slot], arrived.at[slot]
-        )
-        for slot in range(2)
+        pltpu.make_async_copy(sources_hbm, raw_ref, arrived.at[0]),
+        pltpu.make_async_copy(lead_hbm, lead_ref, arrived.at[1]),
     ]
     for copy in copies:
         copy.start()
     for copy in copies:
         copy.wait()
-    traces_ref[...] = held_ref[...].astype(traces_ref.dtype)
-    rows = held_ref.shape[1]
-    if message_ref.shape[0] > rows:
-        message_ref[rows:] = jnp.zeros_like(message_ref[rows:])
+    lead = lead_ref[0]
     entry = my_depth(sizes, bits) == 0
-    message_ref[:rows] = jnp.where(entry, traces_ref[0], traces_ref[1])
-
-
-def begin(sizes, bits, chains, lead, sources):
-    _, rows, face = sources.shape
+    message_ref[...] = raw_ref[jnp.where(entry, lead, 1 - lead)].astype(message_ref.dtype)
+    for slot in range(2):
+        source = raw_ref[lead if slot == 0 else 1 - lead]
+        held_ref[slot] = source
+        traces_ref[slot] = source.astype(traces_ref.dtype)
+
+
+def begin(sizes, bits, lead, sources):
     vmem = pl.BlockSpec(memory_space=pltpu.VMEM)
+    hbm = pl.BlockSpec(memory_space=pl.ANY)
     return pl.pallas_call(
         functools.partial(begin_kernel, sizes, bits),
         out_shape=(
-            pltpu.VMEM((chains * rows, face), jnp.bfloat16),
+            pltpu.VMEM(sources.shape[1:], jnp.bfloat16),
             pltpu.VMEM(sources.shape, jnp.bfloat16),
             pltpu.VMEM(sources.shape, sources.dtype),
         ),
-        in_specs=[pl.BlockSpec(memory_space=pltpu.SMEM), pl.BlockSpec(memory_space=pl.ANY)],
+        in_specs=[hbm, hbm],
         out_specs=(vmem, vmem, vmem),
-        scratch_shapes=[pltpu.SemaphoreType.DMA((2,))],
+        scratch_shapes=[
+            pltpu.SMEM(lead.shape, lead.dtype),
+            pltpu.VMEM(sources.shape, sources.dtype),
+            pltpu.SemaphoreType.DMA((2,)),
+        ],
         compiler_params=ROOM,
         name="begin",
     )(lead, sources)
@@ -162,23 +190,37 @@
     @pl.when((depth == hop) | (back == hop))
     def _():
         slot = jnp.where(depth == hop, 0, 1)
-        summed = x_ref[...].astype(jnp.float32) + y_ref[...].astype(jnp.float32)
-        summed = summed + z_ref[...].astype(jnp.float32)
+        summed = None
+        for axis, ref in enumerate((x_ref, y_ref, z_ref)):
+            index = lax.axis_index(AXES[axis])
+            lower, upper = index > 0, index < sizes[axis] - 1
+            inside = jnp.where(
+                (depth == hop) == bool(bits[axis]), lower.astype(jnp.int32), upper.astype(jnp.int32)
+            )
+            came = jnp.where(inside == 1, ref[...].astype(jnp.float32), 0.0)
+            summed = came if summed is None else summed + came
         mapped = jnp.dot(
             summed.astype(jnp.bfloat16), maps_ref[slot], preferred_element_type=jnp.float32
         )
         source = sources_ref[slot]
-        for chain in range(mapped.shape[0] // rows):
-            part = slice(chain * rows, (chain + 1) * rows)
-            new = (mapped[part] + source).astype(jnp.bfloat16)
-            if not last:
-                results[0][part] = new
+        came = chains_sent(hop, deepest)
+        kept = came if last else chains_sent(hop + 1, deepest)
+        for chain in sorted({*came, *kept}):
+            if chain in came:
+                at = came.index(chain) * rows
+                new = (mapped[at : at + rows] + source).astype(jnp.bfloat16)
+            else:
+                new = source.astype(jnp.bfloat16)
+            if not last and chain in kept:
+                at = kept.index(chain) * rows
+                results[0][at : at + rows] = new
             if chain == max(0, hop - STEPS):
                 traces_ref[place_of(slot)] = new
 
 
 def take_hop(hop, sizes, bits, lead, came, maps, sources, traces):
-    last = hop == sum(size - 1 for size in sizes)
+    deepest = sum(size - 1 for size in sizes)
+    last = hop == deepest
     vmem = pl.BlockSpec(memory_space=pltpu.VMEM)
     came = [came[axis] for axis in reversed(ORDER)]
     held = [pltpu.with_memory_space_constraint(a, pltpu.VMEM) for a in came]
@@ -186,7 +228,9 @@
     shapes = (jax.ShapeDtypeStruct(traces.shape, traces.dtype),)
     if not last:
         shapes = (
-            pltpu.VMEM(came[0].shape, came[0].dtype),
+            pltpu.VMEM(
+                (len(chains_sent(hop + 1, deepest)) * sources.shape[1], sources.shape[2]), traces.dtype
+            ),
             pltpu.VMEM(traces.shape, traces.dtype),
         )
     results = pl.pallas_call(
@@ -202,8 +246,7 @@
 
 def wave(sizes, bits, lead, maps, sources):
     deepest = sum(size - 1 for size in sizes)
-    chains = max(0, deepest - STEPS) + 1
-    message, traces, sources = begin(sizes, bits, chains, lead, sources)
+    message, traces, sources = begin(sizes, bits, lead, sources)
     for hop in range(1, deepest + 1):
         came = [None] * 3
         for axis in ORDER:
@@ -251,8 +294,7 @@
         kind = (code & 1) + 2 * (jnp.right_shift(code, 2) & 1)
 
         def branch(kind):
-            bits = (kind & 1, 1, kind >> 1)
-            return lambda *operands: wave(sizes, bits, *operands)
+            return lambda *operands: wave(sizes, kind_bits(kind), *operands)
 
         traces = lax.switch(
             kind, [branch(kind) for kind in range(4)], lead.reshape(1), maps, rows

time: 57.1 us -> 52.7 us (0.923)
  the two profiles are of different devices: /device:TPU:12 before, /device:TPU:0 now
where the time goes in v1:
time: 52.7 us; the launch traced here: 52.3 us
  starting transfers between devices  27.1 us (51%)
  waiting for transfers between devices  19.4 us (37%)
  Pallas kernels  4.22 us (8%)
  between operations  0.68 us (1%)
  local copies, waits for them, and re-layouts  0.62 us (1%)
    ppermute x21, starting transfers between devices, wave(): came[axis] = lax.ppermute(message, AXES, pairs_of(sizes, bits, axis, hop))  27.1 us
    ppermute x21, waiting for transfers between devices, wave(): came[axis] = lax.ppermute(message, AXES, pairs_of(sizes, bits, axis, hop))  19.4 us
    pallas_call x1, Pallas kernels, load(): pl.pallas_call(load_kernel, out_shape=pltpu.VMEM(maps.shape, maps.dtype),...  2.24 us
  transfers between devices with their start and end apart: 21, of which 7 were waited for; matrix products, arithmetic and copies ran while one was open for 0% of the time, Pallas kernels for 4%

profile of v1, /device:TPU:0, one launch (start us, length us, event | category | flops | bytes accessed | tf_op | source)
XLA Modules:
  0.0 52.3 jit_solution(13083452810414728725)
XLA Ops:
  0.7 51.0 %conditional.1 = (bf16[1,1,1,2,16,1024]{5,4,3,2,1,0:T(8,128)(2,1)S(1)}) conditional(s32[]{:T(128)} %clamp.3, (s32[]{:T(128)}, f32[1,1,1,2,16,1024]{5,4,3,2,1,0:T(8,128)}, bf16[1,1,1,2,1024,1024]{5,4,3,2,1,0:T(8,128)(2,1)}) %tuple.21, (s32[]{:T(128)}, f32[1,1,1,2,16,1024]{5,4,3,2,1,0:T(8,128)}, ...), branch_computations={%region_0.1_spmd, %region_1.2_spmd, %region_2.3_spmd, %region_3.4_... | conditional | bytes 4719440 | solution.py:299
  0.7 1.0 %begin.5 = (bf16[16,1024]{1,0:T(8,128)(2,1)S(1)}, bf16[2,16,1024]{2,1,0:T(8,128)(2,1)S(1)}, f32[2,16,1024]{2,1,0:T(8,128)S(1)}) custom-call(s32[1]{0:T(128)} %bitcast.4.lead_hbm.lead_ref, f32[2,16,1024]{2,1,0:T(8,128)} %bitcast.25), custom_call_target="tpu_custom_call" | custom-call | tf_op jit(solution)/shard_map/cond/branch_1_fun/begin/pallas_call | solution.py:128
  1.6 0.7 %collective-permute-start.23 = (bf16[16,1024]{1,0:T(8,128)(2,1)S(1)}, bf16[16,1024]{1,0:T(8,128)(2,1)S(1)}, u32[]{:S(2)}, u32[]{:S(2)}) collective-permute-start(bf16[16,1024]{1,0:T(8,128)(2,1)S(1)} %get-tuple-element.67.after_ref), channel_id=1, source_target_pairs={{3,11},{7,15},{24,16},{28,20}} | collective-permute-start | bytes 98312 | tf_op jit(solution)/shard_map/cond/branch_1_fun/ppermute | solution.py:253
  2.3 0.7 %collective-permute-start.22 = (bf16[16,1024]{1,0:T(8,128)(2,1)S(1)}, bf16[16,1024]{1,0:T(8,128)(2,1)S(1)}, u32[]{:S(2)}, u32[]{:S(2)}) collective-permute-start(bf16[16,1024]{1,0:T(8,128)(2,1)S(1)} %get-tuple-element.67.after_ref), channel_id=1, source_target_pairs={{3,2},{6,5},{15,14},{16,17},{25,26},{28,29}} | collective-permute-start | bytes 98312 | tf_op jit(solution)/shard_map/cond/branch_1_fun/ppermute | solution.py:253
  3.0 1.3 %collective-permute-start.21 = (bf16[16,1024]{1,0:T(8,128)(2,1)S(1)}, bf16[16,1024]{1,0:T(8,128)(2,1)S(1)}, u32[]{:S(2)}, u32[]{:S(2)}) collective-permute-start(bf16[16,1024]{1,0:T(8,128)(2,1)S(1)} %get-tuple-element.67.after_ref), channel_id=1, source_target_pairs={{3,7},{4,0},{27,31},{28,24}} | collective-permute-start | bytes 98312 | tf_op jit(solution)/shard_map/cond/branch_1_fun/ppermute | solution.py:253
  4.3 2.2 %load.5.maps_ref = bf16[2,1024,1024]{2,1,0:T(8,128)(2,1)S(1)} custom-call(s32[1]{0:T(128)} %bitcast.4.lead_hbm.lead_ref, bf16[2,1024,1024]{2,1,0:T(8,128)(2,1)} %bitcast.21, bf16[16,1024]{1,0:T(8,128)(2,1)S(1)} %get-tuple-element.67.after_ref), custom_call_target="tpu_custom_call" | custom-call | tf_op jit(solution)/shard_map/cond/branch_1_fun/load/pallas_call | solution.py:163
  6.5 0.0 collective-permute-done.23.x_ref
  6.6 0.0 collective-permute-done.22.z_ref
  6.6 0.0 collective-permute-done.21.y_ref
  6.6 1.3 %collective-permute-start.26 = (bf16[32,1024]{1,0:T(8,128)(2,1)S(1)}, bf16[32,1024]{1,0:T(8,128)(2,1)S(1)}, u32[]{:S(2)}, u32[]{:S(2)}) collective-permute-start(bf16[32,1024]{1,0:T(8,128)(2,1)S(1)} %get-tuple-element.71), channel_id=1, source_target_pairs={{2,10},{5,13},{7,15},{8,0},{11,19},{14,22},{17,9},{20,12},{23,31},... | collective-permute-start | bytes 196616 | tf_op jit(solution)/shard_map/cond/branch_1_fun/ppermute | solution.py:253
  7.9 0.7 %collective-permute-start.25 = (bf16[32,1024]{1,0:T(8,128)(2,1)S(1)}, bf16[32,1024]{1,0:T(8,128)(2,1)S(1)}, u32[]{:S(2)}, u32[]{:S(2)}) collective-permute-start(bf16[32,1024]{1,0:T(8,128)(2,1)S(1)} %get-tuple-element.71), channel_id=1, source_target_pairs={{2,1},{7,6},{11,10},{20,21},{24,25},{29,30}} | collective-permute-start | bytes 196616 | tf_op jit(solution)/shard_map/cond/branch_1_fun/ppermute | solution.py:253
  8.6 0.7 %collective-permute-start.24 = (bf16[32,1024]{1,0:T(8,128)(2,1)S(1)}, bf16[32,1024]{1,0:T(8,128)(2,1)S(1)}, u32[]{:S(2)}, u32[]{:S(2)}) collective-permute-start(bf16[32,1024]{1,0:T(8,128)(2,1)S(1)} %get-tuple-element.71), channel_id=1, source_target_pairs={{2,6},{6,2},{11,15},{13,9},{15,11},{16,20},{18,22},{20,16},{25,29}... | collective-permute-start | bytes 196616 | tf_op jit(solution)/shard_map/cond/branch_1_fun/ppermute | solution.py:253
  9.2 3.5 %collective-permute-done.26.x_ref = bf16[32,1024]{1,0:T(8,128)(2,1)S(1)} collective-permute-done((bf16[32,1024]{1,0:T(8,128)(2,1)S(1)}, bf16[32,1024]{1,0:T(8,128)(2,1)S(1)}, u32[]{:S(2)}, u32[]{:S(2)}) %collective-permute-start.26) | collective-permute-done | bytes 65568 | tf_op jit(solution)/shard_map/cond/branch_1_fun/ppermute | solution.py:253
  12.8 0.0 collective-permute-done.25.z_ref
  12.8 0.0 collective-permute-done.24.y_ref
  12.8 0.7 %collective-permute-start.29 = (bf16[32,1024]{1,0:T(8,128)(2,1)S(1)}, bf16[32,1024]{1,0:T(8,128)(2,1)S(1)}, u32[]{:S(2)}, u32[]{:S(2)}) collective-permute-start(bf16[32,1024]{1,0:T(8,128)(2,1)S(1)} %get-tuple-element.73), channel_id=1, source_target_pairs={{1,9},{3,11},{6,14},{10,18},{12,4},{15,23},{16,8},{19,27},{21,13},... | collective-permute-start | bytes 196616 | tf_op jit(solution)/shard_map/cond/branch_1_fun/ppermute | solution.py:253
  13.5 1.3 %collective-permute-start.28 = (bf16[32,1024]{1,0:T(8,128)(2,1)S(1)}, bf16[32,1024]{1,0:T(8,128)(2,1)S(1)}, u32[]{:S(2)}, u32[]{:S(2)}) collective-permute-start(bf16[32,1024]{1,0:T(8,128)(2,1)S(1)} %get-tuple-element.73), channel_id=1, source_target_pairs={{1,0},{6,5},{10,9},{12,13},{15,14},{16,17},{19,18},{21,22},{25,26}... | collective-permute-start | bytes 196616 | tf_op jit(solution)/shard_map/cond/branch_1_fun/ppermute | solution.py:253
  14.8 0.7 %collective-permute-start.27 = (bf16[32,1024]{1,0:T(8,128)(2,1)S(1)}, bf16[32,1024]{1,0:T(8,128)(2,1)S(1)}, u32[]{:S(2)}, u32[]{:S(2)}) collective-permute-start(bf16[32,1024]{1,0:T(8,128)(2,1)S(1)} %get-tuple-element.73), channel_id=1, source_target_pairs={{1,5},{8,12},{10,14},{12,8},{19,23},{21,17},{23,19},{30,26}} | collective-permute-start | bytes 196616 | tf_op jit(solution)/shard_map/cond/branch_1_fun/ppermute | solution.py:253
  15.4 0.0 collective-permute-done.29.x_ref
  15.4 9.5 %collective-permute-done.28.z_ref = bf16[32,1024]{1,0:T(8,128)(2,1)S(1)} collective-permute-done((bf16[32,1024]{1,0:T(8,128)(2,1)S(1)}, bf16[32,1024]{1,0:T(8,128)(2,1)S(1)}, u32[]{:S(2)}, u32[]{:S(2)}) %collective-permute-start.28) | collective-permute-done | bytes 65568 | tf_op jit(solution)/shard_map/cond/branch_1_fun/ppermute | solution.py:253
  24.9 0.0 collective-permute-done.27.y_ref
  25.0 0.5 hop3.5
  25.4 1.9 %collective-permute-start.32 = (bf16[32,1024]{1,0:T(8,128)(2,1)S(1)}, bf16[32,1024]{1,0:T(8,128)(2,1)S(1)}, u32[]{:S(2)}, u32[]{:S(2)}) collective-permute-start(bf16[32,1024]{1,0:T(8,128)(2,1)S(1)} %get-tuple-element.75), channel_id=1, source_target_pairs={{0,8},{2,10},{5,13},{7,15},{8,0},{9,17},{10,2},{13,5},{14,22},{15,... | collective-permute-start | bytes 196616 | tf_op jit(solution)/shard_map/cond/branch_1_fun/ppermute | solution.py:253
  27.4 0.7 %collective-permute-start.31 = (bf16[32,1024]{1,0:T(8,128)(2,1)S(1)}, bf16[32,1024]{1,0:T(8,128)(2,1)S(1)}, u32[]{:S(2)}, u32[]{:S(2)}) collective-permute-start(bf16[32,1024]{1,0:T(8,128)(2,1)S(1)} %get-tuple-element.75), channel_id=1, source_target_pairs={{4,5},{5,4},{6,7},{7,6},{8,9},{9,8},{10,11},{11,10},{13,14},{14,13... | collective-permute-start | bytes 196616 | tf_op jit(solution)/shard_map/cond/branch_1_fun/ppermute | solution.py:253
  28.0 3.2 %collective-permute-start.30 = (bf16[32,1024]{1,0:T(8,128)(2,1)S(1)}, bf16[32,1024]{1,0:T(8,128)(2,1)S(1)}, u32[]{:S(2)}, u32[]{:S(2)}) collective-permute-start(bf16[32,1024]{1,0:T(8,128)(2,1)S(1)} %get-tuple-element.75), channel_id=1, source_target_pairs={{0,4},{4,0},{9,13},{13,9},{18,22},{22,18},{27,31},{31,27}} | collective-permute-start | bytes 196616 | tf_op jit(solution)/shard_map/cond/branch_1_fun/ppermute | solution.py:253
  31.2 0.4 collective-permute-done.32.x_ref
  31.6 0.0 collective-permute-done.31.z_ref
  31.6 0.5 collective-permute-done.30.y_ref
  32.1 0.5 hop4.5
  32.6 0.7 %collective-permute-start.35 = (bf16[32,1024]{1,0:T(8,128)(2,1)S(1)}, bf16[32,1024]{1,0:T(8,128)(2,1)S(1)}, u32[]{:S(2)}, u32[]{:S(2)}) collective-permute-start(bf16[32,1024]{1,0:T(8,128)(2,1)S(1)} %get-tuple-element.77), channel_id=1, source_target_pairs={{4,12},{8,16},{9,1},{11,3},{13,21},{14,6},{17,25},{18,10},{20,28},... | collective-permute-start | bytes 196616 | tf_op jit(solution)/shard_map/cond/branch_1_fun/ppermute | solution.py:253
  33.2 1.3 %collective-permute-start.34 = (bf16[32,1024]{1,0:T(8,128)(2,1)S(1)}, bf16[32,1024]{1,0:T(8,128)(2,1)S(1)}, u32[]{:S(2)}, u32[]{:S(2)}) collective-permute-start(bf16[32,1024]{1,0:T(8,128)(2,1)S(1)} %get-tuple-element.77), channel_id=1, source_target_pairs={{0,1},{2,3},{5,6},{9,10},{13,12},{14,15},{17,16},{18,19},{22,21},{... | collective-permute-start | bytes 196616 | tf_op jit(solution)/shard_map/cond/branch_1_fun/ppermute | solution.py:253
  34.5 0.7 %collective-permute-start.33 = (bf16[32,1024]{1,0:T(8,128)(2,1)S(1)}, bf16[32,1024]{1,0:T(8,128)(2,1)S(1)}, u32[]{:S(2)}, u32[]{:S(2)}) collective-permute-start(bf16[32,1024]{1,0:T(8,128)(2,1)S(1)} %get-tuple-element.77), channel_id=1, source_target_pairs={{5,1},{8,12},{14,10},{17,21},{23,19},{26,30}} | collective-permute-start | bytes 196616 | tf_op jit(solution)/shard_map/cond/branch_1_fun/ppermute | solution.py:253
  35.2 0.0 collective-permute-done.35.x_ref
  35.2 1.2 %collective-permute-done.34.z_ref = bf16[32,1024]{1,0:T(8,128)(2,1)S(1)} collective-permute-done((bf16[32,1024]{1,0:T(8,128)(2,1)S(1)}, bf16[32,1024]{1,0:T(8,128)(2,1)S(1)}, u32[]{:S(2)}, u32[]{:S(2)}) %collective-permute-start.34) | collective-permute-done | bytes 65568 | tf_op jit(solution)/shard_map/cond/branch_1_fun/ppermute | solution.py:253
  36.4 0.0 collective-permute-done.33.y_ref
  36.4 5.6 %collective-permute-start.38 = (bf16[32,1024]{1,0:T(8,128)(2,1)S(1)}, bf16[32,1024]{1,0:T(8,128)(2,1)S(1)}, u32[]{:S(2)}, u32[]{:S(2)}) collective-permute-start(bf16[32,1024]{1,0:T(8,128)(2,1)S(1)} %get-tuple-element.79), channel_id=1, source_target_pairs={{0,8},{9,17},{10,2},{12,20},{13,5},{15,7},{16,24},{18,26},{19,11},... | collective-permute-start | bytes 196616 | tf_op jit(solution)/shard_map/cond/branch_1_fun/ppermute | solution.py:253
  42.1 0.7 %collective-permute-start.37 = (bf16[32,1024]{1,0:T(8,128)(2,1)S(1)}, bf16[32,1024]{1,0:T(8,128)(2,1)S(1)}, u32[]{:S(2)}, u32[]{:S(2)}) collective-permute-start(bf16[32,1024]{1,0:T(8,128)(2,1)S(1)} %get-tuple-element.79), channel_id=1, source_target_pairs={{1,2},{4,5},{6,7},{9,8},{10,11},{13,14},{18,17},{21,20},{22,23},{2... | collective-permute-start | bytes 196616 | tf_op jit(solution)/shard_map/cond/branch_1_fun/ppermute | solution.py:253
  42.8 0.7 %collective-permute-start.36 = (bf16[32,1024]{1,0:T(8,128)(2,1)S(1)}, bf16[32,1024]{1,0:T(8,128)(2,1)S(1)}, u32[]{:S(2)}, u32[]{:S(2)}) collective-permute-start(bf16[32,1024]{1,0:T(8,128)(2,1)S(1)} %get-tuple-element.79), channel_id=1, source_target_pairs={{2,6},{6,2},{11,15},{13,9},{15,11},{16,20},{18,22},{20,16},{25,29}... | collective-permute-start | bytes 196616 | tf_op jit(solution)/shard_map/cond/branch_1_fun/ppermute | solution.py:253
  43.4 0.5 %collective-permute-done.38.x_ref = bf16[32,1024]{1,0:T(8,128)(2,1)S(1)} collective-permute-done((bf16[32,1024]{1,0:T(8,128)(2,1)S(1)}, bf16[32,1024]{1,0:T(8,128)(2,1)S(1)}, u32[]{:S(2)}, u32[]{:S(2)}) %collective-permute-start.38) | collective-permute-done | bytes 65568 | tf_op jit(solution)/shard_map/cond/branch_1_fun/ppermute | solution.py:253
  44.0 0.0 collective-permute-done.37.z_ref
  44.0 0.0 collective-permute-done.36.y_ref
  44.0 1.3 %collective-permute-start.41 = (bf16[16,1024]{1,0:T(8,128)(2,1)S(1)}, bf16[16,1024]{1,0:T(8,128)(2,1)S(1)}, u32[]{:S(2)}, u32[]{:S(2)}) collective-permute-start(bf16[16,1024]{1,0:T(8,128)(2,1)S(1)} %get-tuple-element.81), channel_id=1, source_target_pairs={{8,0},{11,3},{12,4},{15,7},{16,24},{19,27},{20,28},{23,31}} | collective-permute-start | bytes 98312 | tf_op jit(solution)/shard_map/cond/branch_1_fun/ppermute | solution.py:253
  45.3 1.3 %collective-permute-start.40 = (bf16[16,1024]{1,0:T(8,128)(2,1)S(1)}, bf16[16,1024]{1,0:T(8,128)(2,1)S(1)}, u32[]{:S(2)}, u32[]{:S(2)}) collective-permute-start(bf16[16,1024]{1,0:T(8,128)(2,1)S(1)} %get-tuple-element.81), channel_id=1, source_target_pairs={{1,0},{2,3},{5,4},{6,7},{25,24},{26,27},{29,28},{30,31}} | collective-permute-start | bytes 98312 | tf_op jit(solution)/shard_map/cond/branch_1_fun/ppermute | solution.py:253
  46.6 1.3 %collective-permute-start.39 = (bf16[16,1024]{1,0:T(8,128)(2,1)S(1)}, bf16[16,1024]{1,0:T(8,128)(2,1)S(1)}, u32[]{:S(2)}, u32[]{:S(2)}) collective-permute-start(bf16[16,1024]{1,0:T(8,128)(2,1)S(1)} %get-tuple-element.81), channel_id=1, source_target_pairs={{0,4},{7,3},{24,28},{31,27}} | collective-permute-start | bytes 98312 | tf_op jit(solution)/shard_map/cond/branch_1_fun/ppermute | solution.py:253
  47.9 3.7 %collective-permute-done.41.x_ref = bf16[16,1024]{1,0:T(8,128)(2,1)S(1)} collective-permute-done((bf16[16,1024]{1,0:T(8,128)(2,1)S(1)}, bf16[16,1024]{1,0:T(8,128)(2,1)S(1)}, u32[]{:S(2)}, u32[]{:S(2)}) %collective-permute-start.41) | collective-permute-done | bytes 32800 | tf_op jit(solution)/shard_map/cond/branch_1_fun/ppermute | solution.py:253
  51.6 0.0 collective-permute-done.40.z_ref
  51.6 0.0 collective-permute-done.39.y_ref
  51.7 0.0 copy-start
  51.7 0.6 %copy-done = bf16[1,1,1,2,16,1024]{5,4,3,2,1,0:T(8,128)(2,1)} copy-done((bf16[1,1,1,2,16,1024]{5,4,3,2,1,0:T(8,128)(2,1)}, bf16[1,1,1,2,16,1024]{5,4,3,2,1,0:T(8,128)(2,1)S(1)}, u32[]{:S(2)}) %copy-start) | copy-done | bytes 65560
  (5 shorter events, 0.1 us)
Async XLA Ops:
  1.6 4.9 %collective-permute-start.23 = (bf16[16,1024]{1,0:T(8,128)(2,1)S(1)}, bf16[16,1024]{1,0:T(8,128)(2,1)S(1)}, u32[]{:S(2)}, u32[]{:S(2)}) collective-permute-start(bf16[16,1024]{1,0:T(8,128)(2,1)S(1)} %get-tuple-element.67.after_ref), channel_id=1, source_target_pairs={{3,11},{7,15},{24,16},{28,20}} | collective-permute-start | bytes 98312 | tf_op jit(solution)/shard_map/cond/branch_1_fun/ppermute | solution.py:253
  2.3 4.2 %collective-permute-start.22 = (bf16[16,1024]{1,0:T(8,128)(2,1)S(1)}, bf16[16,1024]{1,0:T(8,128)(2,1)S(1)}, u32[]{:S(2)}, u32[]{:S(2)}) collective-permute-start(bf16[16,1024]{1,0:T(8,128)(2,1)S(1)} %get-tuple-element.67.after_ref), channel_id=1, source_target_pairs={{3,2},{6,5},{15,14},{16,17},{25,26},{28,29}} | collective-permute-start | bytes 98312 | tf_op jit(solution)/shard_map/cond/branch_1_fun/ppermute | solution.py:253
  3.0 3.6 %collective-permute-start.21 = (bf16[16,1024]{1,0:T(8,128)(2,1)S(1)}, bf16[16,1024]{1,0:T(8,128)(2,1)S(1)}, u32[]{:S(2)}, u32[]{:S(2)}) collective-permute-start(bf16[16,1024]{1,0:T(8,128)(2,1)S(1)} %get-tuple-element.67.after_ref), channel_id=1, source_target_pairs={{3,7},{4,0},{27,31},{28,24}} | collective-permute-start | bytes 98312 | tf_op jit(solution)/shard_map/cond/branch_1_fun/ppermute | solution.py:253
  6.6 6.2 %collective-permute-start.26 = (bf16[32,1024]{1,0:T(8,128)(2,1)S(1)}, bf16[32,1024]{1,0:T(8,128)(2,1)S(1)}, u32[]{:S(2)}, u32[]{:S(2)}) collective-permute-start(bf16[32,1024]{1,0:T(8,128)(2,1)S(1)} %get-tuple-element.71), channel_id=1, source_target_pairs={{2,10},{5,13},{7,15},{8,0},{11,19},{14,22},{17,9},{20,12},{23,31},... | collective-permute-start | bytes 196616 | tf_op jit(solution)/shard_map/cond/branch_1_fun/ppermute | solution.py:253
  7.9 4.9 %collective-permute-start.25 = (bf16[32,1024]{1,0:T(8,128)(2,1)S(1)}, bf16[32,1024]{1,0:T(8,128)(2,1)S(1)}, u32[]{:S(2)}, u32[]{:S(2)}) collective-permute-start(bf16[32,1024]{1,0:T(8,128)(2,1)S(1)} %get-tuple-element.71), channel_id=1, source_target_pairs={{2,1},{7,6},{11,10},{20,21},{24,25},{29,30}} | collective-permute-start | bytes 196616 | tf_op jit(solution)/shard_map/cond/branch_1_fun/ppermute | solution.py:253
  8.6 4.2 %collective-permute-start.24 = (bf16[32,1024]{1,0:T(8,128)(2,1)S(1)}, bf16[32,1024]{1,0:T(8,128)(2,1)S(1)}, u32[]{:S(2)}, u32[]{:S(2)}) collective-permute-start(bf16[32,1024]{1,0:T(8,128)(2,1)S(1)} %get-tuple-element.71), channel_id=1, source_target_pairs={{2,6},{6,2},{11,15},{13,9},{15,11},{16,20},{18,22},{20,16},{25,29}... | collective-permute-start | bytes 196616 | tf_op jit(solution)/shard_map/cond/branch_1_fun/ppermute | solution.py:253
  12.8 2.6 %collective-permute-start.29 = (bf16[32,1024]{1,0:T(8,128)(2,1)S(1)}, bf16[32,1024]{1,0:T(8,128)(2,1)S(1)}, u32[]{:S(2)}, u32[]{:S(2)}) collective-permute-start(bf16[32,1024]{1,0:T(8,128)(2,1)S(1)} %get-tuple-element.73), channel_id=1, source_target_pairs={{1,9},{3,11},{6,14},{10,18},{12,4},{15,23},{16,8},{19,27},{21,13},... | collective-permute-start | bytes 196616 | tf_op jit(solution)/shard_map/cond/branch_1_fun/ppermute | solution.py:253
  13.5 11.5 %collective-permute-start.28 = (bf16[32,1024]{1,0:T(8,128)(2,1)S(1)}, bf16[32,1024]{1,0:T(8,128)(2,1)S(1)}, u32[]{:S(2)}, u32[]{:S(2)}) collective-permute-start(bf16[32,1024]{1,0:T(8,128)(2,1)S(1)} %get-tuple-element.73), channel_id=1, source_target_pairs={{1,0},{6,5},{10,9},{12,13},{15,14},{16,17},{19,18},{21,22},{25,26}... | collective-permute-start | bytes 196616 | tf_op jit(solution)/shard_map/cond/branch_1_fun/ppermute | solution.py:253
  14.8 10.2 %collective-permute-start.27 = (bf16[32,1024]{1,0:T(8,128)(2,1)S(1)}, bf16[32,1024]{1,0:T(8,128)(2,1)S(1)}, u32[]{:S(2)}, u32[]{:S(2)}) collective-permute-start(bf16[32,1024]{1,0:T(8,128)(2,1)S(1)} %get-tuple-element.73), channel_id=1, source_target_pairs={{1,5},{8,12},{10,14},{12,8},{19,23},{21,17},{23,19},{30,26}} | collective-permute-start | bytes 196616 | tf_op jit(solution)/shard_map/cond/branch_1_fun/ppermute | solution.py:253
  25.4 6.2 %collective-permute-start.32 = (bf16[32,1024]{1,0:T(8,128)(2,1)S(1)}, bf16[32,1024]{1,0:T(8,128)(2,1)S(1)}, u32[]{:S(2)}, u32[]{:S(2)}) collective-permute-start(bf16[32,1024]{1,0:T(8,128)(2,1)S(1)} %get-tuple-element.75), channel_id=1, source_target_pairs={{0,8},{2,10},{5,13},{7,15},{8,0},{9,17},{10,2},{13,5},{14,22},{15,... | collective-permute-start | bytes 196616 | tf_op jit(solution)/shard_map/cond/branch_1_fun/ppermute | solution.py:253
  27.4 4.2 %collective-permute-start.31 = (bf16[32,1024]{1,0:T(8,128)(2,1)S(1)}, bf16[32,1024]{1,0:T(8,128)(2,1)S(1)}, u32[]{:S(2)}, u32[]{:S(2)}) collective-permute-start(bf16[32,1024]{1,0:T(8,128)(2,1)S(1)} %get-tuple-element.75), channel_id=1, source_target_pairs={{4,5},{5,4},{6,7},{7,6},{8,9},{9,8},{10,11},{11,10},{13,14},{14,13... | collective-permute-start | bytes 196616 | tf_op jit(solution)/shard_map/cond/branch_1_fun/ppermute | solution.py:253
  28.0 4.1 %collective-permute-start.30 = (bf16[32,1024]{1,0:T(8,128)(2,1)S(1)}, bf16[32,1024]{1,0:T(8,128)(2,1)S(1)}, u32[]{:S(2)}, u32[]{:S(2)}) collective-permute-start(bf16[32,1024]{1,0:T(8,128)(2,1)S(1)} %get-tuple-element.75), channel_id=1, source_target_pairs={{0,4},{4,0},{9,13},{13,9},{18,22},{22,18},{27,31},{31,27}} | collective-permute-start | bytes 196616 | tf_op jit(solution)/shard_map/cond/branch_1_fun/ppermute | solution.py:253
  32.6 2.7 %collective-permute-start.35 = (bf16[32,1024]{1,0:T(8,128)(2,1)S(1)}, bf16[32,1024]{1,0:T(8,128)(2,1)S(1)}, u32[]{:S(2)}, u32[]{:S(2)}) collective-permute-start(bf16[32,1024]{1,0:T(8,128)(2,1)S(1)} %get-tuple-element.77), channel_id=1, source_target_pairs={{4,12},{8,16},{9,1},{11,3},{13,21},{14,6},{17,25},{18,10},{20,28},... | collective-permute-start | bytes 196616 | tf_op jit(solution)/shard_map/cond/branch_1_fun/ppermute | solution.py:253
  33.2 3.2 %collective-permute-start.34 = (bf16[32,1024]{1,0:T(8,128)(2,1)S(1)}, bf16[32,1024]{1,0:T(8,128)(2,1)S(1)}, u32[]{:S(2)}, u32[]{:S(2)}) collective-permute-start(bf16[32,1024]{1,0:T(8,128)(2,1)S(1)} %get-tuple-element.77), channel_id=1, source_target_pairs={{0,1},{2,3},{5,6},{9,10},{13,12},{14,15},{17,16},{18,19},{22,21},{... | collective-permute-start | bytes 196616 | tf_op jit(solution)/shard_map/cond/branch_1_fun/ppermute | solution.py:253
  34.5 1.9 %collective-permute-start.33 = (bf16[32,1024]{1,0:T(8,128)(2,1)S(1)}, bf16[32,1024]{1,0:T(8,128)(2,1)S(1)}, u32[]{:S(2)}, u32[]{:S(2)}) collective-permute-start(bf16[32,1024]{1,0:T(8,128)(2,1)S(1)} %get-tuple-element.77), channel_id=1, source_target_pairs={{5,1},{8,12},{14,10},{17,21},{23,19},{26,30}} | collective-permute-start | bytes 196616 | tf_op jit(solution)/shard_map/cond/branch_1_fun/ppermute | solution.py:253
  36.4 7.5 %collective-permute-start.38 = (bf16[32,1024]{1,0:T(8,128)(2,1)S(1)}, bf16[32,1024]{1,0:T(8,128)(2,1)S(1)}, u32[]{:S(2)}, u32[]{:S(2)}) collective-permute-start(bf16[32,1024]{1,0:T(8,128)(2,1)S(1)} %get-tuple-element.79), channel_id=1, source_target_pairs={{0,8},{9,17},{10,2},{12,20},{13,5},{15,7},{16,24},{18,26},{19,11},... | collective-permute-start | bytes 196616 | tf_op jit(solution)/shard_map/cond/branch_1_fun/ppermute | solution.py:253
  42.1 1.9 %collective-permute-start.37 = (bf16[32,1024]{1,0:T(8,128)(2,1)S(1)}, bf16[32,1024]{1,0:T(8,128)(2,1)S(1)}, u32[]{:S(2)}, u32[]{:S(2)}) collective-permute-start(bf16[32,1024]{1,0:T(8,128)(2,1)S(1)} %get-tuple-element.79), channel_id=1, source_target_pairs={{1,2},{4,5},{6,7},{9,8},{10,11},{13,14},{18,17},{21,20},{22,23},{2... | collective-permute-start | bytes 196616 | tf_op jit(solution)/shard_map/cond/branch_1_fun/ppermute | solution.py:253
  42.8 1.2 %collective-permute-start.36 = (bf16[32,1024]{1,0:T(8,128)(2,1)S(1)}, bf16[32,1024]{1,0:T(8,128)(2,1)S(1)}, u32[]{:S(2)}, u32[]{:S(2)}) collective-permute-start(bf16[32,1024]{1,0:T(8,128)(2,1)S(1)} %get-tuple-element.79), channel_id=1, source_target_pairs={{2,6},{6,2},{11,15},{13,9},{15,11},{16,20},{18,22},{20,16},{25,29}... | collective-permute-start | bytes 196616 | tf_op jit(solution)/shard_map/cond/branch_1_fun/ppermute | solution.py:253
  44.0 7.6 %collective-permute-start.41 = (bf16[16,1024]{1,0:T(8,128)(2,1)S(1)}, bf16[16,1024]{1,0:T(8,128)(2,1)S(1)}, u32[]{:S(2)}, u32[]{:S(2)}) collective-permute-start(bf16[16,1024]{1,0:T(8,128)(2,1)S(1)} %get-tuple-element.81), channel_id=1, source_target_pairs={{8,0},{11,3},{12,4},{15,7},{16,24},{19,27},{20,28},{23,31}} | collective-permute-start | bytes 98312 | tf_op jit(solution)/shard_map/cond/branch_1_fun/ppermute | solution.py:253
  45.3 6.3 %collective-permute-start.40 = (bf16[16,1024]{1,0:T(8,128)(2,1)S(1)}, bf16[16,1024]{1,0:T(8,128)(2,1)S(1)}, u32[]{:S(2)}, u32[]{:S(2)}) collective-permute-start(bf16[16,1024]{1,0:T(8,128)(2,1)S(1)} %get-tuple-element.81), channel_id=1, source_target_pairs={{1,0},{2,3},{5,4},{6,7},{25,24},{26,27},{29,28},{30,31}} | collective-permute-start | bytes 98312 | tf_op jit(solution)/shard_map/cond/branch_1_fun/ppermute | solution.py:253
  46.6 5.0 %collective-permute-start.39 = (bf16[16,1024]{1,0:T(8,128)(2,1)S(1)}, bf16[16,1024]{1,0:T(8,128)(2,1)S(1)}, u32[]{:S(2)}, u32[]{:S(2)}) collective-permute-start(bf16[16,1024]{1,0:T(8,128)(2,1)S(1)} %get-tuple-element.81), channel_id=1, source_target_pairs={{0,4},{7,3},{24,28},{31,27}} | collective-permute-start | bytes 98312 | tf_op jit(solution)/shard_map/cond/branch_1_fun/ppermute | solution.py:253
  51.7 0.6 %copy-start = (bf16[1,1,1,2,16,1024]{5,4,3,2,1,0:T(8,128)(2,1)}, bf16[1,1,1,2,16,1024]{5,4,3,2,1,0:T(8,128)(2,1)S(1)}, u32[]{:S(2)}) copy-start(bf16[1,1,1,2,16,1024]{5,4,3,2,1,0:T(8,128)(2,1)S(1)} %get-tuple-element.308) | copy-start | bytes 196612

commit v2 on v1

--- a/solution.py
+++ b/solution.py
@@ -57,22 +57,22 @@
 
 SHARED = (
     (
-        (0, 1, 2, 3, 4, 5, 6),
-        (7, 8, 9, 3, 10, 11, 6),
-        (7, 9, 8, 12, 11, 10, 6),
-        (0, 2, 1, 12, 5, 4, 6),
+        (0, 1, 2, -1, 3, 4, 3),
+        (0, 5, 6, -2, 7, 8, 9),
+        (9, 6, 5, -3, 8, 7, 8),
+        (1, 2, 10, -4, 4, 3, 4),
     ),
     (
-        (0, 1, 2, 3, 1, 4, 5),
-        (0, 2, 4, 6, 7, 2, 5),
-        (5, 2, 8, 9, 4, 2, 3),
-        (5, 4, 1, 3, 2, 1, 0),
+        (0, 1, 2, 3, 0, 4, 5),
+        (6, 7, 8, 9, 6, 5, 4),
+        (7, 5, 6, 10, 11, 7, 1),
+        (2, 4, 0, 12, 2, 1, 4),
     ),
     (
-        (0, 1, 2, 3, 4, 5, 6),
-        (7, 8, 9, 10, 11, 12, 6),
-        (8, 7, 13, 3, 12, 11, 6),
-        (1, 0, 14, 10, 5, 4, 6),
+        (0, 1, 2, -1, 3, 4, 5),
+        (6, 7, 8, -2, 9, 10, 9),
+        (5, 6, 7, -3, 10, 9, 10),
+        (5, 0, 1, -4, 4, 3, 4),
     ),
 )
 
@@ -81,18 +81,32 @@
     return (kind & 1, 1, kind >> 1)
 
 
+def swaps_of(sizes, axis, edges):
+    twins = dict(edges)
+    twins.update((target, source) for source, target in edges)
+    for place in places(sizes):
+        if place not in twins:
+            line = [place[:axis] + (i,) + place[axis + 1 :] for i in range(sizes[axis])]
+            left = [other for other in line if other not in twins and other != place]
+            if left:
+                twins[place], twins[left[0]] = left[0], place
+    return set(twins.items())
+
+
 def pairs_of(sizes, bits, axis, hop):
     deepest = sum(size - 1 for size in sizes)
-    own = hop_edges(sizes, bits, axis, hop)
+    own = set(hop_edges(sizes, bits, axis, hop))
     number_of = SHARED[axis][bits[0] + 2 * bits[2]][hop - 1]
     edges = set(own)
     for kind, row in enumerate(SHARED[axis]):
         for other, found in enumerate(row, 1):
             if found == number_of and other <= deepest:
                 edges.update(hop_edges(sizes, kind_bits(kind), axis, other))
+    if number_of < 0:
+        edges = swaps_of(sizes, axis, edges)
     if clash(sorted(edges)):
-        edges = set(own)
-    assert not clash(sorted(edges))
+        edges = own
+    assert not clash(sorted(edges)) and own <= edges
     return sorted((number(sizes, source), number(sizes, target)) for source, target in edges)
 
 

time: 52.7 us -> 49.7 us (0.943)
  the two profiles are of different devices: /device:TPU:0 before, /device:TPU:2 now
where the time goes in v2:
time: 49.7 us; the launch traced here: 49.1 us
  starting transfers between devices  26.2 us (53%)
  waiting for transfers between devices  17.1 us (34%)
  Pallas kernels  4.22 us (8%)
  between operations  0.68 us (1%)
  local copies, waits for them, and re-layouts  0.62 us (1%)
    ppermute x21, starting transfers between devices, wave(): came[axis] = lax.ppermute(message, AXES, pairs_of(sizes, bits, axis, hop))  26.2 us
    ppermute x21, waiting for transfers between devices, wave(): came[axis] = lax.ppermute(message, AXES, pairs_of(sizes, bits, axis, hop))  17.1 us
    pallas_call x1, Pallas kernels, load(): pl.pallas_call(load_kernel, out_shape=pltpu.VMEM(maps.shape, maps.dtype),...  2.24 us
    pallas_call x7, Pallas kernels, take_hop(): pl.pallas_call(functools.partial(hop_kernel, hop, sizes, bits), out_shape...  1.02 us
  transfers between devices with their start and end apart: 21, of which 9 were waited for; matrix products, arithmetic and copies ran while one was open for 0% of the time, Pallas kernels for 5%

profile of v2, /device:TPU:2, one launch (start us, length us, event | category | flops | bytes accessed | tf_op | source)
XLA Modules:
  0.0 49.1 jit_solution(18228212217495634010)
XLA Ops:
  0.7 47.8 %conditional.1 = (bf16[1,1,1,2,16,1024]{5,4,3,2,1,0:T(8,128)(2,1)S(1)}) conditional(s32[]{:T(128)} %clamp.3, (s32[]{:T(128)}, f32[1,1,1,2,16,1024]{5,4,3,2,1,0:T(8,128)}, bf16[1,1,1,2,1024,1024]{5,4,3,2,1,0:T(8,128)(2,1)}) %tuple.21, (s32[]{:T(128)}, f32[1,1,1,2,16,1024]{5,4,3,2,1,0:T(8,128)}, ...), branch_computations={%region_0.1_spmd, %region_1.2_spmd, %region_2.3_spmd, %region_3.4_... | conditional | bytes 4719440 | solution.py:313
  0.7 1.0 %begin.6 = (bf16[16,1024]{1,0:T(8,128)(2,1)S(1)}, bf16[2,16,1024]{2,1,0:T(8,128)(2,1)S(1)}, f32[2,16,1024]{2,1,0:T(8,128)S(1)}) custom-call(s32[1]{0:T(128)} %bitcast.8.lead_hbm.lead_ref, f32[2,16,1024]{2,1,0:T(8,128)} %bitcast.26), custom_call_target="tpu_custom_call" | custom-call | tf_op jit(solution)/shard_map/cond/branch_2_fun/begin/pallas_call | solution.py:142
  1.6 0.7 %collective-permute-start.44 = (bf16[16,1024]{1,0:T(8,128)(2,1)S(1)}, bf16[16,1024]{1,0:T(8,128)(2,1)S(1)}, u32[]{:S(2)}, u32[]{:S(2)}) collective-permute-start(bf16[16,1024]{1,0:T(8,128)(2,1)S(1)} %get-tuple-element.85.after_ref), channel_id=1, source_target_pairs={{7,15},{11,3},{20,28},{24,16}} | collective-permute-start | bytes 98312 | tf_op jit(solution)/shard_map/cond/branch_2_fun/ppermute | solution.py:267
  2.3 0.7 %collective-permute-start.43 = (bf16[16,1024]{1,0:T(8,128)(2,1)S(1)}, bf16[16,1024]{1,0:T(8,128)(2,1)S(1)}, u32[]{:S(2)}, u32[]{:S(2)}) collective-permute-start(bf16[16,1024]{1,0:T(8,128)(2,1)S(1)} %get-tuple-element.85.after_ref), channel_id=1, source_target_pairs={{0,1},{5,4},{7,6},{24,25},{26,27},{31,30}} | collective-permute-start | bytes 98312 | tf_op jit(solution)/shard_map/cond/branch_2_fun/ppermute | solution.py:267
  3.0 0.7 %collective-permute-start.42 = (bf16[16,1024]{1,0:T(8,128)(2,1)S(1)}, bf16[16,1024]{1,0:T(8,128)(2,1)S(1)}, u32[]{:S(2)}, u32[]{:S(2)}) collective-permute-start(bf16[16,1024]{1,0:T(8,128)(2,1)S(1)} %get-tuple-element.85.after_ref), channel_id=1, source_target_pairs={{2,6},{7,3},{11,15},{20,16},{24,28},{29,25}} | collective-permute-start | bytes 98312 | tf_op jit(solution)/shard_map/cond/branch_2_fun/ppermute | solution.py:267
  3.7 2.2 %load.6.maps_ref = bf16[2,1024,1024]{2,1,0:T(8,128)(2,1)S(1)} custom-call(s32[1]{0:T(128)} %bitcast.8.lead_hbm.lead_ref, bf16[2,1024,1024]{2,1,0:T(8,128)(2,1)} %bitcast.22, bf16[16,1024]{1,0:T(8,128)(2,1)S(1)} %get-tuple-element.85.after_ref), custom_call_target="tpu_custom_call" | custom-call | tf_op jit(solution)/shard_map/cond/branch_2_fun/load/pallas_call | solution.py:177
  5.9 0.0 collective-permute-done.44.x_ref
  5.9 0.0 collective-permute-done.43.z_ref
  5.9 0.0 collective-permute-done.42.y_ref
  6.0 1.3 %collective-permute-start.47 = (bf16[32,1024]{1,0:T(8,128)(2,1)S(1)}, bf16[32,1024]{1,0:T(8,128)(2,1)S(1)}, u32[]{:S(2)}, u32[]{:S(2)}) collective-permute-start(bf16[32,1024]{1,0:T(8,128)(2,1)S(1)} %get-tuple-element.89), channel_id=1, source_target_pairs={{1,9},{3,11},{6,14},{10,18},{12,4},{15,23},{16,8},{19,27},{21,13},... | collective-permute-start | bytes 196616 | tf_op jit(solution)/shard_map/cond/branch_2_fun/ppermute | solution.py:267
  7.3 0.7 %collective-permute-start.46 = (bf16[32,1024]{1,0:T(8,128)(2,1)S(1)}, bf16[32,1024]{1,0:T(8,128)(2,1)S(1)}, u32[]{:S(2)}, u32[]{:S(2)}) collective-permute-start(bf16[32,1024]{1,0:T(8,128)(2,1)S(1)} %get-tuple-element.89), channel_id=1, source_target_pairs={{3,2},{6,5},{15,14},{16,17},{25,26},{28,29}} | collective-permute-start | bytes 196616 | tf_op jit(solution)/shard_map/cond/branch_2_fun/ppermute | solution.py:267
  7.9 0.7 %collective-permute-start.45 = (bf16[32,1024]{1,0:T(8,128)(2,1)S(1)}, bf16[32,1024]{1,0:T(8,128)(2,1)S(1)}, u32[]{:S(2)}, u32[]{:S(2)}) collective-permute-start(bf16[32,1024]{1,0:T(8,128)(2,1)S(1)} %get-tuple-element.89), channel_id=1, source_target_pairs={{0,4},{6,2},{15,11},{16,20},{25,29},{31,27}} | collective-permute-start | bytes 196616 | tf_op jit(solution)/shard_map/cond/branch_2_fun/ppermute | solution.py:267
  8.6 4.4 %collective-permute-done.47.x_ref = bf16[32,1024]{1,0:T(8,128)(2,1)S(1)} collective-permute-done((bf16[32,1024]{1,0:T(8,128)(2,1)S(1)}, bf16[32,1024]{1,0:T(8,128)(2,1)S(1)}, u32[]{:S(2)}, u32[]{:S(2)}) %collective-permute-start.47) | collective-permute-done | bytes 65568 | tf_op jit(solution)/shard_map/cond/branch_2_fun/ppermute | solution.py:267
  13.0 0.0 collective-permute-done.46.z_ref
  13.0 0.0 collective-permute-done.45.y_ref
  13.0 0.5 hop2.6
  13.5 1.3 %collective-permute-start.50 = (bf16[32,1024]{1,0:T(8,128)(2,1)S(1)}, bf16[32,1024]{1,0:T(8,128)(2,1)S(1)}, u32[]{:S(2)}, u32[]{:S(2)}) collective-permute-start(bf16[32,1024]{1,0:T(8,128)(2,1)S(1)} %get-tuple-element.91), channel_id=1, source_target_pairs={{2,10},{5,13},{7,15},{8,0},{11,19},{14,22},{17,9},{20,12},{23,31},... | collective-permute-start | bytes 196616 | tf_op jit(solution)/shard_map/cond/branch_2_fun/ppermute | solution.py:267
  14.8 2.2 %collective-permute-start.49 = (bf16[32,1024]{1,0:T(8,128)(2,1)S(1)}, bf16[32,1024]{1,0:T(8,128)(2,1)S(1)}, u32[]{:S(2)}, u32[]{:S(2)}) collective-permute-start(bf16[32,1024]{1,0:T(8,128)(2,1)S(1)} %get-tuple-element.91), channel_id=1, source_target_pairs={{2,1},{5,4},{7,6},{8,9},{11,10},{14,13},{17,18},{20,21},{23,22},{2... | collective-permute-start | bytes 196616 | tf_op jit(solution)/shard_map/cond/branch_2_fun/ppermute | solution.py:267
  17.0 1.3 %collective-permute-start.48 = (bf16[32,1024]{1,0:T(8,128)(2,1)S(1)}, bf16[32,1024]{1,0:T(8,128)(2,1)S(1)}, u32[]{:S(2)}, u32[]{:S(2)}) collective-permute-start(bf16[32,1024]{1,0:T(8,128)(2,1)S(1)} %get-tuple-element.91), channel_id=1, source_target_pairs={{3,7},{5,1},{8,12},{14,10},{17,21},{23,19},{26,30},{28,24}} | collective-permute-start | bytes 196616 | tf_op jit(solution)/shard_map/cond/branch_2_fun/ppermute | solution.py:267
  18.3 0.0 collective-permute-done.50.x_ref
  18.3 0.6 %collective-permute-done.49.z_ref = bf16[32,1024]{1,0:T(8,128)(2,1)S(1)} collective-permute-done((bf16[32,1024]{1,0:T(8,128)(2,1)S(1)}, bf16[32,1024]{1,0:T(8,128)(2,1)S(1)}, u32[]{:S(2)}, u32[]{:S(2)}) %collective-permute-start.49) | collective-permute-done | bytes 65568 | tf_op jit(solution)/shard_map/cond/branch_2_fun/ppermute | solution.py:267
  18.9 0.3 collective-permute-done.48.y_ref
  19.2 0.3 collective-permute-start.53
  19.6 5.5 %collective-permute-start.52 = (bf16[32,1024]{1,0:T(8,128)(2,1)S(1)}, bf16[32,1024]{1,0:T(8,128)(2,1)S(1)}, u32[]{:S(2)}, u32[]{:S(2)}) collective-permute-start(bf16[32,1024]{1,0:T(8,128)(2,1)S(1)} %get-tuple-element.93), channel_id=1, source_target_pairs={{0,1},{1,0},{2,3},{3,2},{4,5},{5,4},{6,7},{7,6},{8,11},{9,10},{10,... | collective-permute-start | bytes 196616 | tf_op jit(solution)/shard_map/cond/branch_2_fun/ppermute | solution.py:267
  25.0 0.7 %collective-permute-start.51 = (bf16[32,1024]{1,0:T(8,128)(2,1)S(1)}, bf16[32,1024]{1,0:T(8,128)(2,1)S(1)}, u32[]{:S(2)}, u32[]{:S(2)}) collective-permute-start(bf16[32,1024]{1,0:T(8,128)(2,1)S(1)} %get-tuple-element.93), channel_id=1, source_target_pairs={{0,4},{4,0},{9,13},{13,9},{18,22},{22,18},{27,31},{31,27}} | collective-permute-start | bytes 196616 | tf_op jit(solution)/shard_map/cond/branch_2_fun/ppermute | solution.py:267
  25.7 0.0 collective-permute-done.53.x_ref
  25.7 1.7 %collective-permute-done.52.z_ref = bf16[32,1024]{1,0:T(8,128)(2,1)S(1)} collective-permute-done((bf16[32,1024]{1,0:T(8,128)(2,1)S(1)}, bf16[32,1024]{1,0:T(8,128)(2,1)S(1)}, u32[]{:S(2)}, u32[]{:S(2)}) %collective-permute-start.52) | collective-permute-done | bytes 65568 | tf_op jit(solution)/shard_map/cond/branch_2_fun/ppermute | solution.py:267
  27.4 0.0 collective-permute-done.51.y_ref
  27.4 1.3 %collective-permute-start.56 = (bf16[32,1024]{1,0:T(8,128)(2,1)S(1)}, bf16[32,1024]{1,0:T(8,128)(2,1)S(1)}, u32[]{:S(2)}, u32[]{:S(2)}) collective-permute-start(bf16[32,1024]{1,0:T(8,128)(2,1)S(1)} %get-tuple-element.95), channel_id=1, source_target_pairs={{0,8},{9,17},{10,2},{12,20},{13,5},{15,7},{16,24},{18,26},{19,11},... | collective-permute-start | bytes 196616 | tf_op jit(solution)/shard_map/cond/branch_2_fun/ppermute | solution.py:267
  28.7 1.3 %collective-permute-start.55 = (bf16[32,1024]{1,0:T(8,128)(2,1)S(1)}, bf16[32,1024]{1,0:T(8,128)(2,1)S(1)}, u32[]{:S(2)}, u32[]{:S(2)}) collective-permute-start(bf16[32,1024]{1,0:T(8,128)(2,1)S(1)} %get-tuple-element.95), channel_id=1, source_target_pairs={{1,2},{4,5},{6,7},{9,8},{10,11},{13,14},{18,17},{21,20},{22,23},{2... | collective-permute-start | bytes 196616 | tf_op jit(solution)/shard_map/cond/branch_2_fun/ppermute | solution.py:267
  30.0 1.3 %collective-permute-start.54 = (bf16[32,1024]{1,0:T(8,128)(2,1)S(1)}, bf16[32,1024]{1,0:T(8,128)(2,1)S(1)}, u32[]{:S(2)}, u32[]{:S(2)}) collective-permute-start(bf16[32,1024]{1,0:T(8,128)(2,1)S(1)} %get-tuple-element.95), channel_id=1, source_target_pairs={{1,5},{10,14},{12,8},{19,23},{21,17},{30,26}} | collective-permute-start | bytes 196616 | tf_op jit(solution)/shard_map/cond/branch_2_fun/ppermute | solution.py:267
  31.3 2.3 %collective-permute-done.56.x_ref = bf16[32,1024]{1,0:T(8,128)(2,1)S(1)} collective-permute-done((bf16[32,1024]{1,0:T(8,128)(2,1)S(1)}, bf16[32,1024]{1,0:T(8,128)(2,1)S(1)}, u32[]{:S(2)}, u32[]{:S(2)}) %collective-permute-start.56) | collective-permute-done | bytes 65568 | tf_op jit(solution)/shard_map/cond/branch_2_fun/ppermute | solution.py:267
  33.6 2.8 %collective-permute-done.55.z_ref = bf16[32,1024]{1,0:T(8,128)(2,1)S(1)} collective-permute-done((bf16[32,1024]{1,0:T(8,128)(2,1)S(1)}, bf16[32,1024]{1,0:T(8,128)(2,1)S(1)}, u32[]{:S(2)}, u32[]{:S(2)}) %collective-permute-start.55) | collective-permute-done | bytes 65568 | tf_op jit(solution)/shard_map/cond/branch_2_fun/ppermute | solution.py:267
  36.3 0.0 collective-permute-done.54.y_ref
  36.3 0.5 hop5.6
  36.8 1.3 %collective-permute-start.59 = (bf16[32,1024]{1,0:T(8,128)(2,1)S(1)}, bf16[32,1024]{1,0:T(8,128)(2,1)S(1)}, u32[]{:S(2)}, u32[]{:S(2)}) collective-permute-start(bf16[32,1024]{1,0:T(8,128)(2,1)S(1)} %get-tuple-element.97), channel_id=1, source_target_pairs={{4,12},{8,16},{9,1},{11,3},{13,21},{14,6},{17,25},{18,10},{20,28},... | collective-permute-start | bytes 196616 | tf_op jit(solution)/shard_map/cond/branch_2_fun/ppermute | solution.py:267
  38.1 0.7 %collective-permute-start.58 = (bf16[32,1024]{1,0:T(8,128)(2,1)S(1)}, bf16[32,1024]{1,0:T(8,128)(2,1)S(1)}, u32[]{:S(2)}, u32[]{:S(2)}) collective-permute-start(bf16[32,1024]{1,0:T(8,128)(2,1)S(1)} %get-tuple-element.97), channel_id=1, source_target_pairs={{0,1},{2,3},{5,6},{9,10},{13,12},{14,15},{17,16},{18,19},{22,21},{... | collective-permute-start | bytes 196616 | tf_op jit(solution)/shard_map/cond/branch_2_fun/ppermute | solution.py:267
  38.8 0.7 %collective-permute-start.57 = (bf16[32,1024]{1,0:T(8,128)(2,1)S(1)}, bf16[32,1024]{1,0:T(8,128)(2,1)S(1)}, u32[]{:S(2)}, u32[]{:S(2)}) collective-permute-start(bf16[32,1024]{1,0:T(8,128)(2,1)S(1)} %get-tuple-element.97), channel_id=1, source_target_pairs={{2,6},{7,3},{11,15},{20,16},{24,28},{29,25}} | collective-permute-start | bytes 196616 | tf_op jit(solution)/shard_map/cond/branch_2_fun/ppermute | solution.py:267
  39.5 0.5 %collective-permute-done.59.x_ref = bf16[32,1024]{1,0:T(8,128)(2,1)S(1)} collective-permute-done((bf16[32,1024]{1,0:T(8,128)(2,1)S(1)}, bf16[32,1024]{1,0:T(8,128)(2,1)S(1)}, u32[]{:S(2)}, u32[]{:S(2)}) %collective-permute-start.59) | collective-permute-done | bytes 65568 | tf_op jit(solution)/shard_map/cond/branch_2_fun/ppermute | solution.py:267
  40.0 0.0 collective-permute-done.58.z_ref
  40.0 0.0 collective-permute-done.57.y_ref
  40.0 1.3 %collective-permute-start.62 = (bf16[16,1024]{1,0:T(8,128)(2,1)S(1)}, bf16[16,1024]{1,0:T(8,128)(2,1)S(1)}, u32[]{:S(2)}, u32[]{:S(2)}) collective-permute-start(bf16[16,1024]{1,0:T(8,128)(2,1)S(1)} %get-tuple-element.99), channel_id=1, source_target_pairs={{0,8},{9,17},{10,2},{12,20},{13,5},{15,7},{16,24},{18,26},{19,11},... | collective-permute-start | bytes 98312 | tf_op jit(solution)/shard_map/cond/branch_2_fun/ppermute | solution.py:267
  41.3 1.3 %collective-permute-start.61 = (bf16[16,1024]{1,0:T(8,128)(2,1)S(1)}, bf16[16,1024]{1,0:T(8,128)(2,1)S(1)}, u32[]{:S(2)}, u32[]{:S(2)}) collective-permute-start(bf16[16,1024]{1,0:T(8,128)(2,1)S(1)} %get-tuple-element.99), channel_id=1, source_target_pairs={{1,2},{4,5},{6,7},{9,8},{10,11},{13,14},{18,17},{21,20},{22,23},{2... | collective-permute-start | bytes 98312 | tf_op jit(solution)/shard_map/cond/branch_2_fun/ppermute | solution.py:267
  42.6 1.3 %collective-permute-start.60 = (bf16[16,1024]{1,0:T(8,128)(2,1)S(1)}, bf16[16,1024]{1,0:T(8,128)(2,1)S(1)}, u32[]{:S(2)}, u32[]{:S(2)}) collective-permute-start(bf16[16,1024]{1,0:T(8,128)(2,1)S(1)} %get-tuple-element.99), channel_id=1, source_target_pairs={{3,7},{5,1},{12,8},{19,23},{26,30},{28,24}} | collective-permute-start | bytes 98312 | tf_op jit(solution)/shard_map/cond/branch_2_fun/ppermute | solution.py:267
  43.9 1.9 %collective-permute-done.62.x_ref = bf16[16,1024]{1,0:T(8,128)(2,1)S(1)} collective-permute-done((bf16[16,1024]{1,0:T(8,128)(2,1)S(1)}, bf16[16,1024]{1,0:T(8,128)(2,1)S(1)}, u32[]{:S(2)}, u32[]{:S(2)}) %collective-permute-start.62) | collective-permute-done | bytes 32800 | tf_op jit(solution)/shard_map/cond/branch_2_fun/ppermute | solution.py:267
  45.9 2.6 %collective-permute-done.61.z_ref = bf16[16,1024]{1,0:T(8,128)(2,1)S(1)} collective-permute-done((bf16[16,1024]{1,0:T(8,128)(2,1)S(1)}, bf16[16,1024]{1,0:T(8,128)(2,1)S(1)}, u32[]{:S(2)}, u32[]{:S(2)}) %collective-permute-start.61) | collective-permute-done | bytes 32800 | tf_op jit(solution)/shard_map/cond/branch_2_fun/ppermute | solution.py:267
  48.4 0.0 collective-permute-done.60.y_ref
  48.5 0.0 copy-start
  48.5 0.6 %copy-done = bf16[1,1,1,2,16,1024]{5,4,3,2,1,0:T(8,128)(2,1)} copy-done((bf16[1,1,1,2,16,1024]{5,4,3,2,1,0:T(8,128)(2,1)}, bf16[1,1,1,2,16,1024]{5,4,3,2,1,0:T(8,128)(2,1)S(1)}, u32[]{:S(2)}) %copy-start) | copy-done | bytes 65560
  (5 shorter events, 0.1 us)
Async XLA Ops:
  1.6 4.3 %collective-permute-start.44 = (bf16[16,1024]{1,0:T(8,128)(2,1)S(1)}, bf16[16,1024]{1,0:T(8,128)(2,1)S(1)}, u32[]{:S(2)}, u32[]{:S(2)}) collective-permute-start(bf16[16,1024]{1,0:T(8,128)(2,1)S(1)} %get-tuple-element.85.after_ref), channel_id=1, source_target_pairs={{7,15},{11,3},{20,28},{24,16}} | collective-permute-start | bytes 98312 | tf_op jit(solution)/shard_map/cond/branch_2_fun/ppermute | solution.py:267
  2.3 3.6 %collective-permute-start.43 = (bf16[16,1024]{1,0:T(8,128)(2,1)S(1)}, bf16[16,1024]{1,0:T(8,128)(2,1)S(1)}, u32[]{:S(2)}, u32[]{:S(2)}) collective-permute-start(bf16[16,1024]{1,0:T(8,128)(2,1)S(1)} %get-tuple-element.85.after_ref), channel_id=1, source_target_pairs={{0,1},{5,4},{7,6},{24,25},{26,27},{31,30}} | collective-permute-start | bytes 98312 | tf_op jit(solution)/shard_map/cond/branch_2_fun/ppermute | solution.py:267
  3.0 2.9 %collective-permute-start.42 = (bf16[16,1024]{1,0:T(8,128)(2,1)S(1)}, bf16[16,1024]{1,0:T(8,128)(2,1)S(1)}, u32[]{:S(2)}, u32[]{:S(2)}) collective-permute-start(bf16[16,1024]{1,0:T(8,128)(2,1)S(1)} %get-tuple-element.85.after_ref), channel_id=1, source_target_pairs={{2,6},{7,3},{11,15},{20,16},{24,28},{29,25}} | collective-permute-start | bytes 98312 | tf_op jit(solution)/shard_map/cond/branch_2_fun/ppermute | solution.py:267
  6.0 7.1 %collective-permute-start.47 = (bf16[32,1024]{1,0:T(8,128)(2,1)S(1)}, bf16[32,1024]{1,0:T(8,128)(2,1)S(1)}, u32[]{:S(2)}, u32[]{:S(2)}) collective-permute-start(bf16[32,1024]{1,0:T(8,128)(2,1)S(1)} %get-tuple-element.89), channel_id=1, source_target_pairs={{1,9},{3,11},{6,14},{10,18},{12,4},{15,23},{16,8},{19,27},{21,13},... | collective-permute-start | bytes 196616 | tf_op jit(solution)/shard_map/cond/branch_2_fun/ppermute | solution.py:267
  7.3 5.8 %collective-permute-start.46 = (bf16[32,1024]{1,0:T(8,128)(2,1)S(1)}, bf16[32,1024]{1,0:T(8,128)(2,1)S(1)}, u32[]{:S(2)}, u32[]{:S(2)}) collective-permute-start(bf16[32,1024]{1,0:T(8,128)(2,1)S(1)} %get-tuple-element.89), channel_id=1, source_target_pairs={{3,2},{6,5},{15,14},{16,17},{25,26},{28,29}} | collective-permute-start | bytes 196616 | tf_op jit(solution)/shard_map/cond/branch_2_fun/ppermute | solution.py:267
  7.9 5.1 %collective-permute-start.45 = (bf16[32,1024]{1,0:T(8,128)(2,1)S(1)}, bf16[32,1024]{1,0:T(8,128)(2,1)S(1)}, u32[]{:S(2)}, u32[]{:S(2)}) collective-permute-start(bf16[32,1024]{1,0:T(8,128)(2,1)S(1)} %get-tuple-element.89), channel_id=1, source_target_pairs={{0,4},{6,2},{15,11},{16,20},{25,29},{31,27}} | collective-permute-start | bytes 196616 | tf_op jit(solution)/shard_map/cond/branch_2_fun/ppermute | solution.py:267
  13.5 4.8 %collective-permute-start.50 = (bf16[32,1024]{1,0:T(8,128)(2,1)S(1)}, bf16[32,1024]{1,0:T(8,128)(2,1)S(1)}, u32[]{:S(2)}, u32[]{:S(2)}) collective-permute-start(bf16[32,1024]{1,0:T(8,128)(2,1)S(1)} %get-tuple-element.91), channel_id=1, source_target_pairs={{2,10},{5,13},{7,15},{8,0},{11,19},{14,22},{17,9},{20,12},{23,31},... | collective-permute-start | bytes 196616 | tf_op jit(solution)/shard_map/cond/branch_2_fun/ppermute | solution.py:267
  14.8 4.1 %collective-permute-start.49 = (bf16[32,1024]{1,0:T(8,128)(2,1)S(1)}, bf16[32,1024]{1,0:T(8,128)(2,1)S(1)}, u32[]{:S(2)}, u32[]{:S(2)}) collective-permute-start(bf16[32,1024]{1,0:T(8,128)(2,1)S(1)} %get-tuple-element.91), channel_id=1, source_target_pairs={{2,1},{5,4},{7,6},{8,9},{11,10},{14,13},{17,18},{20,21},{23,22},{2... | collective-permute-start | bytes 196616 | tf_op jit(solution)/shard_map/cond/branch_2_fun/ppermute | solution.py:267
  17.0 2.2 %collective-permute-start.48 = (bf16[32,1024]{1,0:T(8,128)(2,1)S(1)}, bf16[32,1024]{1,0:T(8,128)(2,1)S(1)}, u32[]{:S(2)}, u32[]{:S(2)}) collective-permute-start(bf16[32,1024]{1,0:T(8,128)(2,1)S(1)} %get-tuple-element.91), channel_id=1, source_target_pairs={{3,7},{5,1},{8,12},{14,10},{17,21},{23,19},{26,30},{28,24}} | collective-permute-start | bytes 196616 | tf_op jit(solution)/shard_map/cond/branch_2_fun/ppermute | solution.py:267
  19.2 6.5 %collective-permute-start.53 = (bf16[32,1024]{1,0:T(8,128)(2,1)S(1)}, bf16[32,1024]{1,0:T(8,128)(2,1)S(1)}, u32[]{:S(2)}, u32[]{:S(2)}) collective-permute-start(bf16[32,1024]{1,0:T(8,128)(2,1)S(1)} %get-tuple-element.93), channel_id=1, source_target_pairs={{0,8},{1,9},{2,26},{3,11},{4,12},{5,29},{6,14},{7,15},{8,0},{9,1},... | collective-permute-start | bytes 196616 | tf_op jit(solution)/shard_map/cond/branch_2_fun/ppermute | solution.py:267
  19.6 7.8 %collective-permute-start.52 = (bf16[32,1024]{1,0:T(8,128)(2,1)S(1)}, bf16[32,1024]{1,0:T(8,128)(2,1)S(1)}, u32[]{:S(2)}, u32[]{:S(2)}) collective-permute-start(bf16[32,1024]{1,0:T(8,128)(2,1)S(1)} %get-tuple-element.93), channel_id=1, source_target_pairs={{0,1},{1,0},{2,3},{3,2},{4,5},{5,4},{6,7},{7,6},{8,11},{9,10},{10,... | collective-permute-start | bytes 196616 | tf_op jit(solution)/shard_map/cond/branch_2_fun/ppermute | solution.py:267
  25.0 2.4 %collective-permute-start.51 = (bf16[32,1024]{1,0:T(8,128)(2,1)S(1)}, bf16[32,1024]{1,0:T(8,128)(2,1)S(1)}, u32[]{:S(2)}, u32[]{:S(2)}) collective-permute-start(bf16[32,1024]{1,0:T(8,128)(2,1)S(1)} %get-tuple-element.93), channel_id=1, source_target_pairs={{0,4},{4,0},{9,13},{13,9},{18,22},{22,18},{27,31},{31,27}} | collective-permute-start | bytes 196616 | tf_op jit(solution)/shard_map/cond/branch_2_fun/ppermute | solution.py:267
  27.4 6.2 %collective-permute-start.56 = (bf16[32,1024]{1,0:T(8,128)(2,1)S(1)}, bf16[32,1024]{1,0:T(8,128)(2,1)S(1)}, u32[]{:S(2)}, u32[]{:S(2)}) collective-permute-start(bf16[32,1024]{1,0:T(8,128)(2,1)S(1)} %get-tuple-element.95), channel_id=1, source_target_pairs={{0,8},{9,17},{10,2},{12,20},{13,5},{15,7},{16,24},{18,26},{19,11},... | collective-permute-start | bytes 196616 | tf_op jit(solution)/shard_map/cond/branch_2_fun/ppermute | solution.py:267
  28.7 7.6 %collective-permute-start.55 = (bf16[32,1024]{1,0:T(8,128)(2,1)S(1)}, bf16[32,1024]{1,0:T(8,128)(2,1)S(1)}, u32[]{:S(2)}, u32[]{:S(2)}) collective-permute-start(bf16[32,1024]{1,0:T(8,128)(2,1)S(1)} %get-tuple-element.95), channel_id=1, source_target_pairs={{1,2},{4,5},{6,7},{9,8},{10,11},{13,14},{18,17},{21,20},{22,23},{2... | collective-permute-start | bytes 196616 | tf_op jit(solution)/shard_map/cond/branch_2_fun/ppermute | solution.py:267
  30.0 6.3 %collective-permute-start.54 = (bf16[32,1024]{1,0:T(8,128)(2,1)S(1)}, bf16[32,1024]{1,0:T(8,128)(2,1)S(1)}, u32[]{:S(2)}, u32[]{:S(2)}) collective-permute-start(bf16[32,1024]{1,0:T(8,128)(2,1)S(1)} %get-tuple-element.95), channel_id=1, source_target_pairs={{1,5},{10,14},{12,8},{19,23},{21,17},{30,26}} | collective-permute-start | bytes 196616 | tf_op jit(solution)/shard_map/cond/branch_2_fun/ppermute | solution.py:267
  36.8 3.2 %collective-permute-start.59 = (bf16[32,1024]{1,0:T(8,128)(2,1)S(1)}, bf16[32,1024]{1,0:T(8,128)(2,1)S(1)}, u32[]{:S(2)}, u32[]{:S(2)}) collective-permute-start(bf16[32,1024]{1,0:T(8,128)(2,1)S(1)} %get-tuple-element.97), channel_id=1, source_target_pairs={{4,12},{8,16},{9,1},{11,3},{13,21},{14,6},{17,25},{18,10},{20,28},... | collective-permute-start | bytes 196616 | tf_op jit(solution)/shard_map/cond/branch_2_fun/ppermute | solution.py:267
  38.1 1.9 %collective-permute-start.58 = (bf16[32,1024]{1,0:T(8,128)(2,1)S(1)}, bf16[32,1024]{1,0:T(8,128)(2,1)S(1)}, u32[]{:S(2)}, u32[]{:S(2)}) collective-permute-start(bf16[32,1024]{1,0:T(8,128)(2,1)S(1)} %get-tuple-element.97), channel_id=1, source_target_pairs={{0,1},{2,3},{5,6},{9,10},{13,12},{14,15},{17,16},{18,19},{22,21},{... | collective-permute-start | bytes 196616 | tf_op jit(solution)/shard_map/cond/branch_2_fun/ppermute | solution.py:267
  38.8 1.2 %collective-permute-start.57 = (bf16[32,1024]{1,0:T(8,128)(2,1)S(1)}, bf16[32,1024]{1,0:T(8,128)(2,1)S(1)}, u32[]{:S(2)}, u32[]{:S(2)}) collective-permute-start(bf16[32,1024]{1,0:T(8,128)(2,1)S(1)} %get-tuple-element.97), channel_id=1, source_target_pairs={{2,6},{7,3},{11,15},{20,16},{24,28},{29,25}} | collective-permute-start | bytes 196616 | tf_op jit(solution)/shard_map/cond/branch_2_fun/ppermute | solution.py:267
  40.0 5.8 %collective-permute-start.62 = (bf16[16,1024]{1,0:T(8,128)(2,1)S(1)}, bf16[16,1024]{1,0:T(8,128)(2,1)S(1)}, u32[]{:S(2)}, u32[]{:S(2)}) collective-permute-start(bf16[16,1024]{1,0:T(8,128)(2,1)S(1)} %get-tuple-element.99), channel_id=1, source_target_pairs={{0,8},{9,17},{10,2},{12,20},{13,5},{15,7},{16,24},{18,26},{19,11},... | collective-permute-start | bytes 98312 | tf_op jit(solution)/shard_map/cond/branch_2_fun/ppermute | solution.py:267
  41.3 7.1 %collective-permute-start.61 = (bf16[16,1024]{1,0:T(8,128)(2,1)S(1)}, bf16[16,1024]{1,0:T(8,128)(2,1)S(1)}, u32[]{:S(2)}, u32[]{:S(2)}) collective-permute-start(bf16[16,1024]{1,0:T(8,128)(2,1)S(1)} %get-tuple-element.99), channel_id=1, source_target_pairs={{1,2},{4,5},{6,7},{9,8},{10,11},{13,14},{18,17},{21,20},{22,23},{2... | collective-permute-start | bytes 98312 | tf_op jit(solution)/shard_map/cond/branch_2_fun/ppermute | solution.py:267
  42.6 5.8 %collective-permute-start.60 = (bf16[16,1024]{1,0:T(8,128)(2,1)S(1)}, bf16[16,1024]{1,0:T(8,128)(2,1)S(1)}, u32[]{:S(2)}, u32[]{:S(2)}) collective-permute-start(bf16[16,1024]{1,0:T(8,128)(2,1)S(1)} %get-tuple-element.99), channel_id=1, source_target_pairs={{3,7},{5,1},{12,8},{19,23},{26,30},{28,24}} | collective-permute-start | bytes 98312 | tf_op jit(solution)/shard_map/cond/branch_2_fun/ppermute | solution.py:267
  48.5 0.6 %copy-start = (bf16[1,1,1,2,16,1024]{5,4,3,2,1,0:T(8,128)(2,1)}, bf16[1,1,1,2,16,1024]{5,4,3,2,1,0:T(8,128)(2,1)S(1)}, u32[]{:S(2)}) copy-start(bf16[1,1,1,2,16,1024]{5,4,3,2,1,0:T(8,128)(2,1)S(1)} %get-tuple-element.308) | copy-start | bytes 196612

commit v3 on v2

--- a/solution.py
+++ b/solution.py
@@ -57,22 +57,22 @@
 
 SHARED = (
     (
-        (0, 1, 2, -1, 3, 4, 3),
-        (0, 5, 6, -2, 7, 8, 9),
-        (9, 6, 5, -3, 8, 7, 8),
-        (1, 2, 10, -4, 4, 3, 4),
+        (0, 1, 2, -1, 3, 4, 5),
+        (6, 7, 8, -2, 9, 10, 5),
+        (6, 8, 7, -3, 10, 9, 5),
+        (0, 11, 1, -3, 4, 3, 6),
     ),
     (
-        (0, 1, 2, 3, 0, 4, 5),
-        (6, 7, 8, 9, 6, 5, 4),
-        (7, 5, 6, 10, 11, 7, 1),
-        (2, 4, 0, 12, 2, 1, 4),
+        (0, 1, 2, 3, 4, 5, 0),
+        (6, 5, 7, 8, 1, 6, 3),
+        (3, 6, 1, 0, 7, 5, 9),
+        (1, 5, 10, 9, 2, 1, 0),
     ),
     (
         (0, 1, 2, -1, 3, 4, 5),
-        (6, 7, 8, -2, 9, 10, 9),
-        (5, 6, 7, -3, 10, 9, 10),
-        (5, 0, 1, -4, 4, 3, 4),
+        (0, 6, 7, -2, 8, 9, 5),
+        (6, 7, 10, -3, 9, 8, 11),
+        (0, 2, 1, -4, 4, 11, 5),
     ),
 )
 
@@ -118,36 +118,40 @@
     return range(max(0, hop - STEPS), min(max(0, deepest - STEPS), hop - 1) + 1)
 
 
-def begin_kernel(sizes, bits, lead_hbm, sources_hbm, message_ref, traces_ref, held_ref, lead_ref, raw_ref, arrived):
-    copies = [
-        pltpu.make_async_copy(sources_hbm, raw_ref, arrived.at[0]),
-        pltpu.make_async_copy(lead_hbm, lead_ref, arrived.at[1]),
-    ]
-    for copy in copies:
-        copy.start()
-    for copy in copies:
-        copy.wait()
-    lead = lead_ref[0]
-    entry = my_depth(sizes, bits) == 0
-    message_ref[...] = raw_ref[jnp.where(entry, lead, 1 - lead)].astype(message_ref.dtype)
-    for slot in range(2):
-        source = raw_ref[lead if slot == 0 else 1 - lead]
-        held_ref[slot] = source
-        traces_ref[slot] = source.astype(traces_ref.dtype)
+def sooner(sizes, bits):
+    return 2 * my_depth(sizes, bits) < sum(size - 1 for size in sizes)
+
+
+def slots_by_arrival(sizes, bits, lead):
+    first = jnp.where(sooner(sizes, bits), lead, 1 - lead)
+    return first, 1 - first
+
+
+def begin_kernel(sizes, bits, lead_hbm, sources_hbm, message_ref, lead_ref, raw_ref, arrived):
+    deepest = sum(size - 1 for size in sizes)
+    depth = my_depth(sizes, bits)
+
+    @pl.when((depth == 0) | (depth == deepest))
+    def _():
+        copies = [
+            pltpu.make_async_copy(sources_hbm, raw_ref, arrived.at[0]),
+            pltpu.make_async_copy(lead_hbm, lead_ref, arrived.at[1]),
+        ]
+        for copy in copies:
+            copy.start()
+        for copy in copies:
+            copy.wait()
+        first, _ = slots_by_arrival(sizes, bits, lead_ref[0])
+        message_ref[...] = raw_ref[first].astype(message_ref.dtype)
 
 
 def begin(sizes, bits, lead, sources):
-    vmem = pl.BlockSpec(memory_space=pltpu.VMEM)
     hbm = pl.BlockSpec(memory_space=pl.ANY)
     return pl.pallas_call(
         functools.partial(begin_kernel, sizes, bits),
-        out_shape=(
-            pltpu.VMEM(sources.shape[1:], jnp.bfloat16),
-            pltpu.VMEM(sources.shape, jnp.bfloat16),
-            pltpu.VMEM(sources.shape, sources.dtype),
-        ),
+        out_shape=pltpu.VMEM(sources.shape[1:], jnp.bfloat16),
         in_specs=[hbm, hbm],
-        out_specs=(vmem, vmem, vmem),
+        out_specs=pl.BlockSpec(memory_space=pltpu.VMEM),
         scratch_shapes=[
             pltpu.SMEM(lead.shape, lead.dtype),
             pltpu.VMEM(sources.shape, sources.dtype),
@@ -158,52 +162,85 @@
     )(lead, sources)
 
 
-def load_kernel(lead_ref, maps_ref, after_ref, held_ref, arrived):
-    lead = lead_ref[0]
+def load_first_kernel(
+    sizes, bits, lead_ref, maps_hbm, sources_hbm, after_ref, map_ref, held_ref, traces_ref, arrived
+):
+    slots = slots_by_arrival(sizes, bits, lead_ref[0])
     copies = [
-        pltpu.make_async_copy(
-            maps_ref.at[lead if slot == 0 else 1 - lead], held_ref.at[slot], arrived.at[slot]
-        )
-        for slot in range(2)
+        pltpu.make_async_copy(sources_hbm.at[slot], held_ref.at[place], arrived.at[place])
+        for place, slot in enumerate(slots)
     ]
+    copies.append(pltpu.make_async_copy(maps_hbm.at[slots[0]], map_ref, arrived.at[2]))
     for copy in copies:
         copy.start()
     for copy in copies:
         copy.wait()
-
-
-def load(lead, maps, after):
+    traces_ref[...] = held_ref[...].astype(traces_ref.dtype)
+
+
+def load_first(sizes, bits, lead, maps, sources, after):
     hbm = pl.BlockSpec(memory_space=pl.ANY)
+    vmem = pl.BlockSpec(memory_space=pltpu.VMEM)
     return pl.pallas_call(
-        load_kernel,
-        out_shape=pltpu.VMEM(maps.shape, maps.dtype),
-        in_specs=[pl.BlockSpec(memory_space=pltpu.SMEM), hbm, hbm],
-        out_specs=pl.BlockSpec(memory_space=pltpu.VMEM),
-        scratch_shapes=[pltpu.SemaphoreType.DMA((2,))],
+        functools.partial(load_first_kernel, sizes, bits),
+        out_shape=(
+            pltpu.VMEM(maps.shape[1:], maps.dtype),
+            pltpu.VMEM(sources.shape, sources.dtype),
+            pltpu.VMEM(sources.shape, jnp.bfloat16),
+        ),
+        in_specs=[pl.BlockSpec(memory_space=pltpu.SMEM), hbm, hbm, vmem],
+        out_specs=(vmem, vmem, vmem),
+        scratch_shapes=[pltpu.SemaphoreType.DMA((3,))],
         compiler_params=ROOM,
-        name="load",
-    )(lead, maps, after)
+        name="load_first",
+    )(lead, maps, sources, pltpu.with_memory_space_constraint(after, pltpu.VMEM))
+
+
+def load_second_kernel(sizes, bits, lead_ref, maps_hbm, after_ref, map_ref, arrived):
+    _, slot = slots_by_arrival(sizes, bits, lead_ref[0])
+    copy = pltpu.make_async_copy(maps_hbm.at[slot], map_ref, arrived)
+    copy.start()
+    copy.wait()
+
+
+def load_second(sizes, bits, lead, maps, after):
+    hbm = pl.BlockSpec(memory_space=pl.ANY)
+    vmem = pl.BlockSpec(memory_space=pltpu.VMEM)
+    return pl.pallas_call(
+        functools.partial(load_second_kernel, sizes, bits),
+        out_shape=pltpu.VMEM(maps.shape[1:], maps.dtype),
+        in_specs=[pl.BlockSpec(memory_space=pltpu.SMEM), hbm, vmem],
+        out_specs=vmem,
+        scratch_shapes=[pltpu.SemaphoreType.DMA(())],
+        compiler_params=ROOM,
+        name="load_second",
+    )(lead, maps, pltpu.with_memory_space_constraint(after, pltpu.VMEM))
+
+
+def chains_sent(hop, deepest):
+    return range(max(0, hop - STEPS), min(max(0, deepest - STEPS), hop - 1) + 1)
 
 
 def hop_kernel(
-    hop, sizes, bits, lead_ref, y_ref, z_ref, x_ref, maps_ref, sources_ref, old_ref, *results
+    hop, sizes, bits, lead_ref, y_ref, z_ref, x_ref, sources_ref, old_ref, *refs
 ):
     deepest = sum(size - 1 for size in sizes)
     depth = my_depth(sizes, bits)
-    back = deepest - depth
     last = hop == deepest
+    results = refs[-1:] if last else refs[-2:]
+    map_ref = refs[0]
     traces_ref = results[-1]
     rows = sources_ref.shape[1]
-
-    def place_of(slot):
-        return jnp.where(lead_ref[0] == 0, slot, 1 - slot) if last else slot
-
-    for slot in range(2):
-        traces_ref[place_of(slot)] = old_ref[slot]
-
-    @pl.when((depth == hop) | (back == hop))
+    turn = 0 if 2 * hop < deepest else 1
+
+    def place_of(turn):
+        return slots_by_arrival(sizes, bits, lead_ref[0])[turn] if last else turn
+
+    for kept in range(2):
+        traces_ref[place_of(kept)] = old_ref[kept]
+
+    @pl.when((depth == hop) | (depth == deepest - hop))
     def _():
-        slot = jnp.where(depth == hop, 0, 1)
         summed = None
         for axis, ref in enumerate((x_ref, y_ref, z_ref)):
             index = lax.axis_index(AXES[axis])
@@ -214,9 +251,9 @@
             came = jnp.where(inside == 1, ref[...].astype(jnp.float32), 0.0)
             summed = came if summed is None else summed + came
         mapped = jnp.dot(
-            summed.astype(jnp.bfloat16), maps_ref[slot], preferred_element_type=jnp.float32
+            summed.astype(jnp.bfloat16), map_ref[...], preferred_element_type=jnp.float32
         )
-        source = sources_ref[slot]
+        source = sources_ref[turn]
         came = chains_sent(hop, deepest)
         kept = came if last else chains_sent(hop + 1, deepest)
         for chain in sorted({*came, *kept}):
@@ -229,28 +266,26 @@
                 at = kept.index(chain) * rows
                 results[0][at : at + rows] = new
             if chain == max(0, hop - STEPS):
-                traces_ref[place_of(slot)] = new
+                traces_ref[place_of(turn)] = new
 
 
 def take_hop(hop, sizes, bits, lead, came, maps, sources, traces):
     deepest = sum(size - 1 for size in sizes)
     last = hop == deepest
     vmem = pl.BlockSpec(memory_space=pltpu.VMEM)
-    came = [came[axis] for axis in reversed(ORDER)]
-    held = [pltpu.with_memory_space_constraint(a, pltpu.VMEM) for a in came]
-    held += [pltpu.with_memory_space_constraint(a, pltpu.VMEM) for a in (maps, sources, traces)]
+    held = [came[axis] for axis in reversed(ORDER)] + [sources, traces] + maps
+    held = [pltpu.with_memory_space_constraint(a, pltpu.VMEM) for a in held]
     shapes = (jax.ShapeDtypeStruct(traces.shape, traces.dtype),)
     if not last:
+        message = (len(chains_sent(hop + 1, deepest)) * sources.shape[1], sources.shape[2])
         shapes = (
-            pltpu.VMEM(
-                (len(chains_sent(hop + 1, deepest)) * sources.shape[1], sources.shape[2]), traces.dtype
-            ),
+            pltpu.VMEM(message, traces.dtype),
             pltpu.VMEM(traces.shape, traces.dtype),
         )
     results = pl.pallas_call(
         functools.partial(hop_kernel, hop, sizes, bits),
         out_shape=shapes,
-        in_specs=[pl.BlockSpec(memory_space=pltpu.SMEM if last else pl.ANY)] + [vmem] * 6,
+        in_specs=[pl.BlockSpec(memory_space=pltpu.SMEM if last else pl.ANY)] + [vmem] * len(held),
         out_specs=(vmem,) * len(shapes),
         compiler_params=ROOM,
         name=f"hop{hop}",
@@ -260,14 +295,20 @@
 
 def wave(sizes, bits, lead, maps, sources):
     deepest = sum(size - 1 for size in sizes)
-    message, traces, sources = begin(sizes, bits, lead, sources)
+    message = begin(sizes, bits, lead, sources)
+    later = min(2, deepest)
     for hop in range(1, deepest + 1):
         came = [None] * 3
         for axis in ORDER:
             came[axis] = lax.ppermute(message, AXES, pairs_of(sizes, bits, axis, hop))
         if hop == 1:
-            maps = load(lead, maps, message)
-        message, traces = take_hop(hop, sizes, bits, lead, came, maps, sources, traces)
+            first, sources, traces = load_first(sizes, bits, lead, maps, sources, message)
+        if hop == later:
+            second = load_second(sizes, bits, lead, maps, message)
+        used = [first] if 2 * hop < deepest else [second]
+        if hop == later and 2 * hop < deepest:
+            used.append(second)
+        message, traces = take_hop(hop, sizes, bits, lead, came, used, sources, traces)
     return traces
 
 

time: 49.7 us -> 49.5 us (level)
  the two profiles are of different devices: /device:TPU:2 before, /device:TPU:0 now
where the time goes in v3:
time: 49.5 us; the launch traced here: 48.7 us
  starting transfers between devices  30.3 us (61%)
  waiting for transfers between devices  13.3 us (27%)
  Pallas kernels  3.44 us (7%)
  between operations  0.67 us (1%)
  local copies, waits for them, and re-layouts  0.65 us (1%)
    ppermute x21, starting transfers between devices, wave(): came[axis] = lax.ppermute(message, AXES, pairs_of(sizes, bits, axis, hop))  30.3 us
    ppermute x21, waiting for transfers between devices, wave(): came[axis] = lax.ppermute(message, AXES, pairs_of(sizes, bits, axis, hop))  13.3 us
    pallas_call x1, Pallas kernels, load_first(): pl.pallas_call(functools.partial(load_first_kernel, sizes, bits), out_sha...  1.85 us
  transfers between devices with their start and end apart: 21, of which 7 were waited for; matrix products, arithmetic and copies ran while one was open for 0% of the time, Pallas kernels for 4%

profile of v3, /device:TPU:0, one launch (start us, length us, event | category | flops | bytes accessed | tf_op | source)
XLA Modules:
  0.0 48.7 jit_solution(7805824442026356560)
XLA Ops:
  0.7 47.4 %conditional.1 = (bf16[1,1,1,2,16,1024]{5,4,3,2,1,0:T(8,128)(2,1)S(1)}) conditional(s32[]{:T(128)} %clamp.3, (s32[]{:T(128)}, f32[1,1,1,2,16,1024]{5,4,3,2,1,0:T(8,128)}, bf16[1,1,1,2,1024,1024]{5,4,3,2,1,0:T(8,128)(2,1)}) %tuple.21, (s32[]{:T(128)}, f32[1,1,1,2,16,1024]{5,4,3,2,1,0:T(8,128)}, ...), branch_computations={%region_0.1_spmd, %region_1.2_spmd, %region_2.3_spmd, %region_3.4_... | conditional | bytes 21496684 | solution.py:354
  0.7 1.0 %begin.7.after_ref = bf16[16,1024]{1,0:T(8,128)(2,1)S(1)} custom-call(s32[1]{0:T(128)} %bitcast.12.lead_hbm.lead_ref, f32[2,16,1024]{2,1,0:T(8,128)} %bitcast.34), custom_call_target="tpu_custom_call" | custom-call | tf_op jit(solution)/shard_map/cond/branch_3_fun/begin/pallas_call | solution.py:150
  1.7 4.0 %collective-permute-start.65 = (bf16[16,1024]{1,0:T(8,128)(2,1)S(1)}, bf16[16,1024]{1,0:T(8,128)(2,1)S(1)}, u32[]{:S(2)}, u32[]{:S(2)}) collective-permute-start(bf16[16,1024]{1,0:T(8,128)(2,1)S(1)} %begin.7.after_ref), channel_id=1, source_target_pairs={{0,8},{4,12},{27,19},{31,23}} | collective-permute-start | bytes 98312 | tf_op jit(solution)/shard_map/cond/branch_3_fun/ppermute | solution.py:303
  5.6 1.3 %collective-permute-start.64 = (bf16[16,1024]{1,0:T(8,128)(2,1)S(1)}, bf16[16,1024]{1,0:T(8,128)(2,1)S(1)}, u32[]{:S(2)}, u32[]{:S(2)}) collective-permute-start(bf16[16,1024]{1,0:T(8,128)(2,1)S(1)} %begin.7.after_ref), channel_id=1, source_target_pairs={{0,1},{3,2},{4,5},{27,26},{28,29},{31,30}} | collective-permute-start | bytes 98312 | tf_op jit(solution)/shard_map/cond/branch_3_fun/ppermute | solution.py:303
  6.9 1.5 %collective-permute-start.63 = (bf16[16,1024]{1,0:T(8,128)(2,1)S(1)}, bf16[16,1024]{1,0:T(8,128)(2,1)S(1)}, u32[]{:S(2)}, u32[]{:S(2)}) collective-permute-start(bf16[16,1024]{1,0:T(8,128)(2,1)S(1)} %begin.7.after_ref), channel_id=1, source_target_pairs={{0,4},{5,1},{8,12},{12,8},{14,10},{17,21},{19,23},{23,19},{26,30},... | collective-permute-start | bytes 98312 | tf_op jit(solution)/shard_map/cond/branch_3_fun/ppermute | solution.py:303
  8.4 0.0 copy-start.3
  8.4 1.9 %load_first.7 = (bf16[1024,1024]{1,0:T(8,128)(2,1)S(1)}, f32[2,16,1024]{2,1,0:T(8,128)S(1)}, bf16[2,16,1024]{2,1,0:T(8,128)(2,1)S(1)}) custom-call(s32[1]{0:T(128)} %bitcast.12.lead_hbm.lead_ref, bf16[2,1024,1024]{2,1,0:T(8,128)(2,1)} %bitcast.26, f32[2,16,1024]{2,1,0:T(8,128)} %bitcast.35, bf16[16,1024]{1,0:T(8,128)(2,1)S(1)} %begin.7.after_ref), custom_call_target="tpu_custom_call" | custom-call | tf_op jit(solution)/shard_map/cond/branch_3_fun/load_first/pallas_call | solution.py:184
  10.3 0.0 collective-permute-done.65.x_ref
  10.3 0.0 collective-permute-done.64.z_ref
  10.3 0.0 collective-permute-done.63.y_ref
  10.3 0.8 %collective-permute-start.68 = (bf16[32,1024]{1,0:T(8,128)(2,1)S(1)}, bf16[32,1024]{1,0:T(8,128)(2,1)S(1)}, u32[]{:S(2)}, u32[]{:S(2)}) collective-permute-start(bf16[32,1024]{1,0:T(8,128)(2,1)S(1)} %get-tuple-element.107.after_ref), channel_id=1, source_target_pairs={{1,9},{4,12},{8,16},{23,15},{27,19},{30,22}} | collective-permute-start | bytes 196616 | tf_op jit(solution)/shard_map/cond/branch_3_fun/ppermute | solution.py:303
  11.1 0.7 %collective-permute-start.67 = (bf16[32,1024]{1,0:T(8,128)(2,1)S(1)}, bf16[32,1024]{1,0:T(8,128)(2,1)S(1)}, u32[]{:S(2)}, u32[]{:S(2)}) collective-permute-start(bf16[32,1024]{1,0:T(8,128)(2,1)S(1)} %get-tuple-element.107.after_ref), channel_id=1, source_target_pairs={{1,2},{4,5},{6,7},{8,9},{11,10},{13,14},{18,17},{20,21},{23,22},{2... | collective-permute-start | bytes 196616 | tf_op jit(solution)/shard_map/cond/branch_3_fun/ppermute | solution.py:303
  11.8 0.7 %collective-permute-start.66 = (bf16[32,1024]{1,0:T(8,128)(2,1)S(1)}, bf16[32,1024]{1,0:T(8,128)(2,1)S(1)}, u32[]{:S(2)}, u32[]{:S(2)}) collective-permute-start(bf16[32,1024]{1,0:T(8,128)(2,1)S(1)} %get-tuple-element.107.after_ref), channel_id=1, source_target_pairs={{1,5},{2,6},{8,12},{11,15},{20,16},{23,19},{29,25},{30,26}} | collective-permute-start | bytes 196616 | tf_op jit(solution)/shard_map/cond/branch_3_fun/ppermute | solution.py:303
  12.5 0.0 copy-done.3
  12.5 0.2 load_second.7.refs_1_.refs_0_
  12.7 0.0 collective-permute-done.68.x_ref
  12.7 0.0 collective-permute-done.67.z_ref
  12.7 0.0 collective-permute-done.66.y_ref
  12.7 4.1 %collective-permute-start.71 = (bf16[32,1024]{1,0:T(8,128)(2,1)S(1)}, bf16[32,1024]{1,0:T(8,128)(2,1)S(1)}, u32[]{:S(2)}, u32[]{:S(2)}) collective-permute-start(bf16[32,1024]{1,0:T(8,128)(2,1)S(1)} %get-tuple-element.109), channel_id=1, source_target_pairs={{0,8},{2,10},{5,13},{9,17},{12,20},{15,7},{16,24},{19,11},{22,14},... | collective-permute-start | bytes 196616 | tf_op jit(solution)/shard_map/cond/branch_3_fun/ppermute | solution.py:303
  16.8 2.4 %collective-permute-start.70 = (bf16[32,1024]{1,0:T(8,128)(2,1)S(1)}, bf16[32,1024]{1,0:T(8,128)(2,1)S(1)}, u32[]{:S(2)}, u32[]{:S(2)}) collective-permute-start(bf16[32,1024]{1,0:T(8,128)(2,1)S(1)} %get-tuple-element.109), channel_id=1, source_target_pairs={{0,1},{2,3},{5,6},{9,10},{12,13},{15,14},{16,17},{19,18},{22,21},{... | collective-permute-start | bytes 196616 | tf_op jit(solution)/shard_map/cond/branch_3_fun/ppermute | solution.py:303
  19.2 0.7 %collective-permute-start.69 = (bf16[32,1024]{1,0:T(8,128)(2,1)S(1)}, bf16[32,1024]{1,0:T(8,128)(2,1)S(1)}, u32[]{:S(2)}, u32[]{:S(2)}) collective-permute-start(bf16[32,1024]{1,0:T(8,128)(2,1)S(1)} %get-tuple-element.109), channel_id=1, source_target_pairs={{2,6},{9,13},{15,11},{16,20},{22,18},{29,25}} | collective-permute-start | bytes 196616 | tf_op jit(solution)/shard_map/cond/branch_3_fun/ppermute | solution.py:303
  19.9 0.0 collective-permute-done.71.x_ref
  19.9 1.2 %collective-permute-done.70.z_ref = bf16[32,1024]{1,0:T(8,128)(2,1)S(1)} collective-permute-done((bf16[32,1024]{1,0:T(8,128)(2,1)S(1)}, bf16[32,1024]{1,0:T(8,128)(2,1)S(1)}, u32[]{:S(2)}, u32[]{:S(2)}) %collective-permute-start.70) | collective-permute-done | bytes 65568 | tf_op jit(solution)/shard_map/cond/branch_3_fun/ppermute | solution.py:303
  21.1 0.0 collective-permute-done.69.y_ref
  21.1 0.1 collective-permute-start.74
  21.2 3.0 %collective-permute-start.73 = (bf16[32,1024]{1,0:T(8,128)(2,1)S(1)}, bf16[32,1024]{1,0:T(8,128)(2,1)S(1)}, u32[]{:S(2)}, u32[]{:S(2)}) collective-permute-start(bf16[32,1024]{1,0:T(8,128)(2,1)S(1)} %get-tuple-element.111), channel_id=1, source_target_pairs={{0,1},{1,0},{2,3},{3,2},{4,5},{5,4},{6,7},{7,6},{8,9},{9,8},{10,11... | collective-permute-start | bytes 196616 | tf_op jit(solution)/shard_map/cond/branch_3_fun/ppermute | solution.py:303
  24.2 0.7 %collective-permute-start.72 = (bf16[32,1024]{1,0:T(8,128)(2,1)S(1)}, bf16[32,1024]{1,0:T(8,128)(2,1)S(1)}, u32[]{:S(2)}, u32[]{:S(2)}) collective-permute-start(bf16[32,1024]{1,0:T(8,128)(2,1)S(1)} %get-tuple-element.111), channel_id=1, source_target_pairs={{3,7},{7,3},{10,14},{14,10},{17,21},{21,17},{24,28},{28,24}} | collective-permute-start | bytes 196616 | tf_op jit(solution)/shard_map/cond/branch_3_fun/ppermute | solution.py:303
  24.9 0.6 %collective-permute-done.74.x_ref = bf16[32,1024]{1,0:T(8,128)(2,1)S(1)} collective-permute-done((bf16[32,1024]{1,0:T(8,128)(2,1)S(1)}, bf16[32,1024]{1,0:T(8,128)(2,1)S(1)}, u32[]{:S(2)}, u32[]{:S(2)}) %collective-permute-start.74) | collective-permute-done | bytes 65568 | tf_op jit(solution)/shard_map/cond/branch_3_fun/ppermute | solution.py:303
  25.5 1.0 %collective-permute-done.73.z_ref = bf16[32,1024]{1,0:T(8,128)(2,1)S(1)} collective-permute-done((bf16[32,1024]{1,0:T(8,128)(2,1)S(1)}, bf16[32,1024]{1,0:T(8,128)(2,1)S(1)}, u32[]{:S(2)}, u32[]{:S(2)}) %collective-permute-start.73) | collective-permute-done | bytes 65568 | tf_op jit(solution)/shard_map/cond/branch_3_fun/ppermute | solution.py:303
  26.4 0.0 collective-permute-done.72.y_ref
  26.5 1.3 %collective-permute-start.77 = (bf16[32,1024]{1,0:T(8,128)(2,1)S(1)}, bf16[32,1024]{1,0:T(8,128)(2,1)S(1)}, u32[]{:S(2)}, u32[]{:S(2)}) collective-permute-start(bf16[32,1024]{1,0:T(8,128)(2,1)S(1)} %get-tuple-element.113), channel_id=1, source_target_pairs={{7,15},{8,0},{10,2},{11,19},{13,5},{14,22},{17,9},{18,26},{20,12},... | collective-permute-start | bytes 196616 | tf_op jit(solution)/shard_map/cond/branch_3_fun/ppermute | solution.py:303
  27.8 1.3 %collective-permute-start.76 = (bf16[32,1024]{1,0:T(8,128)(2,1)S(1)}, bf16[32,1024]{1,0:T(8,128)(2,1)S(1)}, u32[]{:S(2)}, u32[]{:S(2)}) collective-permute-start(bf16[32,1024]{1,0:T(8,128)(2,1)S(1)} %get-tuple-element.113), channel_id=1, source_target_pairs={{1,0},{3,2},{6,5},{10,9},{13,12},{14,15},{17,16},{18,19},{21,22},{... | collective-permute-start | bytes 196616 | tf_op jit(solution)/shard_map/cond/branch_3_fun/ppermute | solution.py:303
  29.1 0.7 %collective-permute-start.75 = (bf16[32,1024]{1,0:T(8,128)(2,1)S(1)}, bf16[32,1024]{1,0:T(8,128)(2,1)S(1)}, u32[]{:S(2)}, u32[]{:S(2)}) collective-permute-start(bf16[32,1024]{1,0:T(8,128)(2,1)S(1)} %get-tuple-element.113), channel_id=1, source_target_pairs={{6,2},{11,15},{13,9},{18,22},{20,16},{25,29}} | collective-permute-start | bytes 196616 | tf_op jit(solution)/shard_map/cond/branch_3_fun/ppermute | solution.py:303
  29.7 2.9 %collective-permute-done.77.x_ref = bf16[32,1024]{1,0:T(8,128)(2,1)S(1)} collective-permute-done((bf16[32,1024]{1,0:T(8,128)(2,1)S(1)}, bf16[32,1024]{1,0:T(8,128)(2,1)S(1)}, u32[]{:S(2)}, u32[]{:S(2)}) %collective-permute-start.77) | collective-permute-done | bytes 65568 | tf_op jit(solution)/shard_map/cond/branch_3_fun/ppermute | solution.py:303
  32.6 1.3 %collective-permute-done.76.z_ref = bf16[32,1024]{1,0:T(8,128)(2,1)S(1)} collective-permute-done((bf16[32,1024]{1,0:T(8,128)(2,1)S(1)}, bf16[32,1024]{1,0:T(8,128)(2,1)S(1)}, u32[]{:S(2)}, u32[]{:S(2)}) %collective-permute-start.76) | collective-permute-done | bytes 65568 | tf_op jit(solution)/shard_map/cond/branch_3_fun/ppermute | solution.py:303
  33.9 0.0 collective-permute-done.75.y_ref
  33.9 0.7 %collective-permute-start.80 = (bf16[32,1024]{1,0:T(8,128)(2,1)S(1)}, bf16[32,1024]{1,0:T(8,128)(2,1)S(1)}, u32[]{:S(2)}, u32[]{:S(2)}) collective-permute-start(bf16[32,1024]{1,0:T(8,128)(2,1)S(1)} %get-tuple-element.115), channel_id=1, source_target_pairs={{3,11},{9,1},{10,18},{12,4},{14,6},{15,23},{16,8},{17,25},{19,27},... | collective-permute-start | bytes 196616 | tf_op jit(solution)/shard_map/cond/branch_3_fun/ppermute | solution.py:303
  34.6 0.7 %collective-permute-start.79 = (bf16[32,1024]{1,0:T(8,128)(2,1)S(1)}, bf16[32,1024]{1,0:T(8,128)(2,1)S(1)}, u32[]{:S(2)}, u32[]{:S(2)}) collective-permute-start(bf16[32,1024]{1,0:T(8,128)(2,1)S(1)} %get-tuple-element.115), channel_id=1, source_target_pairs={{2,1},{5,4},{6,7},{9,8},{22,23},{25,24},{26,27},{29,30}} | collective-permute-start | bytes 196616 | tf_op jit(solution)/shard_map/cond/branch_3_fun/ppermute | solution.py:303
  35.3 1.3 %collective-permute-start.78 = (bf16[32,1024]{1,0:T(8,128)(2,1)S(1)}, bf16[32,1024]{1,0:T(8,128)(2,1)S(1)}, u32[]{:S(2)}, u32[]{:S(2)}) collective-permute-start(bf16[32,1024]{1,0:T(8,128)(2,1)S(1)} %get-tuple-element.115), channel_id=1, source_target_pairs={{0,4},{5,1},{8,12},{12,8},{14,10},{17,21},{19,23},{23,19},{26,30},... | collective-permute-start | bytes 196616 | tf_op jit(solution)/shard_map/cond/branch_3_fun/ppermute | solution.py:303
  36.6 0.0 collective-permute-done.80.x_ref
  36.6 0.0 collective-permute-done.79.z_ref
  36.6 0.9 %collective-permute-done.78.y_ref = bf16[32,1024]{1,0:T(8,128)(2,1)S(1)} collective-permute-done((bf16[32,1024]{1,0:T(8,128)(2,1)S(1)}, bf16[32,1024]{1,0:T(8,128)(2,1)S(1)}, u32[]{:S(2)}, u32[]{:S(2)}) %collective-permute-start.78) | collective-permute-done | bytes 65568 | tf_op jit(solution)/shard_map/cond/branch_3_fun/ppermute | solution.py:303
  37.5 1.3 %collective-permute-start.83 = (bf16[16,1024]{1,0:T(8,128)(2,1)S(1)}, bf16[16,1024]{1,0:T(8,128)(2,1)S(1)}, u32[]{:S(2)}, u32[]{:S(2)}) collective-permute-start(bf16[16,1024]{1,0:T(8,128)(2,1)S(1)} %get-tuple-element.117), channel_id=1, source_target_pairs={{3,11},{7,15},{8,0},{23,31},{24,16},{28,20}} | collective-permute-start | bytes 98312 | tf_op jit(solution)/shard_map/cond/branch_3_fun/ppermute | solution.py:303
  38.8 1.3 %collective-permute-start.82 = (bf16[16,1024]{1,0:T(8,128)(2,1)S(1)}, bf16[16,1024]{1,0:T(8,128)(2,1)S(1)}, u32[]{:S(2)}, u32[]{:S(2)}) collective-permute-start(bf16[16,1024]{1,0:T(8,128)(2,1)S(1)} %get-tuple-element.117), channel_id=1, source_target_pairs={{1,0},{2,3},{5,4},{26,27},{29,28},{30,31}} | collective-permute-start | bytes 98312 | tf_op jit(solution)/shard_map/cond/branch_3_fun/ppermute | solution.py:303
  40.1 2.1 %collective-permute-start.81 = (bf16[16,1024]{1,0:T(8,128)(2,1)S(1)}, bf16[16,1024]{1,0:T(8,128)(2,1)S(1)}, u32[]{:S(2)}, u32[]{:S(2)}) collective-permute-start(bf16[16,1024]{1,0:T(8,128)(2,1)S(1)} %get-tuple-element.117), channel_id=1, source_target_pairs={{0,4},{4,0},{9,13},{13,9},{18,22},{22,18},{27,31},{31,27}} | collective-permute-start | bytes 98312 | tf_op jit(solution)/shard_map/cond/branch_3_fun/ppermute | solution.py:303
  42.2 5.4 %collective-permute-done.83.x_ref = bf16[16,1024]{1,0:T(8,128)(2,1)S(1)} collective-permute-done((bf16[16,1024]{1,0:T(8,128)(2,1)S(1)}, bf16[16,1024]{1,0:T(8,128)(2,1)S(1)}, u32[]{:S(2)}, u32[]{:S(2)}) %collective-permute-start.83) | collective-permute-done | bytes 32800 | tf_op jit(solution)/shard_map/cond/branch_3_fun/ppermute | solution.py:303
  47.6 0.0 collective-permute-done.82.z_ref
  47.6 0.0 collective-permute-done.81.y_ref
  47.6 0.4 hop7.7
  48.0 0.0 copy-start.4
  48.0 0.6 %copy-done.4 = bf16[1,1,1,2,16,1024]{5,4,3,2,1,0:T(8,128)(2,1)} copy-done((bf16[1,1,1,2,16,1024]{5,4,3,2,1,0:T(8,128)(2,1)}, bf16[1,1,1,2,16,1024]{5,4,3,2,1,0:T(8,128)(2,1)S(1)}, u32[]{:S(2)}) %copy-start.4) | copy-done | bytes 65560
  (6 shorter events, 0.1 us)
Async XLA Ops:
  1.7 8.6 %collective-permute-start.65 = (bf16[16,1024]{1,0:T(8,128)(2,1)S(1)}, bf16[16,1024]{1,0:T(8,128)(2,1)S(1)}, u32[]{:S(2)}, u32[]{:S(2)}) collective-permute-start(bf16[16,1024]{1,0:T(8,128)(2,1)S(1)} %begin.7.after_ref), channel_id=1, source_target_pairs={{0,8},{4,12},{27,19},{31,23}} | collective-permute-start | bytes 98312 | tf_op jit(solution)/shard_map/cond/branch_3_fun/ppermute | solution.py:303
  5.6 4.7 %collective-permute-start.64 = (bf16[16,1024]{1,0:T(8,128)(2,1)S(1)}, bf16[16,1024]{1,0:T(8,128)(2,1)S(1)}, u32[]{:S(2)}, u32[]{:S(2)}) collective-permute-start(bf16[16,1024]{1,0:T(8,128)(2,1)S(1)} %begin.7.after_ref), channel_id=1, source_target_pairs={{0,1},{3,2},{4,5},{27,26},{28,29},{31,30}} | collective-permute-start | bytes 98312 | tf_op jit(solution)/shard_map/cond/branch_3_fun/ppermute | solution.py:303
  6.9 3.4 %collective-permute-start.63 = (bf16[16,1024]{1,0:T(8,128)(2,1)S(1)}, bf16[16,1024]{1,0:T(8,128)(2,1)S(1)}, u32[]{:S(2)}, u32[]{:S(2)}) collective-permute-start(bf16[16,1024]{1,0:T(8,128)(2,1)S(1)} %begin.7.after_ref), channel_id=1, source_target_pairs={{0,4},{5,1},{8,12},{12,8},{14,10},{17,21},{19,23},{23,19},{26,30},... | collective-permute-start | bytes 98312 | tf_op jit(solution)/shard_map/cond/branch_3_fun/ppermute | solution.py:303
  8.4 4.1 %copy-start.3 = (bf16[1,1,1,2,1024,1024]{5,4,3,2,1,0:T(8,128)(2,1)S(1)}, bf16[1,1,1,2,1024,1024]{5,4,3,2,1,0:T(8,128)(2,1)}, u32[]{:S(2)}) copy-start(bf16[1,1,1,2,1024,1024]{5,4,3,2,1,0:T(8,128)(2,1)} %get-tuple-element.135) | copy-start | bytes 12582916 | tf_op jit(solution)/shard_map/cond
  10.3 2.3 %collective-permute-start.68 = (bf16[32,1024]{1,0:T(8,128)(2,1)S(1)}, bf16[32,1024]{1,0:T(8,128)(2,1)S(1)}, u32[]{:S(2)}, u32[]{:S(2)}) collective-permute-start(bf16[32,1024]{1,0:T(8,128)(2,1)S(1)} %get-tuple-element.107.after_ref), channel_id=1, source_target_pairs={{1,9},{4,12},{8,16},{23,15},{27,19},{30,22}} | collective-permute-start | bytes 196616 | tf_op jit(solution)/shard_map/cond/branch_3_fun/ppermute | solution.py:303
  11.1 1.5 %collective-permute-start.67 = (bf16[32,1024]{1,0:T(8,128)(2,1)S(1)}, bf16[32,1024]{1,0:T(8,128)(2,1)S(1)}, u32[]{:S(2)}, u32[]{:S(2)}) collective-permute-start(bf16[32,1024]{1,0:T(8,128)(2,1)S(1)} %get-tuple-element.107.after_ref), channel_id=1, source_target_pairs={{1,2},{4,5},{6,7},{8,9},{11,10},{13,14},{18,17},{20,21},{23,22},{2... | collective-permute-start | bytes 196616 | tf_op jit(solution)/shard_map/cond/branch_3_fun/ppermute | solution.py:303
  11.8 0.9 %collective-permute-start.66 = (bf16[32,1024]{1,0:T(8,128)(2,1)S(1)}, bf16[32,1024]{1,0:T(8,128)(2,1)S(1)}, u32[]{:S(2)}, u32[]{:S(2)}) collective-permute-start(bf16[32,1024]{1,0:T(8,128)(2,1)S(1)} %get-tuple-element.107.after_ref), channel_id=1, source_target_pairs={{1,5},{2,6},{8,12},{11,15},{20,16},{23,19},{29,25},{30,26}} | collective-permute-start | bytes 196616 | tf_op jit(solution)/shard_map/cond/branch_3_fun/ppermute | solution.py:303
  12.7 7.2 %collective-permute-start.71 = (bf16[32,1024]{1,0:T(8,128)(2,1)S(1)}, bf16[32,1024]{1,0:T(8,128)(2,1)S(1)}, u32[]{:S(2)}, u32[]{:S(2)}) collective-permute-start(bf16[32,1024]{1,0:T(8,128)(2,1)S(1)} %get-tuple-element.109), channel_id=1, source_target_pairs={{0,8},{2,10},{5,13},{9,17},{12,20},{15,7},{16,24},{19,11},{22,14},... | collective-permute-start | bytes 196616 | tf_op jit(solution)/shard_map/cond/branch_3_fun/ppermute | solution.py:303
  16.8 4.3 %collective-permute-start.70 = (bf16[32,1024]{1,0:T(8,128)(2,1)S(1)}, bf16[32,1024]{1,0:T(8,128)(2,1)S(1)}, u32[]{:S(2)}, u32[]{:S(2)}) collective-permute-start(bf16[32,1024]{1,0:T(8,128)(2,1)S(1)} %get-tuple-element.109), channel_id=1, source_target_pairs={{0,1},{2,3},{5,6},{9,10},{12,13},{15,14},{16,17},{19,18},{22,21},{... | collective-permute-start | bytes 196616 | tf_op jit(solution)/shard_map/cond/branch_3_fun/ppermute | solution.py:303
  19.2 1.9 %collective-permute-start.69 = (bf16[32,1024]{1,0:T(8,128)(2,1)S(1)}, bf16[32,1024]{1,0:T(8,128)(2,1)S(1)}, u32[]{:S(2)}, u32[]{:S(2)}) collective-permute-start(bf16[32,1024]{1,0:T(8,128)(2,1)S(1)} %get-tuple-element.109), channel_id=1, source_target_pairs={{2,6},{9,13},{15,11},{16,20},{22,18},{29,25}} | collective-permute-start | bytes 196616 | tf_op jit(solution)/shard_map/cond/branch_3_fun/ppermute | solution.py:303
  21.1 4.3 %collective-permute-start.74 = (bf16[32,1024]{1,0:T(8,128)(2,1)S(1)}, bf16[32,1024]{1,0:T(8,128)(2,1)S(1)}, u32[]{:S(2)}, u32[]{:S(2)}) collective-permute-start(bf16[32,1024]{1,0:T(8,128)(2,1)S(1)} %get-tuple-element.111), channel_id=1, source_target_pairs={{0,8},{1,9},{2,26},{3,11},{4,12},{5,29},{6,14},{7,15},{8,0},{9,1},... | collective-permute-start | bytes 196616 | tf_op jit(solution)/shard_map/cond/branch_3_fun/ppermute | solution.py:303
  21.2 5.2 %collective-permute-start.73 = (bf16[32,1024]{1,0:T(8,128)(2,1)S(1)}, bf16[32,1024]{1,0:T(8,128)(2,1)S(1)}, u32[]{:S(2)}, u32[]{:S(2)}) collective-permute-start(bf16[32,1024]{1,0:T(8,128)(2,1)S(1)} %get-tuple-element.111), channel_id=1, source_target_pairs={{0,1},{1,0},{2,3},{3,2},{4,5},{5,4},{6,7},{7,6},{8,9},{9,8},{10,11... | collective-permute-start | bytes 196616 | tf_op jit(solution)/shard_map/cond/branch_3_fun/ppermute | solution.py:303
  24.2 2.2 %collective-permute-start.72 = (bf16[32,1024]{1,0:T(8,128)(2,1)S(1)}, bf16[32,1024]{1,0:T(8,128)(2,1)S(1)}, u32[]{:S(2)}, u32[]{:S(2)}) collective-permute-start(bf16[32,1024]{1,0:T(8,128)(2,1)S(1)} %get-tuple-element.111), channel_id=1, source_target_pairs={{3,7},{7,3},{10,14},{14,10},{17,21},{21,17},{24,28},{28,24}} | collective-permute-start | bytes 196616 | tf_op jit(solution)/shard_map/cond/branch_3_fun/ppermute | solution.py:303
  26.5 6.2 %collective-permute-start.77 = (bf16[32,1024]{1,0:T(8,128)(2,1)S(1)}, bf16[32,1024]{1,0:T(8,128)(2,1)S(1)}, u32[]{:S(2)}, u32[]{:S(2)}) collective-permute-start(bf16[32,1024]{1,0:T(8,128)(2,1)S(1)} %get-tuple-element.113), channel_id=1, source_target_pairs={{7,15},{8,0},{10,2},{11,19},{13,5},{14,22},{17,9},{18,26},{20,12},... | collective-permute-start | bytes 196616 | tf_op jit(solution)/shard_map/cond/branch_3_fun/ppermute | solution.py:303
  27.8 6.2 %collective-permute-start.76 = (bf16[32,1024]{1,0:T(8,128)(2,1)S(1)}, bf16[32,1024]{1,0:T(8,128)(2,1)S(1)}, u32[]{:S(2)}, u32[]{:S(2)}) collective-permute-start(bf16[32,1024]{1,0:T(8,128)(2,1)S(1)} %get-tuple-element.113), channel_id=1, source_target_pairs={{1,0},{3,2},{6,5},{10,9},{13,12},{14,15},{17,16},{18,19},{21,22},{... | collective-permute-start | bytes 196616 | tf_op jit(solution)/shard_map/cond/branch_3_fun/ppermute | solution.py:303
  29.1 4.9 %collective-permute-start.75 = (bf16[32,1024]{1,0:T(8,128)(2,1)S(1)}, bf16[32,1024]{1,0:T(8,128)(2,1)S(1)}, u32[]{:S(2)}, u32[]{:S(2)}) collective-permute-start(bf16[32,1024]{1,0:T(8,128)(2,1)S(1)} %get-tuple-element.113), channel_id=1, source_target_pairs={{6,2},{11,15},{13,9},{18,22},{20,16},{25,29}} | collective-permute-start | bytes 196616 | tf_op jit(solution)/shard_map/cond/branch_3_fun/ppermute | solution.py:303
  33.9 2.6 %collective-permute-start.80 = (bf16[32,1024]{1,0:T(8,128)(2,1)S(1)}, bf16[32,1024]{1,0:T(8,128)(2,1)S(1)}, u32[]{:S(2)}, u32[]{:S(2)}) collective-permute-start(bf16[32,1024]{1,0:T(8,128)(2,1)S(1)} %get-tuple-element.115), channel_id=1, source_target_pairs={{3,11},{9,1},{10,18},{12,4},{14,6},{15,23},{16,8},{17,25},{19,27},... | collective-permute-start | bytes 196616 | tf_op jit(solution)/shard_map/cond/branch_3_fun/ppermute | solution.py:303
  34.6 2.0 %collective-permute-start.79 = (bf16[32,1024]{1,0:T(8,128)(2,1)S(1)}, bf16[32,1024]{1,0:T(8,128)(2,1)S(1)}, u32[]{:S(2)}, u32[]{:S(2)}) collective-permute-start(bf16[32,1024]{1,0:T(8,128)(2,1)S(1)} %get-tuple-element.115), channel_id=1, source_target_pairs={{2,1},{5,4},{6,7},{9,8},{22,23},{25,24},{26,27},{29,30}} | collective-permute-start | bytes 196616 | tf_op jit(solution)/shard_map/cond/branch_3_fun/ppermute | solution.py:303
  35.3 2.2 %collective-permute-start.78 = (bf16[32,1024]{1,0:T(8,128)(2,1)S(1)}, bf16[32,1024]{1,0:T(8,128)(2,1)S(1)}, u32[]{:S(2)}, u32[]{:S(2)}) collective-permute-start(bf16[32,1024]{1,0:T(8,128)(2,1)S(1)} %get-tuple-element.115), channel_id=1, source_target_pairs={{0,4},{5,1},{8,12},{12,8},{14,10},{17,21},{19,23},{23,19},{26,30},... | collective-permute-start | bytes 196616 | tf_op jit(solution)/shard_map/cond/branch_3_fun/ppermute | solution.py:303
  37.5 10.1 %collective-permute-start.83 = (bf16[16,1024]{1,0:T(8,128)(2,1)S(1)}, bf16[16,1024]{1,0:T(8,128)(2,1)S(1)}, u32[]{:S(2)}, u32[]{:S(2)}) collective-permute-start(bf16[16,1024]{1,0:T(8,128)(2,1)S(1)} %get-tuple-element.117), channel_id=1, source_target_pairs={{3,11},{7,15},{8,0},{23,31},{24,16},{28,20}} | collective-permute-start | bytes 98312 | tf_op jit(solution)/shard_map/cond/branch_3_fun/ppermute | solution.py:303
  38.8 8.9 %collective-permute-start.82 = (bf16[16,1024]{1,0:T(8,128)(2,1)S(1)}, bf16[16,1024]{1,0:T(8,128)(2,1)S(1)}, u32[]{:S(2)}, u32[]{:S(2)}) collective-permute-start(bf16[16,1024]{1,0:T(8,128)(2,1)S(1)} %get-tuple-element.117), channel_id=1, source_target_pairs={{1,0},{2,3},{5,4},{26,27},{29,28},{30,31}} | collective-permute-start | bytes 98312 | tf_op jit(solution)/shard_map/cond/branch_3_fun/ppermute | solution.py:303
  40.1 7.6 %collective-permute-start.81 = (bf16[16,1024]{1,0:T(8,128)(2,1)S(1)}, bf16[16,1024]{1,0:T(8,128)(2,1)S(1)}, u32[]{:S(2)}, u32[]{:S(2)}) collective-permute-start(bf16[16,1024]{1,0:T(8,128)(2,1)S(1)} %get-tuple-element.117), channel_id=1, source_target_pairs={{0,4},{4,0},{9,13},{13,9},{18,22},{22,18},{27,31},{31,27}} | collective-permute-start | bytes 98312 | tf_op jit(solution)/shard_map/cond/branch_3_fun/ppermute | solution.py:303
  48.0 0.6 %copy-start.4 = (bf16[1,1,1,2,16,1024]{5,4,3,2,1,0:T(8,128)(2,1)}, bf16[1,1,1,2,16,1024]{5,4,3,2,1,0:T(8,128)(2,1)S(1)}, u32[]{:S(2)}) copy-start(bf16[1,1,1,2,16,1024]{5,4,3,2,1,0:T(8,128)(2,1)S(1)} %get-tuple-element.308) | copy-start | bytes 196612

commit v4 on v3

--- a/solution.py
+++ b/solution.py
@@ -57,22 +57,22 @@
 
 SHARED = (
     (
-        (0, 1, 2, -1, 3, 4, 5),
-        (6, 7, 8, -2, 9, 10, 5),
-        (6, 8, 7, -3, 10, 9, 5),
-        (0, 11, 1, -3, 4, 3, 6),
-    ),
-    (
-        (0, 1, 2, 3, 4, 5, 0),
-        (6, 5, 7, 8, 1, 6, 3),
-        (3, 6, 1, 0, 7, 5, 9),
-        (1, 5, 10, 9, 2, 1, 0),
+        (0, 1, 2, -1, 3, 4, 3),
+        (5, 6, 7, -2, 8, 9, 8),
+        (5, 7, 6, -3, 9, 8, 9),
+        (0, 2, 1, -4, 4, 3, 4),
     ),
     (
         (0, 1, 2, -1, 3, 4, 5),
-        (0, 6, 7, -2, 8, 9, 5),
-        (6, 7, 10, -3, 9, 8, 11),
-        (0, 2, 1, -4, 4, 11, 5),
+        (4, 6, 7, -2, 8, 0, 5),
+        (5, 0, 9, -3, 10, 6, 0),
+        (6, 4, 11, -3, 2, 12, 4),
+    ),
+    (
+        (0, 1, 2, -1, 3, 4, 3),
+        (5, 6, 7, -2, 8, 9, 8),
+        (6, 5, 10, -3, 9, 8, 9),
+        (1, 0, 11, -2, 4, 3, 4),
     ),
 )
 

time: 49.5 us -> 47.9 us (0.968); the launches traced: 48.7 us -> 48 us
  starting transfers between devices: 30.3 us -> 26.5 us
  waiting for transfers between devices: 13.3 us -> 16.4 us
    ppermute x21, starting transfers between devices: 30.3 us -> 26.5 us  [wave(): came[axis] = lax.ppermute(message, AXES, pairs_of(sizes, bits, axis, hop))]
    ppermute x21, waiting for transfers between devices: 13.3 us -> 16.4 us  [wave(): came[axis] = lax.ppermute(message, AXES, pairs_of(sizes, bits, axis, hop))]
  transfers between devices with their start and end apart: 21 -> 21, of which waited for: 7 -> 6; matrix products, arithmetic and copies ran while one was open for 0% -> 0% of each run, Pallas kernels for 4% -> 4%
where the time goes in v4:
time: 47.9 us; the launch traced here: 48 us
  starting transfers between devices  26.5 us (55%)
  waiting for transfers between devices  16.4 us (34%)
  Pallas kernels  3.45 us (7%)
  between operations  0.67 us (1%)
  local copies, waits for them, and re-layouts  0.65 us (1%)
    ppermute x21, starting transfers between devices, wave(): came[axis] = lax.ppermute(message, AXES, pairs_of(sizes, bits, axis, hop))  26.5 us
    ppermute x21, waiting for transfers between devices, wave(): came[axis] = lax.ppermute(message, AXES, pairs_of(sizes, bits, axis, hop))  16.4 us
    pallas_call x1, Pallas kernels, load_first(): pl.pallas_call(functools.partial(load_first_kernel, sizes, bits), out_sha...  1.85 us
  transfers between devices with their start and end apart: 21, of which 6 were waited for; matrix products, arithmetic and copies ran while one was open for 0% of the time, Pallas kernels for 4%

profile of v4, /device:TPU:0, one launch (start us, length us, event | category | flops | bytes accessed | tf_op | source)
XLA Modules:
  0.0 48.0 jit_solution(9937199010867913254)
XLA Ops:
  0.7 46.7 %conditional.1 = (bf16[1,1,1,2,16,1024]{5,4,3,2,1,0:T(8,128)(2,1)S(1)}) conditional(s32[]{:T(128)} %clamp.3, (s32[]{:T(128)}, f32[1,1,1,2,16,1024]{5,4,3,2,1,0:T(8,128)}, bf16[1,1,1,2,1024,1024]{5,4,3,2,1,0:T(8,128)(2,1)}) %tuple.21, (s32[]{:T(128)}, f32[1,1,1,2,16,1024]{5,4,3,2,1,0:T(8,128)}, ...), branch_computations={%region_0.1_spmd, %region_1.2_spmd, %region_2.3_spmd, %region_3.4_... | conditional | bytes 21496684 | solution.py:354
  0.7 1.0 %begin.7.after_ref = bf16[16,1024]{1,0:T(8,128)(2,1)S(1)} custom-call(s32[1]{0:T(128)} %bitcast.12.lead_hbm.lead_ref, f32[2,16,1024]{2,1,0:T(8,128)} %bitcast.34), custom_call_target="tpu_custom_call" | custom-call | tf_op jit(solution)/shard_map/cond/branch_3_fun/begin/pallas_call | solution.py:150
  1.7 4.0 %collective-permute-start.65 = (bf16[16,1024]{1,0:T(8,128)(2,1)S(1)}, bf16[16,1024]{1,0:T(8,128)(2,1)S(1)}, u32[]{:S(2)}, u32[]{:S(2)}) collective-permute-start(bf16[16,1024]{1,0:T(8,128)(2,1)S(1)} %begin.7.after_ref), channel_id=1, source_target_pairs={{0,8},{4,12},{27,19},{31,23}} | collective-permute-start | bytes 98312 | tf_op jit(solution)/shard_map/cond/branch_3_fun/ppermute | solution.py:303
  5.6 1.3 %collective-permute-start.64 = (bf16[16,1024]{1,0:T(8,128)(2,1)S(1)}, bf16[16,1024]{1,0:T(8,128)(2,1)S(1)}, u32[]{:S(2)}, u32[]{:S(2)}) collective-permute-start(bf16[16,1024]{1,0:T(8,128)(2,1)S(1)} %begin.7.after_ref), channel_id=1, source_target_pairs={{0,1},{5,6},{12,13},{19,18},{26,25},{31,30}} | collective-permute-start | bytes 98312 | tf_op jit(solution)/shard_map/cond/branch_3_fun/ppermute | solution.py:303
  6.9 1.3 %collective-permute-start.63 = (bf16[16,1024]{1,0:T(8,128)(2,1)S(1)}, bf16[16,1024]{1,0:T(8,128)(2,1)S(1)}, u32[]{:S(2)}, u32[]{:S(2)}) collective-permute-start(bf16[16,1024]{1,0:T(8,128)(2,1)S(1)} %begin.7.after_ref), channel_id=1, source_target_pairs={{0,4},{2,6},{11,15},{20,16},{29,25},{31,27}} | collective-permute-start | bytes 98312 | tf_op jit(solution)/shard_map/cond/branch_3_fun/ppermute | solution.py:303
  8.2 0.0 copy-start.3
  8.2 1.9 %load_first.7 = (bf16[1024,1024]{1,0:T(8,128)(2,1)S(1)}, f32[2,16,1024]{2,1,0:T(8,128)S(1)}, bf16[2,16,1024]{2,1,0:T(8,128)(2,1)S(1)}) custom-call(s32[1]{0:T(128)} %bitcast.12.lead_hbm.lead_ref, bf16[2,1024,1024]{2,1,0:T(8,128)(2,1)} %bitcast.26, f32[2,16,1024]{2,1,0:T(8,128)} %bitcast.35, bf16[16,1024]{1,0:T(8,128)(2,1)S(1)} %begin.7.after_ref), custom_call_target="tpu_custom_call" | custom-call | tf_op jit(solution)/shard_map/cond/branch_3_fun/load_first/pallas_call | solution.py:184
  10.1 0.0 collective-permute-done.65.x_ref
  10.1 0.0 collective-permute-done.64.z_ref
  10.1 0.0 collective-permute-done.63.y_ref
  10.2 0.8 %collective-permute-start.68 = (bf16[32,1024]{1,0:T(8,128)(2,1)S(1)}, bf16[32,1024]{1,0:T(8,128)(2,1)S(1)}, u32[]{:S(2)}, u32[]{:S(2)}) collective-permute-start(bf16[32,1024]{1,0:T(8,128)(2,1)S(1)} %get-tuple-element.107.after_ref), channel_id=1, source_target_pairs={{1,9},{4,12},{6,14},{8,16},{11,3},{13,21},{18,10},{20,28},{23,15},... | collective-permute-start | bytes 196616 | tf_op jit(solution)/shard_map/cond/branch_3_fun/ppermute | solution.py:303
  11.0 0.7 %collective-permute-start.67 = (bf16[32,1024]{1,0:T(8,128)(2,1)S(1)}, bf16[32,1024]{1,0:T(8,128)(2,1)S(1)}, u32[]{:S(2)}, u32[]{:S(2)}) collective-permute-start(bf16[32,1024]{1,0:T(8,128)(2,1)S(1)} %get-tuple-element.107.after_ref), channel_id=1, source_target_pairs={{1,2},{4,5},{8,9},{23,22},{27,26},{30,29}} | collective-permute-start | bytes 196616 | tf_op jit(solution)/shard_map/cond/branch_3_fun/ppermute | solution.py:303
  11.6 1.3 %collective-permute-start.66 = (bf16[32,1024]{1,0:T(8,128)(2,1)S(1)}, bf16[32,1024]{1,0:T(8,128)(2,1)S(1)}, u32[]{:S(2)}, u32[]{:S(2)}) collective-permute-start(bf16[32,1024]{1,0:T(8,128)(2,1)S(1)} %get-tuple-element.107.after_ref), channel_id=1, source_target_pairs={{1,5},{3,7},{4,0},{8,12},{23,19},{27,31},{28,24},{30,26}} | collective-permute-start | bytes 196616 | tf_op jit(solution)/shard_map/cond/branch_3_fun/ppermute | solution.py:303
  12.9 0.0 copy-done.3
  12.9 0.2 load_second.7.refs_1_.refs_0_
  13.1 0.0 collective-permute-done.68.x_ref
  13.1 0.0 collective-permute-done.67.z_ref
  13.1 2.0 %collective-permute-done.66.y_ref = bf16[32,1024]{1,0:T(8,128)(2,1)S(1)} collective-permute-done((bf16[32,1024]{1,0:T(8,128)(2,1)S(1)}, bf16[32,1024]{1,0:T(8,128)(2,1)S(1)}, u32[]{:S(2)}, u32[]{:S(2)}) %collective-permute-start.66) | collective-permute-done | bytes 65568 | tf_op jit(solution)/shard_map/cond/branch_3_fun/ppermute | solution.py:303
  15.1 2.1 %collective-permute-start.71 = (bf16[32,1024]{1,0:T(8,128)(2,1)S(1)}, bf16[32,1024]{1,0:T(8,128)(2,1)S(1)}, u32[]{:S(2)}, u32[]{:S(2)}) collective-permute-start(bf16[32,1024]{1,0:T(8,128)(2,1)S(1)} %get-tuple-element.109), channel_id=1, source_target_pairs={{0,8},{2,10},{5,13},{9,17},{12,20},{15,7},{16,24},{19,11},{22,14},... | collective-permute-start | bytes 196616 | tf_op jit(solution)/shard_map/cond/branch_3_fun/ppermute | solution.py:303
  17.2 0.7 %collective-permute-start.70 = (bf16[32,1024]{1,0:T(8,128)(2,1)S(1)}, bf16[32,1024]{1,0:T(8,128)(2,1)S(1)}, u32[]{:S(2)}, u32[]{:S(2)}) collective-permute-start(bf16[32,1024]{1,0:T(8,128)(2,1)S(1)} %get-tuple-element.109), channel_id=1, source_target_pairs={{2,3},{5,6},{9,10},{12,13},{15,14},{16,17},{19,18},{22,21},{26,25}... | collective-permute-start | bytes 196616 | tf_op jit(solution)/shard_map/cond/branch_3_fun/ppermute | solution.py:303
  17.9 0.7 %collective-permute-start.69 = (bf16[32,1024]{1,0:T(8,128)(2,1)S(1)}, bf16[32,1024]{1,0:T(8,128)(2,1)S(1)}, u32[]{:S(2)}, u32[]{:S(2)}) collective-permute-start(bf16[32,1024]{1,0:T(8,128)(2,1)S(1)} %get-tuple-element.109), channel_id=1, source_target_pairs={{2,6},{9,13},{15,11},{16,20},{22,18},{29,25}} | collective-permute-start | bytes 196616 | tf_op jit(solution)/shard_map/cond/branch_3_fun/ppermute | solution.py:303
  18.6 0.5 %collective-permute-done.71.x_ref = bf16[32,1024]{1,0:T(8,128)(2,1)S(1)} collective-permute-done((bf16[32,1024]{1,0:T(8,128)(2,1)S(1)}, bf16[32,1024]{1,0:T(8,128)(2,1)S(1)}, u32[]{:S(2)}, u32[]{:S(2)}) %collective-permute-start.71) | collective-permute-done | bytes 65568 | tf_op jit(solution)/shard_map/cond/branch_3_fun/ppermute | solution.py:303
  19.1 0.0 collective-permute-done.70.z_ref
  19.1 0.0 collective-permute-done.69.y_ref
  19.1 2.4 %collective-permute-start.74 = (bf16[32,1024]{1,0:T(8,128)(2,1)S(1)}, bf16[32,1024]{1,0:T(8,128)(2,1)S(1)}, u32[]{:S(2)}, u32[]{:S(2)}) collective-permute-start(bf16[32,1024]{1,0:T(8,128)(2,1)S(1)} %get-tuple-element.111), channel_id=1, source_target_pairs={{0,8},{1,9},{2,26},{3,11},{4,12},{5,29},{6,14},{7,15},{8,0},{9,1},... | collective-permute-start | bytes 196616 | tf_op jit(solution)/shard_map/cond/branch_3_fun/ppermute | solution.py:303
  21.6 2.3 %collective-permute-start.73 = (bf16[32,1024]{1,0:T(8,128)(2,1)S(1)}, bf16[32,1024]{1,0:T(8,128)(2,1)S(1)}, u32[]{:S(2)}, u32[]{:S(2)}) collective-permute-start(bf16[32,1024]{1,0:T(8,128)(2,1)S(1)} %get-tuple-element.111), channel_id=1, source_target_pairs={{0,1},{1,0},{2,3},{3,2},{4,5},{5,4},{6,7},{7,6},{8,9},{9,8},{10,11... | collective-permute-start | bytes 196616 | tf_op jit(solution)/shard_map/cond/branch_3_fun/ppermute | solution.py:303
  23.8 0.0 collective-permute-start.72
  23.8 0.0 collective-permute-done.74.x_ref
  23.8 2.2 %collective-permute-done.73.z_ref = bf16[32,1024]{1,0:T(8,128)(2,1)S(1)} collective-permute-done((bf16[32,1024]{1,0:T(8,128)(2,1)S(1)}, bf16[32,1024]{1,0:T(8,128)(2,1)S(1)}, u32[]{:S(2)}, u32[]{:S(2)}) %collective-permute-start.73) | collective-permute-done | bytes 65568 | tf_op jit(solution)/shard_map/cond/branch_3_fun/ppermute | solution.py:303
  26.1 0.0 collective-permute-done.72.y_ref
  26.1 1.3 %collective-permute-start.77 = (bf16[32,1024]{1,0:T(8,128)(2,1)S(1)}, bf16[32,1024]{1,0:T(8,128)(2,1)S(1)}, u32[]{:S(2)}, u32[]{:S(2)}) collective-permute-start(bf16[32,1024]{1,0:T(8,128)(2,1)S(1)} %get-tuple-element.113), channel_id=1, source_target_pairs={{7,15},{8,0},{10,2},{11,19},{13,5},{14,22},{17,9},{18,26},{20,12},... | collective-permute-start | bytes 196616 | tf_op jit(solution)/shard_map/cond/branch_3_fun/ppermute | solution.py:303
  27.4 1.3 %collective-permute-start.76 = (bf16[32,1024]{1,0:T(8,128)(2,1)S(1)}, bf16[32,1024]{1,0:T(8,128)(2,1)S(1)}, u32[]{:S(2)}, u32[]{:S(2)}) collective-permute-start(bf16[32,1024]{1,0:T(8,128)(2,1)S(1)} %get-tuple-element.113), channel_id=1, source_target_pairs={{1,0},{3,2},{6,5},{10,9},{13,12},{14,15},{17,16},{18,19},{21,22},{... | collective-permute-start | bytes 196616 | tf_op jit(solution)/shard_map/cond/branch_3_fun/ppermute | solution.py:303
  28.7 0.7 %collective-permute-start.75 = (bf16[32,1024]{1,0:T(8,128)(2,1)S(1)}, bf16[32,1024]{1,0:T(8,128)(2,1)S(1)}, u32[]{:S(2)}, u32[]{:S(2)}) collective-permute-start(bf16[32,1024]{1,0:T(8,128)(2,1)S(1)} %get-tuple-element.113), channel_id=1, source_target_pairs={{6,2},{11,15},{13,9},{18,22},{20,16},{25,29}} | collective-permute-start | bytes 196616 | tf_op jit(solution)/shard_map/cond/branch_3_fun/ppermute | solution.py:303
  29.3 2.9 %collective-permute-done.77.x_ref = bf16[32,1024]{1,0:T(8,128)(2,1)S(1)} collective-permute-done((bf16[32,1024]{1,0:T(8,128)(2,1)S(1)}, bf16[32,1024]{1,0:T(8,128)(2,1)S(1)}, u32[]{:S(2)}, u32[]{:S(2)}) %collective-permute-start.77) | collective-permute-done | bytes 65568 | tf_op jit(solution)/shard_map/cond/branch_3_fun/ppermute | solution.py:303
  32.2 1.3 %collective-permute-done.76.z_ref = bf16[32,1024]{1,0:T(8,128)(2,1)S(1)} collective-permute-done((bf16[32,1024]{1,0:T(8,128)(2,1)S(1)}, bf16[32,1024]{1,0:T(8,128)(2,1)S(1)}, u32[]{:S(2)}, u32[]{:S(2)}) %collective-permute-start.76) | collective-permute-done | bytes 65568 | tf_op jit(solution)/shard_map/cond/branch_3_fun/ppermute | solution.py:303
  33.5 0.0 collective-permute-done.75.y_ref
  33.6 0.7 %collective-permute-start.80 = (bf16[32,1024]{1,0:T(8,128)(2,1)S(1)}, bf16[32,1024]{1,0:T(8,128)(2,1)S(1)}, u32[]{:S(2)}, u32[]{:S(2)}) collective-permute-start(bf16[32,1024]{1,0:T(8,128)(2,1)S(1)} %get-tuple-element.115), channel_id=1, source_target_pairs={{3,11},{9,1},{10,18},{12,4},{14,6},{15,23},{16,8},{17,25},{19,27},... | collective-permute-start | bytes 196616 | tf_op jit(solution)/shard_map/cond/branch_3_fun/ppermute | solution.py:303
  34.2 0.7 %collective-permute-start.79 = (bf16[32,1024]{1,0:T(8,128)(2,1)S(1)}, bf16[32,1024]{1,0:T(8,128)(2,1)S(1)}, u32[]{:S(2)}, u32[]{:S(2)}) collective-permute-start(bf16[32,1024]{1,0:T(8,128)(2,1)S(1)} %get-tuple-element.115), channel_id=1, source_target_pairs={{2,1},{5,4},{7,6},{9,8},{10,11},{14,13},{17,18},{21,20},{22,23},{2... | collective-permute-start | bytes 196616 | tf_op jit(solution)/shard_map/cond/branch_3_fun/ppermute | solution.py:303
  34.9 0.7 %collective-permute-start.78 = (bf16[32,1024]{1,0:T(8,128)(2,1)S(1)}, bf16[32,1024]{1,0:T(8,128)(2,1)S(1)}, u32[]{:S(2)}, u32[]{:S(2)}) collective-permute-start(bf16[32,1024]{1,0:T(8,128)(2,1)S(1)} %get-tuple-element.115), channel_id=1, source_target_pairs={{5,1},{12,8},{19,23},{26,30}} | collective-permute-start | bytes 196616 | tf_op jit(solution)/shard_map/cond/branch_3_fun/ppermute | solution.py:303
  35.6 0.0 collective-permute-done.80.x_ref
  35.6 0.0 collective-permute-done.79.z_ref
  35.6 0.0 collective-permute-done.78.y_ref
  35.6 1.3 %collective-permute-start.83 = (bf16[16,1024]{1,0:T(8,128)(2,1)S(1)}, bf16[16,1024]{1,0:T(8,128)(2,1)S(1)}, u32[]{:S(2)}, u32[]{:S(2)}) collective-permute-start(bf16[16,1024]{1,0:T(8,128)(2,1)S(1)} %get-tuple-element.117), channel_id=1, source_target_pairs={{7,15},{8,0},{10,2},{11,19},{13,5},{14,22},{17,9},{18,26},{20,12},... | collective-permute-start | bytes 98312 | tf_op jit(solution)/shard_map/cond/branch_3_fun/ppermute | solution.py:303
  36.9 1.3 %collective-permute-start.82 = (bf16[16,1024]{1,0:T(8,128)(2,1)S(1)}, bf16[16,1024]{1,0:T(8,128)(2,1)S(1)}, u32[]{:S(2)}, u32[]{:S(2)}) collective-permute-start(bf16[16,1024]{1,0:T(8,128)(2,1)S(1)} %get-tuple-element.117), channel_id=1, source_target_pairs={{1,0},{3,2},{6,5},{10,9},{13,12},{14,15},{17,16},{18,19},{21,22},{... | collective-permute-start | bytes 98312 | tf_op jit(solution)/shard_map/cond/branch_3_fun/ppermute | solution.py:303
  38.2 1.3 %collective-permute-start.81 = (bf16[16,1024]{1,0:T(8,128)(2,1)S(1)}, bf16[16,1024]{1,0:T(8,128)(2,1)S(1)}, u32[]{:S(2)}, u32[]{:S(2)}) collective-permute-start(bf16[16,1024]{1,0:T(8,128)(2,1)S(1)} %get-tuple-element.117), channel_id=1, source_target_pairs={{1,5},{3,7},{4,0},{8,12},{23,19},{27,31},{28,24},{30,26}} | collective-permute-start | bytes 98312 | tf_op jit(solution)/shard_map/cond/branch_3_fun/ppermute | solution.py:303
  39.5 7.4 %collective-permute-done.83.x_ref = bf16[16,1024]{1,0:T(8,128)(2,1)S(1)} collective-permute-done((bf16[16,1024]{1,0:T(8,128)(2,1)S(1)}, bf16[16,1024]{1,0:T(8,128)(2,1)S(1)}, u32[]{:S(2)}, u32[]{:S(2)}) %collective-permute-start.83) | collective-permute-done | bytes 32800 | tf_op jit(solution)/shard_map/cond/branch_3_fun/ppermute | solution.py:303
  46.9 0.0 collective-permute-done.82.z_ref
  47.0 0.0 collective-permute-done.81.y_ref
  47.0 0.4 hop7.7
  47.4 0.0 copy-start.4
  47.4 0.6 %copy-done.4 = bf16[1,1,1,2,16,1024]{5,4,3,2,1,0:T(8,128)(2,1)} copy-done((bf16[1,1,1,2,16,1024]{5,4,3,2,1,0:T(8,128)(2,1)}, bf16[1,1,1,2,16,1024]{5,4,3,2,1,0:T(8,128)(2,1)S(1)}, u32[]{:S(2)}) %copy-start.4) | copy-done | bytes 65560
  (6 shorter events, 0.1 us)
Async XLA Ops:
  1.7 8.4 %collective-permute-start.65 = (bf16[16,1024]{1,0:T(8,128)(2,1)S(1)}, bf16[16,1024]{1,0:T(8,128)(2,1)S(1)}, u32[]{:S(2)}, u32[]{:S(2)}) collective-permute-start(bf16[16,1024]{1,0:T(8,128)(2,1)S(1)} %begin.7.after_ref), channel_id=1, source_target_pairs={{0,8},{4,12},{27,19},{31,23}} | collective-permute-start | bytes 98312 | tf_op jit(solution)/shard_map/cond/branch_3_fun/ppermute | solution.py:303
  5.6 4.5 %collective-permute-start.64 = (bf16[16,1024]{1,0:T(8,128)(2,1)S(1)}, bf16[16,1024]{1,0:T(8,128)(2,1)S(1)}, u32[]{:S(2)}, u32[]{:S(2)}) collective-permute-start(bf16[16,1024]{1,0:T(8,128)(2,1)S(1)} %begin.7.after_ref), channel_id=1, source_target_pairs={{0,1},{5,6},{12,13},{19,18},{26,25},{31,30}} | collective-permute-start | bytes 98312 | tf_op jit(solution)/shard_map/cond/branch_3_fun/ppermute | solution.py:303
  6.9 3.2 %collective-permute-start.63 = (bf16[16,1024]{1,0:T(8,128)(2,1)S(1)}, bf16[16,1024]{1,0:T(8,128)(2,1)S(1)}, u32[]{:S(2)}, u32[]{:S(2)}) collective-permute-start(bf16[16,1024]{1,0:T(8,128)(2,1)S(1)} %begin.7.after_ref), channel_id=1, source_target_pairs={{0,4},{2,6},{11,15},{20,16},{29,25},{31,27}} | collective-permute-start | bytes 98312 | tf_op jit(solution)/shard_map/cond/branch_3_fun/ppermute | solution.py:303
  8.2 4.7 %copy-start.3 = (bf16[1,1,1,2,1024,1024]{5,4,3,2,1,0:T(8,128)(2,1)S(1)}, bf16[1,1,1,2,1024,1024]{5,4,3,2,1,0:T(8,128)(2,1)}, u32[]{:S(2)}) copy-start(bf16[1,1,1,2,1024,1024]{5,4,3,2,1,0:T(8,128)(2,1)} %get-tuple-element.135) | copy-start | bytes 12582916 | tf_op jit(solution)/shard_map/cond
  10.2 3.0 %collective-permute-start.68 = (bf16[32,1024]{1,0:T(8,128)(2,1)S(1)}, bf16[32,1024]{1,0:T(8,128)(2,1)S(1)}, u32[]{:S(2)}, u32[]{:S(2)}) collective-permute-start(bf16[32,1024]{1,0:T(8,128)(2,1)S(1)} %get-tuple-element.107.after_ref), channel_id=1, source_target_pairs={{1,9},{4,12},{6,14},{8,16},{11,3},{13,21},{18,10},{20,28},{23,15},... | collective-permute-start | bytes 196616 | tf_op jit(solution)/shard_map/cond/branch_3_fun/ppermute | solution.py:303
  11.0 2.2 %collective-permute-start.67 = (bf16[32,1024]{1,0:T(8,128)(2,1)S(1)}, bf16[32,1024]{1,0:T(8,128)(2,1)S(1)}, u32[]{:S(2)}, u32[]{:S(2)}) collective-permute-start(bf16[32,1024]{1,0:T(8,128)(2,1)S(1)} %get-tuple-element.107.after_ref), channel_id=1, source_target_pairs={{1,2},{4,5},{8,9},{23,22},{27,26},{30,29}} | collective-permute-start | bytes 196616 | tf_op jit(solution)/shard_map/cond/branch_3_fun/ppermute | solution.py:303
  11.6 3.5 %collective-permute-start.66 = (bf16[32,1024]{1,0:T(8,128)(2,1)S(1)}, bf16[32,1024]{1,0:T(8,128)(2,1)S(1)}, u32[]{:S(2)}, u32[]{:S(2)}) collective-permute-start(bf16[32,1024]{1,0:T(8,128)(2,1)S(1)} %get-tuple-element.107.after_ref), channel_id=1, source_target_pairs={{1,5},{3,7},{4,0},{8,12},{23,19},{27,31},{28,24},{30,26}} | collective-permute-start | bytes 196616 | tf_op jit(solution)/shard_map/cond/branch_3_fun/ppermute | solution.py:303
  15.1 4.0 %collective-permute-start.71 = (bf16[32,1024]{1,0:T(8,128)(2,1)S(1)}, bf16[32,1024]{1,0:T(8,128)(2,1)S(1)}, u32[]{:S(2)}, u32[]{:S(2)}) collective-permute-start(bf16[32,1024]{1,0:T(8,128)(2,1)S(1)} %get-tuple-element.109), channel_id=1, source_target_pairs={{0,8},{2,10},{5,13},{9,17},{12,20},{15,7},{16,24},{19,11},{22,14},... | collective-permute-start | bytes 196616 | tf_op jit(solution)/shard_map/cond/branch_3_fun/ppermute | solution.py:303
  17.2 1.9 %collective-permute-start.70 = (bf16[32,1024]{1,0:T(8,128)(2,1)S(1)}, bf16[32,1024]{1,0:T(8,128)(2,1)S(1)}, u32[]{:S(2)}, u32[]{:S(2)}) collective-permute-start(bf16[32,1024]{1,0:T(8,128)(2,1)S(1)} %get-tuple-element.109), channel_id=1, source_target_pairs={{2,3},{5,6},{9,10},{12,13},{15,14},{16,17},{19,18},{22,21},{26,25}... | collective-permute-start | bytes 196616 | tf_op jit(solution)/shard_map/cond/branch_3_fun/ppermute | solution.py:303
  17.9 1.2 %collective-permute-start.69 = (bf16[32,1024]{1,0:T(8,128)(2,1)S(1)}, bf16[32,1024]{1,0:T(8,128)(2,1)S(1)}, u32[]{:S(2)}, u32[]{:S(2)}) collective-permute-start(bf16[32,1024]{1,0:T(8,128)(2,1)S(1)} %get-tuple-element.109), channel_id=1, source_target_pairs={{2,6},{9,13},{15,11},{16,20},{22,18},{29,25}} | collective-permute-start | bytes 196616 | tf_op jit(solution)/shard_map/cond/branch_3_fun/ppermute | solution.py:303
  19.1 4.7 %collective-permute-start.74 = (bf16[32,1024]{1,0:T(8,128)(2,1)S(1)}, bf16[32,1024]{1,0:T(8,128)(2,1)S(1)}, u32[]{:S(2)}, u32[]{:S(2)}) collective-permute-start(bf16[32,1024]{1,0:T(8,128)(2,1)S(1)} %get-tuple-element.111), channel_id=1, source_target_pairs={{0,8},{1,9},{2,26},{3,11},{4,12},{5,29},{6,14},{7,15},{8,0},{9,1},... | collective-permute-start | bytes 196616 | tf_op jit(solution)/shard_map/cond/branch_3_fun/ppermute | solution.py:303
  21.6 4.5 %collective-permute-start.73 = (bf16[32,1024]{1,0:T(8,128)(2,1)S(1)}, bf16[32,1024]{1,0:T(8,128)(2,1)S(1)}, u32[]{:S(2)}, u32[]{:S(2)}) collective-permute-start(bf16[32,1024]{1,0:T(8,128)(2,1)S(1)} %get-tuple-element.111), channel_id=1, source_target_pairs={{0,1},{1,0},{2,3},{3,2},{4,5},{5,4},{6,7},{7,6},{8,9},{9,8},{10,11... | collective-permute-start | bytes 196616 | tf_op jit(solution)/shard_map/cond/branch_3_fun/ppermute | solution.py:303
  23.8 2.2 %collective-permute-start.72 = (bf16[32,1024]{1,0:T(8,128)(2,1)S(1)}, bf16[32,1024]{1,0:T(8,128)(2,1)S(1)}, u32[]{:S(2)}, u32[]{:S(2)}) collective-permute-start(bf16[32,1024]{1,0:T(8,128)(2,1)S(1)} %get-tuple-element.111), channel_id=1, source_target_pairs={{0,4},{1,5},{2,6},{3,7},{4,0},{5,1},{6,2},{7,3},{8,12},{9,13},{10,... | collective-permute-start | bytes 196616 | tf_op jit(solution)/shard_map/cond/branch_3_fun/ppermute | solution.py:303
  26.1 6.2 %collective-permute-start.77 = (bf16[32,1024]{1,0:T(8,128)(2,1)S(1)}, bf16[32,1024]{1,0:T(8,128)(2,1)S(1)}, u32[]{:S(2)}, u32[]{:S(2)}) collective-permute-start(bf16[32,1024]{1,0:T(8,128)(2,1)S(1)} %get-tuple-element.113), channel_id=1, source_target_pairs={{7,15},{8,0},{10,2},{11,19},{13,5},{14,22},{17,9},{18,26},{20,12},... | collective-permute-start | bytes 196616 | tf_op jit(solution)/shard_map/cond/branch_3_fun/ppermute | solution.py:303
  27.4 6.2 %collective-permute-start.76 = (bf16[32,1024]{1,0:T(8,128)(2,1)S(1)}, bf16[32,1024]{1,0:T(8,128)(2,1)S(1)}, u32[]{:S(2)}, u32[]{:S(2)}) collective-permute-start(bf16[32,1024]{1,0:T(8,128)(2,1)S(1)} %get-tuple-element.113), channel_id=1, source_target_pairs={{1,0},{3,2},{6,5},{10,9},{13,12},{14,15},{17,16},{18,19},{21,22},{... | collective-permute-start | bytes 196616 | tf_op jit(solution)/shard_map/cond/branch_3_fun/ppermute | solution.py:303
  28.7 4.9 %collective-permute-start.75 = (bf16[32,1024]{1,0:T(8,128)(2,1)S(1)}, bf16[32,1024]{1,0:T(8,128)(2,1)S(1)}, u32[]{:S(2)}, u32[]{:S(2)}) collective-permute-start(bf16[32,1024]{1,0:T(8,128)(2,1)S(1)} %get-tuple-element.113), channel_id=1, source_target_pairs={{6,2},{11,15},{13,9},{18,22},{20,16},{25,29}} | collective-permute-start | bytes 196616 | tf_op jit(solution)/shard_map/cond/branch_3_fun/ppermute | solution.py:303
  33.6 2.0 %collective-permute-start.80 = (bf16[32,1024]{1,0:T(8,128)(2,1)S(1)}, bf16[32,1024]{1,0:T(8,128)(2,1)S(1)}, u32[]{:S(2)}, u32[]{:S(2)}) collective-permute-start(bf16[32,1024]{1,0:T(8,128)(2,1)S(1)} %get-tuple-element.115), channel_id=1, source_target_pairs={{3,11},{9,1},{10,18},{12,4},{14,6},{15,23},{16,8},{17,25},{19,27},... | collective-permute-start | bytes 196616 | tf_op jit(solution)/shard_map/cond/branch_3_fun/ppermute | solution.py:303
  34.2 1.4 %collective-permute-start.79 = (bf16[32,1024]{1,0:T(8,128)(2,1)S(1)}, bf16[32,1024]{1,0:T(8,128)(2,1)S(1)}, u32[]{:S(2)}, u32[]{:S(2)}) collective-permute-start(bf16[32,1024]{1,0:T(8,128)(2,1)S(1)} %get-tuple-element.115), channel_id=1, source_target_pairs={{2,1},{5,4},{7,6},{9,8},{10,11},{14,13},{17,18},{21,20},{22,23},{2... | collective-permute-start | bytes 196616 | tf_op jit(solution)/shard_map/cond/branch_3_fun/ppermute | solution.py:303
  34.9 0.7 %collective-permute-start.78 = (bf16[32,1024]{1,0:T(8,128)(2,1)S(1)}, bf16[32,1024]{1,0:T(8,128)(2,1)S(1)}, u32[]{:S(2)}, u32[]{:S(2)}) collective-permute-start(bf16[32,1024]{1,0:T(8,128)(2,1)S(1)} %get-tuple-element.115), channel_id=1, source_target_pairs={{5,1},{12,8},{19,23},{26,30}} | collective-permute-start | bytes 196616 | tf_op jit(solution)/shard_map/cond/branch_3_fun/ppermute | solution.py:303
  35.6 11.3 %collective-permute-start.83 = (bf16[16,1024]{1,0:T(8,128)(2,1)S(1)}, bf16[16,1024]{1,0:T(8,128)(2,1)S(1)}, u32[]{:S(2)}, u32[]{:S(2)}) collective-permute-start(bf16[16,1024]{1,0:T(8,128)(2,1)S(1)} %get-tuple-element.117), channel_id=1, source_target_pairs={{7,15},{8,0},{10,2},{11,19},{13,5},{14,22},{17,9},{18,26},{20,12},... | collective-permute-start | bytes 98312 | tf_op jit(solution)/shard_map/cond/branch_3_fun/ppermute | solution.py:303
  36.9 10.0 %collective-permute-start.82 = (bf16[16,1024]{1,0:T(8,128)(2,1)S(1)}, bf16[16,1024]{1,0:T(8,128)(2,1)S(1)}, u32[]{:S(2)}, u32[]{:S(2)}) collective-permute-start(bf16[16,1024]{1,0:T(8,128)(2,1)S(1)} %get-tuple-element.117), channel_id=1, source_target_pairs={{1,0},{3,2},{6,5},{10,9},{13,12},{14,15},{17,16},{18,19},{21,22},{... | collective-permute-start | bytes 98312 | tf_op jit(solution)/shard_map/cond/branch_3_fun/ppermute | solution.py:303
  38.2 8.7 %collective-permute-start.81 = (bf16[16,1024]{1,0:T(8,128)(2,1)S(1)}, bf16[16,1024]{1,0:T(8,128)(2,1)S(1)}, u32[]{:S(2)}, u32[]{:S(2)}) collective-permute-start(bf16[16,1024]{1,0:T(8,128)(2,1)S(1)} %get-tuple-element.117), channel_id=1, source_target_pairs={{1,5},{3,7},{4,0},{8,12},{23,19},{27,31},{28,24},{30,26}} | collective-permute-start | bytes 98312 | tf_op jit(solution)/shard_map/cond/branch_3_fun/ppermute | solution.py:303
  47.4 0.6 %copy-start.4 = (bf16[1,1,1,2,16,1024]{5,4,3,2,1,0:T(8,128)(2,1)}, bf16[1,1,1,2,16,1024]{5,4,3,2,1,0:T(8,128)(2,1)S(1)}, u32[]{:S(2)}) copy-start(bf16[1,1,1,2,16,1024]{5,4,3,2,1,0:T(8,128)(2,1)S(1)} %get-tuple-element.308) | copy-start | bytes 196612

commit v5 on v4

--- a/solution.py
+++ b/solution.py
@@ -227,17 +227,21 @@
     deepest = sum(size - 1 for size in sizes)
     depth = my_depth(sizes, bits)
     last = hop == deepest
+    if last:
+        *refs, out_ref, kept_ref, sent = refs
+        slots = slots_by_arrival(sizes, bits, lead_ref[0])
+        early = pltpu.make_async_copy(old_ref.at[0], out_ref.at[slots[0]], sent.at[0])
+        early.start()
+        refs = [*refs, kept_ref]
     results = refs[-1:] if last else refs[-2:]
     map_ref = refs[0]
     traces_ref = results[-1]
     rows = sources_ref.shape[1]
     turn = 0 if 2 * hop < deepest else 1
-
-    def place_of(turn):
-        return slots_by_arrival(sizes, bits, lead_ref[0])[turn] if last else turn
+    assert turn == 1 or not last
 
     for kept in range(2):
-        traces_ref[place_of(kept)] = old_ref[kept]
+        traces_ref[kept] = old_ref[kept]
 
     @pl.when((depth == hop) | (depth == deepest - hop))
     def _():
@@ -266,7 +270,13 @@
                 at = kept.index(chain) * rows
                 results[0][at : at + rows] = new
             if chain == max(0, hop - STEPS):
-                traces_ref[place_of(turn)] = new
+                traces_ref[turn] = new
+
+    if last:
+        late = pltpu.make_async_copy(kept_ref.at[1], out_ref.at[slots[1]], sent.at[1])
+        late.start()
+        early.wait()
+        late.wait()
 
 
 def take_hop(hop, sizes, bits, lead, came, maps, sources, traces):
@@ -275,7 +285,7 @@
     vmem = pl.BlockSpec(memory_space=pltpu.VMEM)
     held = [came[axis] for axis in reversed(ORDER)] + [sources, traces] + maps
     held = [pltpu.with_memory_space_constraint(a, pltpu.VMEM) for a in held]
-    shapes = (jax.ShapeDtypeStruct(traces.shape, traces.dtype),)
+    shapes = (pltpu.HBM(traces.shape, traces.dtype),)
     if not last:
         message = (len(chains_sent(hop + 1, deepest)) * sources.shape[1], sources.shape[2])
         shapes = (
@@ -286,7 +296,11 @@
         functools.partial(hop_kernel, hop, sizes, bits),
         out_shape=shapes,
         in_specs=[pl.BlockSpec(memory_space=pltpu.SMEM if last else pl.ANY)] + [vmem] * len(held),
-        out_specs=(vmem,) * len(shapes),
+        out_specs=(pl.BlockSpec(memory_space=pl.ANY),) if last else (vmem,) * len(shapes),
+        scratch_shapes=[
+            pltpu.VMEM(traces.shape, traces.dtype),
+            pltpu.SemaphoreType.DMA((2,)),
+        ] if last else [],
         compiler_params=ROOM,
         name=f"hop{hop}",
     )(lead, *held)

time: 47.9 us -> 47.5 us (level)
  the two profiles are of different devices: /device:TPU:0 before, /device:TPU:2 now
where the time goes in v5:
time: 47.5 us; the launch traced here: 47.2 us
  starting transfers between devices  25 us (53%)
  waiting for transfers between devices  17.5 us (37%)
  Pallas kernels  3.7 us (8%)
  between operations  0.66 us (1%)
    ppermute x21, starting transfers between devices, wave(): came[axis] = lax.ppermute(message, AXES, pairs_of(sizes, bits, axis, hop))  25 us
    ppermute x21, waiting for transfers between devices, wave(): came[axis] = lax.ppermute(message, AXES, pairs_of(sizes, bits, axis, hop))  17.5 us
    pallas_call x1, Pallas kernels, load_first(): pl.pallas_call(functools.partial(load_first_kernel, sizes, bits), out_sha...  1.85 us
    pallas_call x7, Pallas kernels, take_hop(): pl.pallas_call(functools.partial(hop_kernel, hop, sizes, bits), out_shape...  1.64 us
  transfers between devices with their start and end apart: 21, of which 9 were waited for; matrix products, arithmetic and copies ran while one was open for 0% of the time, Pallas kernels for 4%

profile of v5, /device:TPU:2, one launch (start us, length us, event | category | flops | bytes accessed | tf_op | source)
XLA Modules:
  0.0 47.2 jit_solution(15671560257040918915)
XLA Ops:
  0.7 46.5 %conditional.1 = (bf16[1,1,1,2,16,1024]{5,4,3,2,1,0:T(8,128)(2,1)}) conditional(s32[]{:T(128)} %clamp.3, (s32[]{:T(128)}, f32[1,1,1,2,16,1024]{5,4,3,2,1,0:T(8,128)}, bf16[1,1,1,2,1024,1024]{5,4,3,2,1,0:T(8,128)(2,1)}) %tuple.21, (s32[]{:T(128)}, f32[1,1,1,2,16,1024]{5,4,3,2,1,0:T(8,128)}, ...), branch_computations={%region_0.1_spmd, %region_1.2_spmd, %region_2.3_spmd, %region_3.4_... | conditional | bytes 21496684 | solution.py:368
  0.7 1.3 %collective-permute-start.2 = (bf16[16,1024]{1,0:T(8,128)(2,1)S(1)}, bf16[16,1024]{1,0:T(8,128)(2,1)S(1)}, u32[]{:S(2)}, u32[]{:S(2)}) collective-permute-start(bf16[16,1024]{1,0:T(8,128)(2,1)S(1)} %begin.4.after_ref), channel_id=1, source_target_pairs={{0,8},{4,12},{27,19},{31,23}} | collective-permute-start | bytes 98312 | tf_op jit(solution)/shard_map/cond/branch_0_fun/ppermute | solution.py:317
  2.0 2.9 %collective-permute-start.1 = (bf16[16,1024]{1,0:T(8,128)(2,1)S(1)}, bf16[16,1024]{1,0:T(8,128)(2,1)S(1)}, u32[]{:S(2)}, u32[]{:S(2)}) collective-permute-start(bf16[16,1024]{1,0:T(8,128)(2,1)S(1)} %begin.4.after_ref), channel_id=1, source_target_pairs={{1,2},{4,5},{8,9},{23,22},{27,26},{30,29}} | collective-permute-start | bytes 98312 | tf_op jit(solution)/shard_map/cond/branch_0_fun/ppermute | solution.py:317
  4.9 0.7 %collective-permute-start = (bf16[16,1024]{1,0:T(8,128)(2,1)S(1)}, bf16[16,1024]{1,0:T(8,128)(2,1)S(1)}, u32[]{:S(2)}, u32[]{:S(2)}) collective-permute-start(bf16[16,1024]{1,0:T(8,128)(2,1)S(1)} %begin.4.after_ref), channel_id=1, source_target_pairs={{3,7},{4,0},{6,2},{15,11},{16,20},{25,29},{27,31},{28,24}} | collective-permute-start | bytes 98312 | tf_op jit(solution)/shard_map/cond/branch_0_fun/ppermute | solution.py:317
  5.6 0.0 copy-start
  5.6 1.9 %load_first.4 = (bf16[1024,1024]{1,0:T(8,128)(2,1)S(1)}, f32[2,16,1024]{2,1,0:T(8,128)S(1)}, bf16[2,16,1024]{2,1,0:T(8,128)(2,1)S(1)}) custom-call(s32[1]{0:T(128)} %bitcast.lead_hbm.lead_ref, bf16[2,1024,1024]{2,1,0:T(8,128)(2,1)} %bitcast.20, f32[2,16,1024]{2,1,0:T(8,128)} %bitcast.29, bf16[16,1024]{1,0:T(8,128)(2,1)S(1)} %begin.4.after_ref), custom_call_target="tpu_custom_call" | custom-call | tf_op jit(solution)/shard_map/cond/branch_0_fun/load_first/pallas_call | solution.py:184
  7.4 0.0 collective-permute-done.2.x_ref
  7.4 0.0 collective-permute-done.1.z_ref
  7.5 0.0 collective-permute-done.y_ref
  7.5 1.4 %collective-permute-start.5 = (bf16[32,1024]{1,0:T(8,128)(2,1)S(1)}, bf16[32,1024]{1,0:T(8,128)(2,1)S(1)}, u32[]{:S(2)}, u32[]{:S(2)}) collective-permute-start(bf16[32,1024]{1,0:T(8,128)(2,1)S(1)} %get-tuple-element.53.after_ref), channel_id=1, source_target_pairs={{0,8},{2,10},{5,13},{9,17},{12,20},{15,7},{16,24},{19,11},{22,14},... | collective-permute-start | bytes 196616 | tf_op jit(solution)/shard_map/cond/branch_0_fun/ppermute | solution.py:317
  8.9 0.7 %collective-permute-start.4 = (bf16[32,1024]{1,0:T(8,128)(2,1)S(1)}, bf16[32,1024]{1,0:T(8,128)(2,1)S(1)}, u32[]{:S(2)}, u32[]{:S(2)}) collective-permute-start(bf16[32,1024]{1,0:T(8,128)(2,1)S(1)} %get-tuple-element.53.after_ref), channel_id=1, source_target_pairs={{0,1},{5,6},{12,13},{19,18},{26,25},{31,30}} | collective-permute-start | bytes 196616 | tf_op jit(solution)/shard_map/cond/branch_0_fun/ppermute | solution.py:317
  9.6 1.3 %collective-permute-start.3 = (bf16[32,1024]{1,0:T(8,128)(2,1)S(1)}, bf16[32,1024]{1,0:T(8,128)(2,1)S(1)}, u32[]{:S(2)}, u32[]{:S(2)}) collective-permute-start(bf16[32,1024]{1,0:T(8,128)(2,1)S(1)} %get-tuple-element.53.after_ref), channel_id=1, source_target_pairs={{5,1},{12,8},{19,23},{26,30}} | collective-permute-start | bytes 196616 | tf_op jit(solution)/shard_map/cond/branch_0_fun/ppermute | solution.py:317
  10.9 0.0 copy-done
  10.9 0.2 load_second.4.refs_1_.refs_0_
  11.1 2.7 %collective-permute-done.5.x_ref = bf16[32,1024]{1,0:T(8,128)(2,1)S(1)} collective-permute-done((bf16[32,1024]{1,0:T(8,128)(2,1)S(1)}, bf16[32,1024]{1,0:T(8,128)(2,1)S(1)}, u32[]{:S(2)}, u32[]{:S(2)}) %collective-permute-start.5) | collective-permute-done | bytes 65568 | tf_op jit(solution)/shard_map/cond/branch_0_fun/ppermute | solution.py:317
  13.8 0.0 collective-permute-done.4.z_ref
  13.8 0.0 collective-permute-done.3.y_ref
  13.8 0.5 hop2.4
  14.3 1.3 %collective-permute-start.8 = (bf16[32,1024]{1,0:T(8,128)(2,1)S(1)}, bf16[32,1024]{1,0:T(8,128)(2,1)S(1)}, u32[]{:S(2)}, u32[]{:S(2)}) collective-permute-start(bf16[32,1024]{1,0:T(8,128)(2,1)S(1)} %get-tuple-element.55), channel_id=1, source_target_pairs={{1,9},{4,12},{6,14},{8,16},{11,3},{13,21},{18,10},{20,28},{23,15},... | collective-permute-start | bytes 196616 | tf_op jit(solution)/shard_map/cond/branch_0_fun/ppermute | solution.py:317
  15.6 1.3 %collective-permute-start.7 = (bf16[32,1024]{1,0:T(8,128)(2,1)S(1)}, bf16[32,1024]{1,0:T(8,128)(2,1)S(1)}, u32[]{:S(2)}, u32[]{:S(2)}) collective-permute-start(bf16[32,1024]{1,0:T(8,128)(2,1)S(1)} %get-tuple-element.55), channel_id=1, source_target_pairs={{1,2},{6,7},{8,9},{11,10},{13,14},{18,17},{20,21},{23,22},{25,24},... | collective-permute-start | bytes 196616 | tf_op jit(solution)/shard_map/cond/branch_0_fun/ppermute | solution.py:317
  16.9 0.7 %collective-permute-start.6 = (bf16[32,1024]{1,0:T(8,128)(2,1)S(1)}, bf16[32,1024]{1,0:T(8,128)(2,1)S(1)}, u32[]{:S(2)}, u32[]{:S(2)}) collective-permute-start(bf16[32,1024]{1,0:T(8,128)(2,1)S(1)} %get-tuple-element.55), channel_id=1, source_target_pairs={{6,2},{11,15},{13,9},{18,22},{20,16},{25,29}} | collective-permute-start | bytes 196616 | tf_op jit(solution)/shard_map/cond/branch_0_fun/ppermute | solution.py:317
  17.5 0.0 collective-permute-done.8.x_ref
  17.5 1.2 %collective-permute-done.7.z_ref = bf16[32,1024]{1,0:T(8,128)(2,1)S(1)} collective-permute-done((bf16[32,1024]{1,0:T(8,128)(2,1)S(1)}, bf16[32,1024]{1,0:T(8,128)(2,1)S(1)}, u32[]{:S(2)}, u32[]{:S(2)}) %collective-permute-start.7) | collective-permute-done | bytes 65568 | tf_op jit(solution)/shard_map/cond/branch_0_fun/ppermute | solution.py:317
  18.8 0.0 collective-permute-done.6.y_ref
  18.8 0.1 collective-permute-start.11
  18.8 3.8 %collective-permute-start.10 = (bf16[32,1024]{1,0:T(8,128)(2,1)S(1)}, bf16[32,1024]{1,0:T(8,128)(2,1)S(1)}, u32[]{:S(2)}, u32[]{:S(2)}) collective-permute-start(bf16[32,1024]{1,0:T(8,128)(2,1)S(1)} %get-tuple-element.57), channel_id=1, source_target_pairs={{0,1},{1,0},{2,3},{3,2},{4,5},{5,4},{6,7},{7,6},{8,11},{9,10},{10,... | collective-permute-start | bytes 196616 | tf_op jit(solution)/shard_map/cond/branch_0_fun/ppermute | solution.py:317
  22.6 0.0 collective-permute-start.9
  22.6 0.5 %collective-permute-done.11.x_ref = bf16[32,1024]{1,0:T(8,128)(2,1)S(1)} collective-permute-done((bf16[32,1024]{1,0:T(8,128)(2,1)S(1)}, bf16[32,1024]{1,0:T(8,128)(2,1)S(1)}, u32[]{:S(2)}, u32[]{:S(2)}) %collective-permute-start.11) | collective-permute-done | bytes 65568 | tf_op jit(solution)/shard_map/cond/branch_0_fun/ppermute | solution.py:317
  23.1 1.9 %collective-permute-done.10.z_ref = bf16[32,1024]{1,0:T(8,128)(2,1)S(1)} collective-permute-done((bf16[32,1024]{1,0:T(8,128)(2,1)S(1)}, bf16[32,1024]{1,0:T(8,128)(2,1)S(1)}, u32[]{:S(2)}, u32[]{:S(2)}) %collective-permute-start.10) | collective-permute-done | bytes 65568 | tf_op jit(solution)/shard_map/cond/branch_0_fun/ppermute | solution.py:317
  25.0 0.0 collective-permute-done.9.y_ref
  25.0 1.3 %collective-permute-start.14 = (bf16[32,1024]{1,0:T(8,128)(2,1)S(1)}, bf16[32,1024]{1,0:T(8,128)(2,1)S(1)}, u32[]{:S(2)}, u32[]{:S(2)}) collective-permute-start(bf16[32,1024]{1,0:T(8,128)(2,1)S(1)} %get-tuple-element.59), channel_id=1, source_target_pairs={{3,11},{9,1},{10,18},{12,4},{14,6},{15,23},{16,8},{17,25},{19,27},... | collective-permute-start | bytes 196616 | tf_op jit(solution)/shard_map/cond/branch_0_fun/ppermute | solution.py:317
  26.3 1.3 %collective-permute-start.13 = (bf16[32,1024]{1,0:T(8,128)(2,1)S(1)}, bf16[32,1024]{1,0:T(8,128)(2,1)S(1)}, u32[]{:S(2)}, u32[]{:S(2)}) collective-permute-start(bf16[32,1024]{1,0:T(8,128)(2,1)S(1)} %get-tuple-element.59), channel_id=1, source_target_pairs={{2,1},{5,4},{7,6},{9,8},{10,11},{14,13},{17,18},{21,20},{22,23},{2... | collective-permute-start | bytes 196616 | tf_op jit(solution)/shard_map/cond/branch_0_fun/ppermute | solution.py:317
  27.6 0.7 %collective-permute-start.12 = (bf16[32,1024]{1,0:T(8,128)(2,1)S(1)}, bf16[32,1024]{1,0:T(8,128)(2,1)S(1)}, u32[]{:S(2)}, u32[]{:S(2)}) collective-permute-start(bf16[32,1024]{1,0:T(8,128)(2,1)S(1)} %get-tuple-element.59), channel_id=1, source_target_pairs={{2,6},{9,13},{15,11},{16,20},{22,18},{29,25}} | collective-permute-start | bytes 196616 | tf_op jit(solution)/shard_map/cond/branch_0_fun/ppermute | solution.py:317
  28.3 5.0 %collective-permute-done.14.x_ref = bf16[32,1024]{1,0:T(8,128)(2,1)S(1)} collective-permute-done((bf16[32,1024]{1,0:T(8,128)(2,1)S(1)}, bf16[32,1024]{1,0:T(8,128)(2,1)S(1)}, u32[]{:S(2)}, u32[]{:S(2)}) %collective-permute-start.14) | collective-permute-done | bytes 65568 | tf_op jit(solution)/shard_map/cond/branch_0_fun/ppermute | solution.py:317
  33.3 1.3 %collective-permute-done.13.z_ref = bf16[32,1024]{1,0:T(8,128)(2,1)S(1)} collective-permute-done((bf16[32,1024]{1,0:T(8,128)(2,1)S(1)}, bf16[32,1024]{1,0:T(8,128)(2,1)S(1)}, u32[]{:S(2)}, u32[]{:S(2)}) %collective-permute-start.13) | collective-permute-done | bytes 65568 | tf_op jit(solution)/shard_map/cond/branch_0_fun/ppermute | solution.py:317
  34.6 0.0 collective-permute-done.12.y_ref
  34.6 0.5 hop5.4
  35.0 1.3 %collective-permute-start.17 = (bf16[32,1024]{1,0:T(8,128)(2,1)S(1)}, bf16[32,1024]{1,0:T(8,128)(2,1)S(1)}, u32[]{:S(2)}, u32[]{:S(2)}) collective-permute-start(bf16[32,1024]{1,0:T(8,128)(2,1)S(1)} %get-tuple-element.61), channel_id=1, source_target_pairs={{7,15},{8,0},{10,2},{11,19},{13,5},{14,22},{17,9},{18,26},{20,12},... | collective-permute-start | bytes 196616 | tf_op jit(solution)/shard_map/cond/branch_0_fun/ppermute | solution.py:317
  36.4 0.7 %collective-permute-start.16 = (bf16[32,1024]{1,0:T(8,128)(2,1)S(1)}, bf16[32,1024]{1,0:T(8,128)(2,1)S(1)}, u32[]{:S(2)}, u32[]{:S(2)}) collective-permute-start(bf16[32,1024]{1,0:T(8,128)(2,1)S(1)} %get-tuple-element.61), channel_id=1, source_target_pairs={{1,0},{3,2},{6,5},{10,9},{13,12},{14,15},{17,16},{18,19},{21,22},{... | collective-permute-start | bytes 196616 | tf_op jit(solution)/shard_map/cond/branch_0_fun/ppermute | solution.py:317
  37.0 1.3 %collective-permute-start.15 = (bf16[32,1024]{1,0:T(8,128)(2,1)S(1)}, bf16[32,1024]{1,0:T(8,128)(2,1)S(1)}, u32[]{:S(2)}, u32[]{:S(2)}) collective-permute-start(bf16[32,1024]{1,0:T(8,128)(2,1)S(1)} %get-tuple-element.61), channel_id=1, source_target_pairs={{1,5},{3,7},{4,0},{8,12},{23,19},{27,31},{28,24},{30,26}} | collective-permute-start | bytes 196616 | tf_op jit(solution)/shard_map/cond/branch_0_fun/ppermute | solution.py:317
  38.3 0.0 collective-permute-done.17.x_ref
  38.3 0.0 collective-permute-done.16.z_ref
  38.3 0.9 %collective-permute-done.15.y_ref = bf16[32,1024]{1,0:T(8,128)(2,1)S(1)} collective-permute-done((bf16[32,1024]{1,0:T(8,128)(2,1)S(1)}, bf16[32,1024]{1,0:T(8,128)(2,1)S(1)}, u32[]{:S(2)}, u32[]{:S(2)}) %collective-permute-start.15) | collective-permute-done | bytes 65568 | tf_op jit(solution)/shard_map/cond/branch_0_fun/ppermute | solution.py:317
  39.2 1.3 %collective-permute-start.20 = (bf16[16,1024]{1,0:T(8,128)(2,1)S(1)}, bf16[16,1024]{1,0:T(8,128)(2,1)S(1)}, u32[]{:S(2)}, u32[]{:S(2)}) collective-permute-start(bf16[16,1024]{1,0:T(8,128)(2,1)S(1)} %get-tuple-element.63), channel_id=1, source_target_pairs={{3,11},{9,1},{10,18},{12,4},{14,6},{15,23},{16,8},{17,25},{19,27},... | collective-permute-start | bytes 98312 | tf_op jit(solution)/shard_map/cond/branch_0_fun/ppermute | solution.py:317
  40.5 1.3 %collective-permute-start.19 = (bf16[16,1024]{1,0:T(8,128)(2,1)S(1)}, bf16[16,1024]{1,0:T(8,128)(2,1)S(1)}, u32[]{:S(2)}, u32[]{:S(2)}) collective-permute-start(bf16[16,1024]{1,0:T(8,128)(2,1)S(1)} %get-tuple-element.63), channel_id=1, source_target_pairs={{2,1},{5,4},{7,6},{9,8},{10,11},{14,13},{17,18},{21,20},{22,23},{2... | collective-permute-start | bytes 98312 | tf_op jit(solution)/shard_map/cond/branch_0_fun/ppermute | solution.py:317
  41.8 0.7 %collective-permute-start.18 = (bf16[16,1024]{1,0:T(8,128)(2,1)S(1)}, bf16[16,1024]{1,0:T(8,128)(2,1)S(1)}, u32[]{:S(2)}, u32[]{:S(2)}) collective-permute-start(bf16[16,1024]{1,0:T(8,128)(2,1)S(1)} %get-tuple-element.63), channel_id=1, source_target_pairs={{0,4},{7,3},{24,28},{31,27}} | collective-permute-start | bytes 98312 | tf_op jit(solution)/shard_map/cond/branch_0_fun/ppermute | solution.py:317
  42.5 3.6 %collective-permute-done.20.x_ref = bf16[16,1024]{1,0:T(8,128)(2,1)S(1)} collective-permute-done((bf16[16,1024]{1,0:T(8,128)(2,1)S(1)}, bf16[16,1024]{1,0:T(8,128)(2,1)S(1)}, u32[]{:S(2)}, u32[]{:S(2)}) %collective-permute-start.20) | collective-permute-done | bytes 32800 | tf_op jit(solution)/shard_map/cond/branch_0_fun/ppermute | solution.py:317
  46.1 0.4 collective-permute-done.19.z_ref
  46.5 0.0 collective-permute-done.18.y_ref
  46.5 0.7 %hop7.4 = bf16[2,16,1024]{2,1,0:T(8,128)(2,1)} custom-call(s32[1]{0:T(128)} %bitcast.lead_hbm.lead_ref, bf16[16,1024]{1,0:T(8,128)(2,1)S(1)} %collective-permute-done.18.y_ref, bf16[16,1024]{1,0:T(8,128)(2,1)S(1)} %collective-permute-done.19.z_ref, bf16[16,1024]{1,0:T(8,128)(2,1)S(1)} %collective-permute-done.20.x_ref, ...), custom_call_target="tpu_custom_call" | custom-call | tf_op jit(solution)/shard_map/cond/branch_0_fun/hop7/pallas_call | solution.py:295
  (5 shorter events, 0.1 us)
Async XLA Ops:
  0.7 6.7 %collective-permute-start.2 = (bf16[16,1024]{1,0:T(8,128)(2,1)S(1)}, bf16[16,1024]{1,0:T(8,128)(2,1)S(1)}, u32[]{:S(2)}, u32[]{:S(2)}) collective-permute-start(bf16[16,1024]{1,0:T(8,128)(2,1)S(1)} %begin.4.after_ref), channel_id=1, source_target_pairs={{0,8},{4,12},{27,19},{31,23}} | collective-permute-start | bytes 98312 | tf_op jit(solution)/shard_map/cond/branch_0_fun/ppermute | solution.py:317
  2.0 5.4 %collective-permute-start.1 = (bf16[16,1024]{1,0:T(8,128)(2,1)S(1)}, bf16[16,1024]{1,0:T(8,128)(2,1)S(1)}, u32[]{:S(2)}, u32[]{:S(2)}) collective-permute-start(bf16[16,1024]{1,0:T(8,128)(2,1)S(1)} %begin.4.after_ref), channel_id=1, source_target_pairs={{1,2},{4,5},{8,9},{23,22},{27,26},{30,29}} | collective-permute-start | bytes 98312 | tf_op jit(solution)/shard_map/cond/branch_0_fun/ppermute | solution.py:317
  4.9 2.6 %collective-permute-start = (bf16[16,1024]{1,0:T(8,128)(2,1)S(1)}, bf16[16,1024]{1,0:T(8,128)(2,1)S(1)}, u32[]{:S(2)}, u32[]{:S(2)}) collective-permute-start(bf16[16,1024]{1,0:T(8,128)(2,1)S(1)} %begin.4.after_ref), channel_id=1, source_target_pairs={{3,7},{4,0},{6,2},{15,11},{16,20},{25,29},{27,31},{28,24}} | collective-permute-start | bytes 98312 | tf_op jit(solution)/shard_map/cond/branch_0_fun/ppermute | solution.py:317
  5.6 5.3 %copy-start = (bf16[1,1,1,2,1024,1024]{5,4,3,2,1,0:T(8,128)(2,1)S(1)}, bf16[1,1,1,2,1024,1024]{5,4,3,2,1,0:T(8,128)(2,1)}, u32[]{:S(2)}) copy-start(bf16[1,1,1,2,1024,1024]{5,4,3,2,1,0:T(8,128)(2,1)} %get-tuple-element.132) | copy-start | bytes 12582916 | tf_op jit(solution)/shard_map/cond
  7.5 6.3 %collective-permute-start.5 = (bf16[32,1024]{1,0:T(8,128)(2,1)S(1)}, bf16[32,1024]{1,0:T(8,128)(2,1)S(1)}, u32[]{:S(2)}, u32[]{:S(2)}) collective-permute-start(bf16[32,1024]{1,0:T(8,128)(2,1)S(1)} %get-tuple-element.53.after_ref), channel_id=1, source_target_pairs={{0,8},{2,10},{5,13},{9,17},{12,20},{15,7},{16,24},{19,11},{22,14},... | collective-permute-start | bytes 196616 | tf_op jit(solution)/shard_map/cond/branch_0_fun/ppermute | solution.py:317
  8.9 4.9 %collective-permute-start.4 = (bf16[32,1024]{1,0:T(8,128)(2,1)S(1)}, bf16[32,1024]{1,0:T(8,128)(2,1)S(1)}, u32[]{:S(2)}, u32[]{:S(2)}) collective-permute-start(bf16[32,1024]{1,0:T(8,128)(2,1)S(1)} %get-tuple-element.53.after_ref), channel_id=1, source_target_pairs={{0,1},{5,6},{12,13},{19,18},{26,25},{31,30}} | collective-permute-start | bytes 196616 | tf_op jit(solution)/shard_map/cond/branch_0_fun/ppermute | solution.py:317
  9.6 4.2 %collective-permute-start.3 = (bf16[32,1024]{1,0:T(8,128)(2,1)S(1)}, bf16[32,1024]{1,0:T(8,128)(2,1)S(1)}, u32[]{:S(2)}, u32[]{:S(2)}) collective-permute-start(bf16[32,1024]{1,0:T(8,128)(2,1)S(1)} %get-tuple-element.53.after_ref), channel_id=1, source_target_pairs={{5,1},{12,8},{19,23},{26,30}} | collective-permute-start | bytes 196616 | tf_op jit(solution)/shard_map/cond/branch_0_fun/ppermute | solution.py:317
  14.3 3.3 %collective-permute-start.8 = (bf16[32,1024]{1,0:T(8,128)(2,1)S(1)}, bf16[32,1024]{1,0:T(8,128)(2,1)S(1)}, u32[]{:S(2)}, u32[]{:S(2)}) collective-permute-start(bf16[32,1024]{1,0:T(8,128)(2,1)S(1)} %get-tuple-element.55), channel_id=1, source_target_pairs={{1,9},{4,12},{6,14},{8,16},{11,3},{13,21},{18,10},{20,28},{23,15},... | collective-permute-start | bytes 196616 | tf_op jit(solution)/shard_map/cond/branch_0_fun/ppermute | solution.py:317
  15.6 3.2 %collective-permute-start.7 = (bf16[32,1024]{1,0:T(8,128)(2,1)S(1)}, bf16[32,1024]{1,0:T(8,128)(2,1)S(1)}, u32[]{:S(2)}, u32[]{:S(2)}) collective-permute-start(bf16[32,1024]{1,0:T(8,128)(2,1)S(1)} %get-tuple-element.55), channel_id=1, source_target_pairs={{1,2},{6,7},{8,9},{11,10},{13,14},{18,17},{20,21},{23,22},{25,24},... | collective-permute-start | bytes 196616 | tf_op jit(solution)/shard_map/cond/branch_0_fun/ppermute | solution.py:317
  16.9 1.9 %collective-permute-start.6 = (bf16[32,1024]{1,0:T(8,128)(2,1)S(1)}, bf16[32,1024]{1,0:T(8,128)(2,1)S(1)}, u32[]{:S(2)}, u32[]{:S(2)}) collective-permute-start(bf16[32,1024]{1,0:T(8,128)(2,1)S(1)} %get-tuple-element.55), channel_id=1, source_target_pairs={{6,2},{11,15},{13,9},{18,22},{20,16},{25,29}} | collective-permute-start | bytes 196616 | tf_op jit(solution)/shard_map/cond/branch_0_fun/ppermute | solution.py:317
  18.8 4.3 %collective-permute-start.11 = (bf16[32,1024]{1,0:T(8,128)(2,1)S(1)}, bf16[32,1024]{1,0:T(8,128)(2,1)S(1)}, u32[]{:S(2)}, u32[]{:S(2)}) collective-permute-start(bf16[32,1024]{1,0:T(8,128)(2,1)S(1)} %get-tuple-element.57), channel_id=1, source_target_pairs={{0,8},{1,25},{2,10},{3,11},{4,12},{5,13},{6,30},{7,15},{8,0},{9,17... | collective-permute-start | bytes 196616 | tf_op jit(solution)/shard_map/cond/branch_0_fun/ppermute | solution.py:317
  18.8 6.1 %collective-permute-start.10 = (bf16[32,1024]{1,0:T(8,128)(2,1)S(1)}, bf16[32,1024]{1,0:T(8,128)(2,1)S(1)}, u32[]{:S(2)}, u32[]{:S(2)}) collective-permute-start(bf16[32,1024]{1,0:T(8,128)(2,1)S(1)} %get-tuple-element.57), channel_id=1, source_target_pairs={{0,1},{1,0},{2,3},{3,2},{4,5},{5,4},{6,7},{7,6},{8,11},{9,10},{10,... | collective-permute-start | bytes 196616 | tf_op jit(solution)/shard_map/cond/branch_0_fun/ppermute | solution.py:317
  22.6 2.4 %collective-permute-start.9 = (bf16[32,1024]{1,0:T(8,128)(2,1)S(1)}, bf16[32,1024]{1,0:T(8,128)(2,1)S(1)}, u32[]{:S(2)}, u32[]{:S(2)}) collective-permute-start(bf16[32,1024]{1,0:T(8,128)(2,1)S(1)} %get-tuple-element.57), channel_id=1, source_target_pairs={{0,4},{1,5},{2,6},{3,7},{4,0},{5,1},{6,2},{7,3},{8,12},{9,13},{10,... | collective-permute-start | bytes 196616 | tf_op jit(solution)/shard_map/cond/branch_0_fun/ppermute | solution.py:317
  25.0 8.3 %collective-permute-start.14 = (bf16[32,1024]{1,0:T(8,128)(2,1)S(1)}, bf16[32,1024]{1,0:T(8,128)(2,1)S(1)}, u32[]{:S(2)}, u32[]{:S(2)}) collective-permute-start(bf16[32,1024]{1,0:T(8,128)(2,1)S(1)} %get-tuple-element.59), channel_id=1, source_target_pairs={{3,11},{9,1},{10,18},{12,4},{14,6},{15,23},{16,8},{17,25},{19,27},... | collective-permute-start | bytes 196616 | tf_op jit(solution)/shard_map/cond/branch_0_fun/ppermute | solution.py:317
  26.3 8.3 %collective-permute-start.13 = (bf16[32,1024]{1,0:T(8,128)(2,1)S(1)}, bf16[32,1024]{1,0:T(8,128)(2,1)S(1)}, u32[]{:S(2)}, u32[]{:S(2)}) collective-permute-start(bf16[32,1024]{1,0:T(8,128)(2,1)S(1)} %get-tuple-element.59), channel_id=1, source_target_pairs={{2,1},{5,4},{7,6},{9,8},{10,11},{14,13},{17,18},{21,20},{22,23},{2... | collective-permute-start | bytes 196616 | tf_op jit(solution)/shard_map/cond/branch_0_fun/ppermute | solution.py:317
  27.6 7.0 %collective-permute-start.12 = (bf16[32,1024]{1,0:T(8,128)(2,1)S(1)}, bf16[32,1024]{1,0:T(8,128)(2,1)S(1)}, u32[]{:S(2)}, u32[]{:S(2)}) collective-permute-start(bf16[32,1024]{1,0:T(8,128)(2,1)S(1)} %get-tuple-element.59), channel_id=1, source_target_pairs={{2,6},{9,13},{15,11},{16,20},{22,18},{29,25}} | collective-permute-start | bytes 196616 | tf_op jit(solution)/shard_map/cond/branch_0_fun/ppermute | solution.py:317
  35.0 3.3 %collective-permute-start.17 = (bf16[32,1024]{1,0:T(8,128)(2,1)S(1)}, bf16[32,1024]{1,0:T(8,128)(2,1)S(1)}, u32[]{:S(2)}, u32[]{:S(2)}) collective-permute-start(bf16[32,1024]{1,0:T(8,128)(2,1)S(1)} %get-tuple-element.61), channel_id=1, source_target_pairs={{7,15},{8,0},{10,2},{11,19},{13,5},{14,22},{17,9},{18,26},{20,12},... | collective-permute-start | bytes 196616 | tf_op jit(solution)/shard_map/cond/branch_0_fun/ppermute | solution.py:317
  36.4 2.0 %collective-permute-start.16 = (bf16[32,1024]{1,0:T(8,128)(2,1)S(1)}, bf16[32,1024]{1,0:T(8,128)(2,1)S(1)}, u32[]{:S(2)}, u32[]{:S(2)}) collective-permute-start(bf16[32,1024]{1,0:T(8,128)(2,1)S(1)} %get-tuple-element.61), channel_id=1, source_target_pairs={{1,0},{3,2},{6,5},{10,9},{13,12},{14,15},{17,16},{18,19},{21,22},{... | collective-permute-start | bytes 196616 | tf_op jit(solution)/shard_map/cond/branch_0_fun/ppermute | solution.py:317
  37.0 2.2 %collective-permute-start.15 = (bf16[32,1024]{1,0:T(8,128)(2,1)S(1)}, bf16[32,1024]{1,0:T(8,128)(2,1)S(1)}, u32[]{:S(2)}, u32[]{:S(2)}) collective-permute-start(bf16[32,1024]{1,0:T(8,128)(2,1)S(1)} %get-tuple-element.61), channel_id=1, source_target_pairs={{1,5},{3,7},{4,0},{8,12},{23,19},{27,31},{28,24},{30,26}} | collective-permute-start | bytes 196616 | tf_op jit(solution)/shard_map/cond/branch_0_fun/ppermute | solution.py:317
  39.2 6.9 %collective-permute-start.20 = (bf16[16,1024]{1,0:T(8,128)(2,1)S(1)}, bf16[16,1024]{1,0:T(8,128)(2,1)S(1)}, u32[]{:S(2)}, u32[]{:S(2)}) collective-permute-start(bf16[16,1024]{1,0:T(8,128)(2,1)S(1)} %get-tuple-element.63), channel_id=1, source_target_pairs={{3,11},{9,1},{10,18},{12,4},{14,6},{15,23},{16,8},{17,25},{19,27},... | collective-permute-start | bytes 98312 | tf_op jit(solution)/shard_map/cond/branch_0_fun/ppermute | solution.py:317
  40.5 6.0 %collective-permute-start.19 = (bf16[16,1024]{1,0:T(8,128)(2,1)S(1)}, bf16[16,1024]{1,0:T(8,128)(2,1)S(1)}, u32[]{:S(2)}, u32[]{:S(2)}) collective-permute-start(bf16[16,1024]{1,0:T(8,128)(2,1)S(1)} %get-tuple-element.63), channel_id=1, source_target_pairs={{2,1},{5,4},{7,6},{9,8},{10,11},{14,13},{17,18},{21,20},{22,23},{2... | collective-permute-start | bytes 98312 | tf_op jit(solution)/shard_map/cond/branch_0_fun/ppermute | solution.py:317
  41.8 4.7 %collective-permute-start.18 = (bf16[16,1024]{1,0:T(8,128)(2,1)S(1)}, bf16[16,1024]{1,0:T(8,128)(2,1)S(1)}, u32[]{:S(2)}, u32[]{:S(2)}) collective-permute-start(bf16[16,1024]{1,0:T(8,128)(2,1)S(1)} %get-tuple-element.63), channel_id=1, source_target_pairs={{0,4},{7,3},{24,28},{31,27}} | collective-permute-start | bytes 98312 | tf_op jit(solution)/shard_map/cond/branch_0_fun/ppermute | solution.py:317
